TPU v7x, 128 devices: a whole 4x4x4 slice. The times are simulated.
128 devices in a mesh: gx: 8 (over z, core), gy: 16 (over x, y).
Axes of the slice: x: 4, y: 4, z: 4, core: 2. Of those that a mesh axis runs over, the one named last changes fastest.
Arguments:
- depth: float32 [4096, 128, 128], P(('gx', 'gy')), may hold values from 0.1 to 2
- discharge: float32 [4096, 2, 128, 128], P(('gx', 'gy')), may hold values from -3 to 3
- bed: float32 [4096, 128, 128], P(('gx', 'gy')), may hold values from -1.5 to 2.5
- friction: float32 [4096, 128, 128], P(('gx', 'gy')), may hold values from 0.004 to 0.1
- tile_ids: int32 [4096], P(('gx', 'gy')), may hold values from -1 to 4095, as said below
- neighbors: int32 [4096, 4], P(('gx', 'gy')), may hold values from -1 to 4095, as said below
- moves: int32 [128, 2, 8, 2], P(('gx', 'gy')), may hold values from -1 to 4095, as said below
Outputs:
- new_depth: float32 [4096, 128, 128], P(('gx', 'gy'))
- new_discharge: float32 [4096, 2, 128, 128], P(('gx', 'gy'))
Inputs may be any that keep to these rules, and one draw needn't show every extreme that they name: `tile_ids`: each owner's wet tiles after the moves fill its first slots: those that stayed, in curve order, then those arrived from lower gy, then those arrived from higher gy; an empty slot is -1. `neighbors`: links are symmetric and join only slots with tile_ids >= 0. The tile beside on side 0 or 1 is held by the same owner or by the owner at gx - 1 or gx + 1 respectively; on side 2 or 3 by the same owner or the owner at gy - 1 or gy + 1. At most 4 tiles of an owner have their side 0 (or side 1) neighbour on another owner, and at most 8 their side 2 (or side 3) neighbour; both bounds are reached on some owner. Entries are global slots, -1 if unused, used entries first. Leaving slots lie on the owner and hold no tile that stays; landing slots lie on the owner and are either left by a tile or hold no tile before the moves. The m-th tile leaving owner (a, b) toward higher gy is the m-th arriving at (a, b + 1) from lower gy, and likewise downward; owners at the ends of gy list nothing toward the outside. All 8 entries of a direction are used on some owners.
All inputs are finite; a program needn't handle non-finite values.
Results may differ from a plain program's by a relative error of at most 0.00002.
Values sent between devices are 32-bit elements; how exact they have to be, the bound alone decides.
No kernel may reach another device: no remote copies, remote signals or barrier semaphores. Data moves between devices by JAX's collectives and lax.ppermute only.
A program may use at most 128 MiB of HBM per device.

v0:
```python
import jax
import jax.numpy as jnp
from jax import lax
from jax.sharding import PartitionSpec as P

BLOCK_ROWS = 8
BLOCK_COLS = 4
STEPS = 4


gravity = 9.81
step_time = 0.25
spacing = 2.0
min_depth = 0.15


def shifted(block, axis, distance):
    devices = range(lax.axis_size(axis))
    route = [(i - distance, i) for i in devices if i - distance in devices]
    return lax.ppermute(block, axis, route)


def face_flux(flow, h_lo, h_hi, z_lo, z_hi, n_lo, n_hi):
    depth_face = jnp.maximum(0.5 * (h_lo + h_hi), min_depth)
    drive = flow - gravity * step_time / spacing * depth_face * (h_hi + z_hi - (h_lo + z_lo))
    drag = 1.0 + gravity * step_time * 0.5 * (n_lo + n_hi) * jnp.abs(flow) * jnp.exp(
        -(7.0 / 3.0) * jnp.log(depth_face)
    )
    return drive / drag


def pass_along_gx(rows, shift_by):
    return shifted(rows, "gx", shift_by)


def pass_along_gy(rows, shift_by):
    return shifted(rows, "gy", shift_by)


def carry_tiles(payload, shift_by):
    return shifted(payload, "gy", shift_by)


def pick_rows(rows, wanted, count):
    order = jnp.cumsum(wanted.astype(jnp.int32)) - 1
    hit = wanted[None, :] & (order[None, :] == jnp.arange(count)[:, None])
    chosen = jnp.sum(jnp.where(hit, jnp.arange(wanted.shape[0])[None, :], 0), 1)
    return jnp.take(rows, chosen, axis=0)


def place_rows(arrived, rows, link, owner_id, base):
    slots = rows.shape[0]
    exists = link >= 0
    local = exists & (link // slots == owner_id)
    remote = exists & ~local
    order = jnp.sum(remote[None, :] & (link[None, :] < link[:, None]), 1)
    far_rows = jnp.take(arrived, jnp.minimum(order, arrived.shape[0] - 1), axis=0)
    near_rows = jnp.take(rows, jnp.clip(link - base, 0, slots - 1), axis=0)
    return jnp.where(
        remote[:, None, None], far_rows, jnp.where(local[:, None, None], near_rows, 0.0)
    )


def shards(depth, discharge, bed, friction, tile_ids, neighbors, moves):
    slots = depth.shape[0]
    tile = depth.shape[1]
    owner_id = lax.axis_index(("gx", "gy"))
    base = owner_id * slots
    plan = moves[0]

    def local_slots(entries):
        return jnp.where(entries >= 0, entries - base, slots)

    leave_down = local_slots(plan[0, :, 0])
    leave_up = local_slots(plan[1, :, 0])
    land_low = local_slots(plan[0, :, 1])
    land_high = local_slots(plan[1, :, 1])

    def bundle(anchor):
        chosen = jnp.minimum(anchor, slots - 1)
        return jnp.concatenate(
            [
                depth[chosen][:, None],
                discharge[chosen],
                bed[chosen][:, None],
                friction[chosen][:, None],
            ],
            1,
        )

    to_low = bundle(leave_down)
    to_high = bundle(leave_up)
    from_low = carry_tiles(to_high, 1)
    from_high = carry_tiles(to_low, -1)
    leaving = jnp.any(
        jnp.arange(slots)[:, None] == jnp.concatenate([leave_down, leave_up])[None, :], 1
    )
    landing = jnp.concatenate([land_low, land_high])
    arrived = jnp.concatenate([from_low, from_high], 0)

    def settle(field, fresh):
        shape = (-1,) + (1,) * (field.ndim - 1)
        kept = jnp.where(leaving.reshape(shape), 0.0, field)
        return kept.at[landing].set(fresh, mode="drop")

    h = settle(depth, arrived[:, 0])
    flows = settle(discharge, arrived[:, 1:3])
    z = settle(bed, arrived[:, 3])
    fr = settle(friction, arrived[:, 4])
    qx = flows[:, 0]
    qy = flows[:, 1]
    exists = neighbors >= 0
    remote = exists & (neighbors // slots != owner_id)
    inside_x = jnp.arange(tile)[None, :, None] < tile - 1
    inside_y = jnp.arange(tile)[None, None, :] < tile - 1
    first_x = jnp.arange(tile)[None, :, None] == 0
    first_y = jnp.arange(tile)[None, None, :] == 0
    for turn in range(STEPS):
        low_rows = jnp.stack([h[:, 0, :], z[:, 0, :], fr[:, 0, :]], 1)
        left_cols = jnp.stack([h[:, :, 0], z[:, :, 0], fr[:, :, 0]], 1)
        got_above = pass_along_gx(pick_rows(low_rows, remote[:, 0], BLOCK_COLS), -1)
        got_right = pass_along_gy(pick_rows(left_cols, remote[:, 2], BLOCK_ROWS), -1)
        above = place_rows(got_above, low_rows, neighbors[:, 1], owner_id, base)
        right = place_rows(got_right, left_cols, neighbors[:, 3], owner_id, base)
        h_hi = jnp.where(inside_x, jnp.roll(h, -1, 1), above[:, 0, :][:, None, :])
        z_hi = jnp.where(inside_x, jnp.roll(z, -1, 1), above[:, 1, :][:, None, :])
        n_hi = jnp.where(inside_x, jnp.roll(fr, -1, 1), above[:, 2, :][:, None, :])
        qx_new = jnp.where(
            inside_x | exists[:, 1][:, None, None], face_flux(qx, h, h_hi, z, z_hi, fr, n_hi), 0.0
        )
        h_rt = jnp.where(inside_y, jnp.roll(h, -1, 2), right[:, 0, :][:, :, None])
        z_rt = jnp.where(inside_y, jnp.roll(z, -1, 2), right[:, 1, :][:, :, None])
        n_rt = jnp.where(inside_y, jnp.roll(fr, -1, 2), right[:, 2, :][:, :, None])
        qy_new = jnp.where(
            inside_y | exists[:, 3][:, None, None], face_flux(qy, h, h_rt, z, z_rt, fr, n_rt), 0.0
        )
        last_qx = qx_new[:, -1, :][:, None, :]
        last_qy = qy_new[:, :, -1][:, None, :]
        got_qx = pass_along_gx(pick_rows(last_qx, remote[:, 1], BLOCK_COLS), 1)
        got_qy = pass_along_gy(pick_rows(last_qy, remote[:, 3], BLOCK_ROWS), 1)
        edge_qx = place_rows(got_qx, last_qx, neighbors[:, 0], owner_id, base)[:, 0, :]
        edge_qy = place_rows(got_qy, last_qy, neighbors[:, 2], owner_id, base)[:, 0, :]
        in_x = jnp.where(first_x, edge_qx[:, None, :], jnp.roll(qx_new, 1, 1))
        in_y = jnp.where(first_y, edge_qy[:, :, None], jnp.roll(qy_new, 1, 2))
        h = h + step_time / spacing * (in_x - qx_new + (in_y - qy_new))
        qx = qx_new
        qy = qy_new
    live = (tile_ids >= 0)[:, None, None]
    new_depth = jnp.where(live, h, 0.0)
    new_discharge = jnp.stack([jnp.where(live, qx, 0.0), jnp.where(live, qy, 0.0)], 1)
    return (new_depth, new_discharge)


def solution(mesh):
    return jax.shard_map(
        shards,
        mesh=mesh,
        in_specs=(
            P(("gx", "gy"), None, None),
            P(("gx", "gy"), None, None, None),
            P(("gx", "gy"), None, None),
            P(("gx", "gy"), None, None),
            P(("gx", "gy")),
            P(("gx", "gy"), None),
            P(("gx", "gy"), None, None, None),
        ),
        out_specs=(P(("gx", "gy"), None, None), P(("gx", "gy"), None, None, None)),
        check_vma=False,
    )
```

profile of v0, /device:TPU:56, one launch (start us, length us, event | category | flops | bytes accessed | tf_op | source)
XLA Modules:
  0.0 354.7 jit_solution(11104600455577306828)
XLA Ops:
  36.8 5.1 %broadcast_select_fusion = f32[32,2,128,128]{3,2,1,0:T(8,128)} fusion(f32[32,2,128,128]{3,2,1,0:T(8,128)} %param.28, pred[32]{0:T(512)(128)(4,1)S(1)} %fusion.53), kind=kLoop, calls=%fused_computation.116 | loop fusion | flops 1048576 | bytes 8388640 | tf_op jit(solution)/shard_map/jit(_where)/select_n | solution.py:103
  44.7 30.8 %collective-permute-done = f32[8,5,128,128]{3,2,1,0:T(8,128)} collective-permute-done((f32[8,5,128,128]{3,2,1,0:T(8,128)}, f32[8,5,128,128]{3,2,1,0:T(8,128)}, u32[]{:S(2)}, u32[]{:S(2)}) %collective-permute-start) | collective-permute-done | bytes 2621472 | tf_op jit(solution)/shard_map/ppermute | solution.py:20
  77.5 16.2 %collective-permute-done.1 = f32[8,5,128,128]{3,2,1,0:T(8,128)} collective-permute-done((f32[8,5,128,128]{3,2,1,0:T(8,128)}, f32[8,5,128,128]{3,2,1,0:T(8,128)}, u32[]{:S(2)}, u32[]{:S(2)}) %collective-permute-start.1) | collective-permute-done | bytes 2621472 | tf_op jit(solution)/shard_map/ppermute | solution.py:20
  131.5 4.4 %scatter_fusion.1 = f32[32,2,128,128]{3,2,1,0:T(8,128)} fusion(f32[32,2,128,128]{3,2,1,0:T(8,128)} %broadcast_select_fusion, s32[16]{0:T(128)S(1)} %fusion.64, f32[16,2,128,128]{3,2,1,0:T(8,128)} %slice.550), kind=kCustom, calls=%fused_computation.57 | custom fusion | bytes 6291520 | tf_op jit(solution)/shard_map/scatter | solution.py:104
  136.8 6.8 %divide_select_fusion.7 = f32[32,128,128]{2,1,0:T(8,128)S(1)} fusion(f32[32,128,128]{2,1,0:T(8,128)} %scatter_fusion.3, f32[32,2,128,128]{3,2,1,0:T(8,128)} %scatter_fusion.1, f32[32,128,128]{2,1,0:T(8,128)} %scatter_fusion, f32[32,1,128]{2,1,0:T(1,128)S(1)} %slice.553, f32[32,127,128]{2,1,0:T(8,128)} %slice.552, f32[32,128]{1,0:T(8,128)S(1)} %bitcast.353, ...), kind=kLoop, calls=%fused_computation.115 | loop fusion | flops 12582912 | bytes 16830592 | tf_op jit(solution)/shard_map/jit(_where)/select_n | solution.py:128
  158.0 9.7 %divide_select_fusion.6 = (f32[32,128,128]{2,1,0:T(8,128)S(1)}, f32[32,128,128]{2,1,0:T(8,128)}, f32[32,128,128]{2,1,0:T(8,128)}) fusion(f32[32,128,128]{2,1,0:T(8,128)} %scatter_fusion.3, f32[32,2,128,128]{3,2,1,0:T(8,128)} %scatter_fusion.1, f32[32,128,128]{2,1,0:T(8,128)} %scatter_fusion, f32[32,128,1]{2,1,0:T(8,128)} %get-tuple-element.85, ...), kind=kLoop, calls=%fused_computation.114 | loop fusion | flops 12582912 | bytes 21024896 | tf_op jit(solution)/shard_map/jit(_where)/select_n | solution.py:134
  170.3 5.7 %collective-permute-start.5 = (f32[8,1,128]{2,0,1:T(8,128)S(1)}, f32[8,1,128]{2,0,1:T(8,128)S(1)}, u32[]{:S(2)}, u32[]{:S(2)}) collective-permute-start(f32[8,1,128]{2,0,1:T(8,128)S(1)} %bitcast_select_fusion.19), channel_id=1, source_target_pairs={{0,1},{1,2},{2,3},{3,4},{4,5},{5,6},{6,7},{7,8},{8,9},{9,10},{10,1... | collective-permute-start | bytes 12296 | tf_op jit(solution)/shard_map/ppermute | solution.py:20
  178.0 5.6 %fusion.3 = f32[32,128,128]{2,1,0:T(8,128)S(1)} fusion(f32[32,128,128]{2,1,0:T(8,128)} %scatter_fusion, f32[32,128,128]{2,1,0:T(8,128)} %copy-done.10, f32[32,127,128]{2,1,0:T(8,128)} %bitcast.292, f32[32,1,128]{2,1,0:T(1,128)S(1)} %slice.563, f32[32,128,128]{2,1,0:T(8,128)} %copy-done.8, f32[32,128,127]{2,1,0:T(8,128)} %bitcast.290, ...), kind=kLoop, calls=%fused_computation.72 | loop fusion | flops 4718592 | bytes 12615808 | tf_op jit(solution)/shard_map/add | solution.py:145
  196.4 6.7 %divide_select_fusion.5 = f32[32,128,128]{2,1,0:T(8,128)S(1)} fusion(f32[32,128,128]{2,1,0:T(8,128)} %copy-done.10, f32[32,128,128]{2,1,0:T(8,128)} %scatter_fusion.3, f32[32,128,128]{2,1,0:T(8,128)} %copy-done.5, f32[32,1,128]{2,1,0:T(1,128)S(1)} %slice.578, f32[32,127,128]{2,1,0:T(8,128)} %slice.577, f32[32,128]{1,0:T(8,128)S(1)} %bitcast.347, ...), kind=kLoop, calls=%fused_computation.113 | loop fusion | flops 12582912 | bytes 16830592 | tf_op jit(solution)/shard_map/jit(_where)/select_n | solution.py:128
  213.5 6.6 %divide_select_fusion.4 = f32[32,128,128]{2,1,0:T(8,128)S(1)} fusion(f32[32,128,128]{2,1,0:T(8,128)} %copy-done.8, f32[32,128,128]{2,1,0:T(8,128)} %scatter_fusion.3, f32[32,128,128]{2,1,0:T(8,128)} %get-tuple-element.46, f32[32,128,128]{2,1,0:T(8,128)} %get-tuple-element.45, f32[32,128,128]{2,1,0:T(8,128)} %copy-done.5, ...), kind=kLoop, calls=%fused_computation.112 | loop fusion | flops 11534336 | bytes 16830592 | tf_op jit(solution)/shard_map/jit(_where)/select_n | solution.py:134
  222.8 6.2 %collective-permute-start.9 = (f32[8,1,128]{2,0,1:T(8,128)S(1)}, f32[8,1,128]{2,0,1:T(8,128)S(1)}, u32[]{:S(2)}, u32[]{:S(2)}) collective-permute-start(f32[8,1,128]{2,0,1:T(8,128)S(1)} %bitcast_select_fusion.18), channel_id=1, source_target_pairs={{0,1},{1,2},{2,3},{3,4},{4,5},{5,6},{6,7},{7,8},{8,9},{9,10},{10,1... | collective-permute-start | bytes 12296 | tf_op jit(solution)/shard_map/ppermute | solution.py:20
  230.8 5.5 %fusion.8 = f32[32,128,128]{2,1,0:T(8,128)S(1)} fusion(f32[32,128,128]{2,1,0:T(8,128)} %copy-done.5, f32[32,128,128]{2,1,0:T(8,128)} %copy-done.12, f32[32,127,128]{2,1,0:T(8,128)} %bitcast.294, f32[32,1,128]{2,1,0:T(1,128)S(1)} %slice.582, f32[32,128,128]{2,1,0:T(8,128)} %copy-done.9, f32[32,128,127]{2,1,0:T(8,128)} %bitcast.291, ...), kind=kLoop, calls=%fused_computation.83 | loop fusion | flops 4718592 | bytes 12615808 | tf_op jit(solution)/shard_map/add | solution.py:145
  248.9 6.7 %divide_select_fusion.3 = f32[32,128,128]{2,1,0:T(8,128)S(1)} fusion(f32[32,128,128]{2,1,0:T(8,128)} %copy-done.12, f32[32,128,128]{2,1,0:T(8,128)} %scatter_fusion.3, f32[32,128,128]{2,1,0:T(8,128)} %copy-done.6, f32[32,1,128]{2,1,0:T(1,128)S(1)} %slice.592, f32[32,127,128]{2,1,0:T(8,128)} %slice.591, f32[32,128]{1,0:T(8,128)S(1)} %bitcast.350, ...), kind=kLoop, calls=%fused_computation.111 | loop fusion | flops 12582912 | bytes 16830592 | tf_op jit(solution)/shard_map/jit(_where)/select_n | solution.py:128
  259.9 3.6 %slice.598 = f32[32,128,127]{2,1,0:T(8,128)} slice(f32[32,128,128]{2,1,0:T(8,128)} %copy-done.6), slice={[0:32], [0:128], [1:128]} | slice | bytes 4161536 | tf_op jit(solution)/shard_map/jit(_roll_static)/slice | solution.py:131
  266.1 6.6 %divide_select_fusion.2 = f32[32,128,128]{2,1,0:T(8,128)S(1)} fusion(f32[32,128,128]{2,1,0:T(8,128)} %copy-done.9, f32[32,128,128]{2,1,0:T(8,128)} %scatter_fusion.3, f32[32,128,128]{2,1,0:T(8,128)} %get-tuple-element.46, f32[32,128,128]{2,1,0:T(8,128)} %get-tuple-element.45, f32[32,128,128]{2,1,0:T(8,128)} %copy-done.6, ...), kind=kLoop, calls=%fused_computation.110 | loop fusion | flops 11534336 | bytes 16830592 | tf_op jit(solution)/shard_map/jit(_where)/select_n | solution.py:134
  275.4 5.8 %collective-permute-start.13 = (f32[8,1,128]{2,0,1:T(8,128)S(1)}, f32[8,1,128]{2,0,1:T(8,128)S(1)}, u32[]{:S(2)}, u32[]{:S(2)}) collective-permute-start(f32[8,1,128]{2,0,1:T(8,128)S(1)} %bitcast_select_fusion.17), channel_id=1, source_target_pairs={{0,1},{1,2},{2,3},{3,4},{4,5},{5,6},{6,7},{7,8},{8,9},{9,10},{10,1... | collective-permute-start | bytes 12296 | tf_op jit(solution)/shard_map/ppermute | solution.py:20
  283.2 5.6 %fusion.13 = f32[32,128,128]{2,1,0:T(8,128)S(1)} fusion(f32[32,128,128]{2,1,0:T(8,128)} %copy-done.6, f32[32,128,128]{2,1,0:T(8,128)} %copy-done.11, f32[32,127,128]{2,1,0:T(8,128)} %bitcast.293, f32[32,1,128]{2,1,0:T(1,128)S(1)} %slice.596, f32[32,128,128]{2,1,0:T(8,128)} %copy-done.7, f32[32,128,127]{2,1,0:T(8,128)} %bitcast.289, ...), kind=kLoop, calls=%fused_computation.92 | loop fusion | flops 4718592 | bytes 12615808 | tf_op jit(solution)/shard_map/add | solution.py:145
  299.6 7.4 %select_bitcast_fusion.1 = (f32[32,1,128,128]{3,2,0,1:T(8,128)}, f32[32,128,128]{2,1,0:T(8,128)S(1)}) fusion(pred[32]{0:T(512)(128)(4,1)S(1)} %broadcast_compare_fusion.1, f32[32,128,128]{2,1,0:T(8,128)} %copy-done.11, f32[32,128,128]{2,1,0:T(8,128)} %scatter_fusion.3, f32[32,128]{1,0:T(8,128)S(1)} %bitcast.338, f32[32,1,128]{2,1,0:T(1,128)S(1)} %slice.557, ...), kind=kLoop, calls=%fused_computation.107 | loop fusion | flops 13107200 | bytes 18927776 | tf_op jit(solution)/shard_map/stack | solution.py:150
  318.8 4.3 %collective-permute-done.16 = f32[8,3,128]{2,1,0:T(4,128)S(1)} collective-permute-done((f32[8,3,128]{2,1,0:T(4,128)S(1)}, f32[8,3,128]{2,1,0:T(4,128)S(1)}, u32[]{:S(2)}, u32[]{:S(2)}) %collective-permute-start.16) | collective-permute-done | bytes 12320 | tf_op jit(solution)/shard_map/ppermute | solution.py:20
  323.9 7.8 %select_bitcast_fusion = (f32[32,1,128,128]{3,2,0,1:T(8,128)}, f32[32,128,128]{2,1,0:T(8,128)S(1)}) fusion(pred[32]{0:T(512)(128)(4,1)S(1)} %broadcast_compare_fusion.1, f32[32,128,128]{2,1,0:T(8,128)} %copy-done.7, f32[32,128,128]{2,1,0:T(8,128)} %scatter_fusion.3, f32[32,128,128]{2,1,0:T(8,128)} %get-tuple-element.46, f32[32,128]{1,0:T(8,128)S(1)} %bitcast.332, ...), kind=kLoop, calls=%fused_computation.106 | loop fusion | flops 12058624 | bytes 18927776 | tf_op jit(solution)/shard_map/stack | solution.py:150
  334.5 3.9 %collective-permute-start.17 = (f32[8,1,128]{2,0,1:T(8,128)S(1)}, f32[8,1,128]{2,0,1:T(8,128)S(1)}, u32[]{:S(2)}, u32[]{:S(2)}) collective-permute-start(f32[8,1,128]{2,0,1:T(8,128)S(1)} %bitcast_select_fusion.16), channel_id=1, source_target_pairs={{0,1},{1,2},{2,3},{3,4},{4,5},{5,6},{6,7},{7,8},{8,9},{9,10},{10,1... | collective-permute-start | bytes 12296 | tf_op jit(solution)/shard_map/ppermute | solution.py:20
  338.4 4.0 %pad_maximum_fusion = f32[32,2,128,128]{3,2,0,1:T(8,128)} fusion(f32[32,1,128,128]{3,2,0,1:T(8,128)S(1)} %copy-done.16, f32[32,1,128,128]{3,2,0,1:T(8,128)} %get-tuple-element.28), kind=kLoop, calls=%fused_computation.60 | loop fusion | flops 1048576 | bytes 8388608 | tf_op jit(solution)/shard_map/stack | solution.py:150
  343.0 4.8 %copy.265 = f32[32,2,128,128]{3,2,1,0:T(8,128)} copy(f32[32,2,128,128]{3,2,0,1:T(8,128)} %pad_maximum_fusion) | data formatting | bytes 8388608
  348.5 6.2 %fusion.19 = f32[32,128,128]{2,1,0:T(8,128)} fusion(f32[32,128,128]{2,1,0:T(8,128)S(1)} %copy-done.4, f32[32,128,128]{2,1,0:T(8,128)} %copy-done.14, f32[32,127,128]{2,1,0:T(8,128)} %bitcast.296, f32[32,1,128]{2,1,0:T(1,128)S(1)} %slice.610, f32[32,128,128]{2,1,0:T(8,128)} %copy-done.13, f32[32,128,127]{2,1,0:T(8,128)} %bitcast.295, ...), kind=kLoop, calls=%fused_computation.102 | loop fusion | flops 5242880 | bytes 12615840 | tf_op jit(solution)/shard_map/jit(_where)/select_n | solution.py:149
  (275 shorter events, 177.0 us)
Async XLA Ops:
  1.4 8.9 %copy-start.19 = (f32[32,128,128]{2,1,0:T(8,128)S(1)}, f32[32,128,128]{2,1,0:T(8,128)}, u32[]{:S(2)}) copy-start(f32[32,128,128]{2,1,0:T(8,128)} %param.27) | copy-start | bytes 6291460
  14.7 60.8 %collective-permute-start = (f32[8,5,128,128]{3,2,1,0:T(8,128)}, f32[8,5,128,128]{3,2,1,0:T(8,128)}, u32[]{:S(2)}, u32[]{:S(2)}) collective-permute-start(f32[8,5,128,128]{3,2,1,0:T(8,128)} %pad_maximum_fusion.1), channel_id=1, source_target_pairs={{0,1},{1,2},{2,3},{3,4},{4,5},{5,6},{6,7},{7,8},{8,9},{9,10},{10,1... | collective-permute-start | bytes 7864328 | tf_op jit(solution)/shard_map/ppermute | solution.py:20
  27.9 5.9 %copy-start.22 = (s32[1,2,8,2]{2,3,1,0:T(2,128)S(1)}, s32[1,2,8,2]{2,3,1,0:T(2,128)}, u32[]{:S(2)}) copy-start(s32[1,2,8,2]{2,3,1,0:T(2,128)} %param.33) | copy-start | bytes 388
  27.9 5.9 %copy-start.21 = (s32[32,4]{0,1:T(4,128)S(1)}, s32[32,4]{0,1:T(4,128)}, u32[]{:S(2)}) copy-start(s32[32,4]{0,1:T(4,128)} %param.32) | copy-start | bytes 1540
  31.0 62.6 %collective-permute-start.1 = (f32[8,5,128,128]{3,2,1,0:T(8,128)}, f32[8,5,128,128]{3,2,1,0:T(8,128)}, u32[]{:S(2)}, u32[]{:S(2)}) collective-permute-start(f32[8,5,128,128]{3,2,1,0:T(8,128)} %pad_maximum_fusion.2), channel_id=1, source_target_pairs={{1,0},{2,1},{3,2},{4,3},{5,4},{6,5},{7,6},{8,7},{9,8},{10,9},{11,1... | collective-permute-start | bytes 7864328 | tf_op jit(solution)/shard_map/ppermute | solution.py:20
  117.7 18.3 %collective-permute-start.2 = (f32[4,3,128]{2,1,0:T(4,128)S(1)}, f32[4,3,128]{2,1,0:T(4,128)S(1)}, u32[]{:S(2)}, u32[]{:S(2)}) collective-permute-start(f32[4,3,128]{2,1,0:T(4,128)S(1)} %broadcast_select_fusion.11), channel_id=1, source_target_pairs={{16,0},{32,16},{48,32},{64,48},{80,64},{96,80},{112,96},{17,1},{33... | collective-permute-start | bytes 18440 | tf_op jit(solution)/shard_map/ppermute | solution.py:20
  129.6 27.5 %collective-permute-start.4 = (f32[8,3,128]{2,1,0:T(4,128)S(1)}, f32[8,3,128]{2,1,0:T(4,128)S(1)}, u32[]{:S(2)}, u32[]{:S(2)}) collective-permute-start(f32[8,3,128]{2,1,0:T(4,128)S(1)} %broadcast_select_fusion.7), channel_id=1, source_target_pairs={{1,0},{2,1},{3,2},{4,3},{5,4},{6,5},{7,6},{8,7},{9,8},{10,9},{11,1... | collective-permute-start | bytes 36872 | tf_op jit(solution)/shard_map/ppermute | solution.py:20
  145.7 10.9 %collective-permute-start.3 = (f32[4,1,128]{2,0,1:T(4,128)S(1)}, f32[4,1,128]{2,0,1:T(4,128)S(1)}, u32[]{:S(2)}, u32[]{:S(2)}) collective-permute-start(f32[4,1,128]{2,0,1:T(4,128)S(1)} %bitcast_select_fusion.23), channel_id=1, source_target_pairs={{0,16},{16,32},{32,48},{48,64},{64,80},{80,96},{96,112},{1,17},{17... | collective-permute-start | bytes 6152 | tf_op jit(solution)/shard_map/ppermute | solution.py:20
  170.3 7.0 %collective-permute-start.5 = (f32[8,1,128]{2,0,1:T(8,128)S(1)}, f32[8,1,128]{2,0,1:T(8,128)S(1)}, u32[]{:S(2)}, u32[]{:S(2)}) collective-permute-start(f32[8,1,128]{2,0,1:T(8,128)S(1)} %bitcast_select_fusion.19), channel_id=1, source_target_pairs={{0,1},{1,2},{2,3},{3,4},{4,5},{5,6},{6,7},{7,8},{8,9},{9,10},{10,1... | collective-permute-start | bytes 12296 | tf_op jit(solution)/shard_map/ppermute | solution.py:20
  186.4 9.1 %collective-permute-start.6 = (f32[4,3,128]{2,1,0:T(4,128)S(1)}, f32[4,3,128]{2,1,0:T(4,128)S(1)}, u32[]{:S(2)}, u32[]{:S(2)}) collective-permute-start(f32[4,3,128]{2,1,0:T(4,128)S(1)} %broadcast_select_fusion.10), channel_id=1, source_target_pairs={{16,0},{32,16},{48,32},{64,48},{80,64},{96,80},{112,96},{17,1},{33... | collective-permute-start | bytes 18440 | tf_op jit(solution)/shard_map/ppermute | solution.py:20
  193.6 19.1 %collective-permute-start.8 = (f32[8,3,128]{2,1,0:T(4,128)S(1)}, f32[8,3,128]{2,1,0:T(4,128)S(1)}, u32[]{:S(2)}, u32[]{:S(2)}) collective-permute-start(f32[8,3,128]{2,1,0:T(4,128)S(1)} %broadcast_select_fusion.6), channel_id=1, source_target_pairs={{1,0},{2,1},{3,2},{4,3},{5,4},{6,5},{7,6},{8,7},{9,8},{10,9},{11,1... | collective-permute-start | bytes 36872 | tf_op jit(solution)/shard_map/ppermute | solution.py:20
  205.2 6.9 %collective-permute-start.7 = (f32[4,1,128]{2,0,1:T(4,128)S(1)}, f32[4,1,128]{2,0,1:T(4,128)S(1)}, u32[]{:S(2)}, u32[]{:S(2)}) collective-permute-start(f32[4,1,128]{2,0,1:T(4,128)S(1)} %bitcast_select_fusion.22), channel_id=1, source_target_pairs={{0,16},{16,32},{32,48},{48,64},{64,80},{80,96},{96,112},{1,17},{17... | collective-permute-start | bytes 6152 | tf_op jit(solution)/shard_map/ppermute | solution.py:20
  222.8 7.3 %collective-permute-start.9 = (f32[8,1,128]{2,0,1:T(8,128)S(1)}, f32[8,1,128]{2,0,1:T(8,128)S(1)}, u32[]{:S(2)}, u32[]{:S(2)}) collective-permute-start(f32[8,1,128]{2,0,1:T(8,128)S(1)} %bitcast_select_fusion.18), channel_id=1, source_target_pairs={{0,1},{1,2},{2,3},{3,4},{4,5},{5,6},{6,7},{7,8},{8,9},{9,10},{10,1... | collective-permute-start | bytes 12296 | tf_op jit(solution)/shard_map/ppermute | solution.py:20
  238.9 9.1 %collective-permute-start.10 = (f32[4,3,128]{2,1,0:T(4,128)S(1)}, f32[4,3,128]{2,1,0:T(4,128)S(1)}, u32[]{:S(2)}, u32[]{:S(2)}) collective-permute-start(f32[4,3,128]{2,1,0:T(4,128)S(1)} %broadcast_select_fusion.9), channel_id=1, source_target_pairs={{16,0},{32,16},{48,32},{64,48},{80,64},{96,80},{112,96},{17,1},{33... | collective-permute-start | bytes 18440 | tf_op jit(solution)/shard_map/ppermute | solution.py:20
  246.1 19.1 %collective-permute-start.12 = (f32[8,3,128]{2,1,0:T(4,128)S(1)}, f32[8,3,128]{2,1,0:T(4,128)S(1)}, u32[]{:S(2)}, u32[]{:S(2)}) collective-permute-start(f32[8,3,128]{2,1,0:T(4,128)S(1)} %broadcast_select_fusion.5), channel_id=1, source_target_pairs={{1,0},{2,1},{3,2},{4,3},{5,4},{6,5},{7,6},{8,7},{9,8},{10,9},{11,1... | collective-permute-start | bytes 36872 | tf_op jit(solution)/shard_map/ppermute | solution.py:20
  248.9 11.0 %copy-start.23 = (s32[32]{0:T(128)S(1)}, s32[32]{0:T(128)}, u32[]{:S(2)}) copy-start(s32[32]{0:T(128)} %param.31) | copy-start | bytes 388
  257.7 7.0 %collective-permute-start.11 = (f32[4,1,128]{2,0,1:T(4,128)S(1)}, f32[4,1,128]{2,0,1:T(4,128)S(1)}, u32[]{:S(2)}, u32[]{:S(2)}) collective-permute-start(f32[4,1,128]{2,0,1:T(4,128)S(1)} %bitcast_select_fusion.21), channel_id=1, source_target_pairs={{0,16},{16,32},{32,48},{48,64},{64,80},{80,96},{96,112},{1,17},{17... | collective-permute-start | bytes 6152 | tf_op jit(solution)/shard_map/ppermute | solution.py:20
  275.4 7.1 %collective-permute-start.13 = (f32[8,1,128]{2,0,1:T(8,128)S(1)}, f32[8,1,128]{2,0,1:T(8,128)S(1)}, u32[]{:S(2)}, u32[]{:S(2)}) collective-permute-start(f32[8,1,128]{2,0,1:T(8,128)S(1)} %bitcast_select_fusion.17), channel_id=1, source_target_pairs={{0,1},{1,2},{2,3},{3,4},{4,5},{5,6},{6,7},{7,8},{8,9},{9,10},{10,1... | collective-permute-start | bytes 12296 | tf_op jit(solution)/shard_map/ppermute | solution.py:20
  291.6 7.1 %collective-permute-start.14 = (f32[4,3,128]{2,1,0:T(4,128)S(1)}, f32[4,3,128]{2,1,0:T(4,128)S(1)}, u32[]{:S(2)}, u32[]{:S(2)}) collective-permute-start(f32[4,3,128]{2,1,0:T(4,128)S(1)} %broadcast_select_fusion.8), channel_id=1, source_target_pairs={{16,0},{32,16},{48,32},{64,48},{80,64},{96,80},{112,96},{17,1},{33... | collective-permute-start | bytes 18440 | tf_op jit(solution)/shard_map/ppermute | solution.py:20
  308.9 9.2 %collective-permute-start.15 = (f32[4,1,128]{2,0,1:T(4,128)S(1)}, f32[4,1,128]{2,0,1:T(4,128)S(1)}, u32[]{:S(2)}, u32[]{:S(2)}) collective-permute-start(f32[4,1,128]{2,0,1:T(4,128)S(1)} %bitcast_select_fusion.20), channel_id=1, source_target_pairs={{0,16},{16,32},{32,48},{48,64},{64,80},{80,96},{96,112},{1,17},{17... | collective-permute-start | bytes 6152 | tf_op jit(solution)/shard_map/ppermute | solution.py:20
  315.3 7.7 %collective-permute-start.16 = (f32[8,3,128]{2,1,0:T(4,128)S(1)}, f32[8,3,128]{2,1,0:T(4,128)S(1)}, u32[]{:S(2)}, u32[]{:S(2)}) collective-permute-start(f32[8,3,128]{2,1,0:T(4,128)S(1)} %broadcast_select_fusion.4), channel_id=1, source_target_pairs={{1,0},{2,1},{3,2},{4,3},{5,4},{6,5},{7,6},{8,7},{9,8},{10,9},{11,1... | collective-permute-start | bytes 36872 | tf_op jit(solution)/shard_map/ppermute | solution.py:20
  331.7 6.7 %copy-start.16 = (f32[32,1,128,128]{3,2,0,1:T(8,128)S(1)}, f32[32,1,128,128]{3,2,0,1:T(8,128)}, u32[]{:S(2)}) copy-start(f32[32,1,128,128]{3,2,0,1:T(8,128)} %get-tuple-element.30) | copy-start | bytes 6291460
  334.5 13.3 %collective-permute-start.17 = (f32[8,1,128]{2,0,1:T(8,128)S(1)}, f32[8,1,128]{2,0,1:T(8,128)S(1)}, u32[]{:S(2)}, u32[]{:S(2)}) collective-permute-start(f32[8,1,128]{2,0,1:T(8,128)S(1)} %bitcast_select_fusion.16), channel_id=1, source_target_pairs={{0,1},{1,2},{2,3},{3,4},{4,5},{5,6},{6,7},{7,8},{8,9},{9,10},{10,1... | collective-permute-start | bytes 12296 | tf_op jit(solution)/shard_map/ppermute | solution.py:20
  343.0 5.5 %copy-start.4 = (f32[32,128,128]{2,1,0:T(8,128)S(1)}, f32[32,128,128]{2,1,0:T(8,128)}, u32[]{:S(2)}) copy-start(f32[32,128,128]{2,1,0:T(8,128)} %copy-done.3) | copy-start | bytes 6291460
  (18 other events, 45.7 us)
where the time goes:
time: 357 us; the launch traced here: 355 us
  local copies, waits for them, and re-layouts  139 us (39%)
  other arithmetic  106 us (30%)
  starting transfers between devices  54.2 us (15%)
  waiting for transfers between devices  53.1 us (15%)
    ppermute x18, starting transfers between devices, shifted(): return lax.ppermute(block, axis, route)  54.2 us
    ppermute x18, waiting for transfers between devices, shifted(): return lax.ppermute(block, axis, route)  53.1 us
    slice x12, local copies, waits for them, and re-layouts, shards(): h_rt = jnp.where(inside_y, jnp.roll(h, -1, 2), right[:, 0, :][:, :, None])  23.7 us
    select_n x3, other arithmetic, shards(): jnp.where(inside_y | exists[:, 3][:, None, None], face_flux(qy, h, h_rt,...  22.9 us
    select_n x3, other arithmetic, shards(): jnp.where(inside_x | exists[:, 1][:, None, None], face_flux(qx, h, h_hi,...  20.3 us
    another operation x3, other arithmetic, shards(): jnp.stack([jnp.where(live, qx, 0.0), jnp.where(live, qy, 0.0)], 1)  19.1 us
    add x3, other arithmetic, shards(): h = h + step_time / spacing * (in_x - qx_new + (in_y - qy_new))  16.6 us
    unnamed x50, local copies, waits for them, and re-layouts  14.5 us
  transfers between devices with their start and end apart: 18, of which 6 were waited for; matrix products, arithmetic and copies ran while one was open for 32% of the time, Pallas kernels for 0%

commit v1 on v0

v1 whole, which is shorter than its diff:
```python
import jax
import jax.numpy as jnp
from jax import lax
from jax.experimental import pallas as pl
from jax.experimental.pallas import tpu as pltpu
from jax.sharding import PartitionSpec as P

TILE = 128
SLOTS = 32
MOVERS = 8
DEPTH = 4
STRIPS = 2 * DEPTH
ROUNDS = 4
PER_ROUND = MOVERS // ROUNDS
FIELD = STRIPS * TILE
CHUNK_ROWS = PER_ROUND * 5 * TILE
GROUP = 8
BUFFERS = 4

gravity = 9.81
step_time = 0.25
spacing = 2.0
min_depth = 0.15
PULL = gravity * step_time / spacing
RUB = gravity * step_time * 0.5
GAIN = step_time / spacing

f32 = jnp.float32
bf16 = jnp.bfloat16
i32 = jnp.int32


def flux(flow, h_lo, h_hi, slope, rub):
    depth_face = jnp.maximum(0.5 * (h_lo + h_hi), min_depth)
    drive = flow - (PULL * depth_face) * ((h_hi - h_lo) + slope)
    loss = jnp.exp2(jnp.log2(depth_face) * (-7.0 / 3.0))
    return drive / (1.0 + (rub * jnp.abs(flow)) * loss)


def iota(shape, dim):
    return lax.broadcasted_iota(i32, shape, dim)


def route(onehot, rows):
    a = rows.astype(bf16)
    rest = rows - a.astype(f32)
    b = rest.astype(bf16)
    c = (rest - b.astype(f32)).astype(bf16)
    take = onehot.astype(bf16)

    def part(x):
        return jnp.dot(take, x, preferred_element_type=f32)

    return part(a) + part(b) + part(c)


def side_links(nb_ref, base, side):
    link = nb_ref[:, side : side + 1].astype(f32) - base.astype(f32)
    missing = nb_ref[:, side : side + 1] < 0
    local = (link >= 0.0) & (link < SLOTS)
    far = jnp.where(missing | local, 0.0, 1.0)
    square = (SLOTS, SLOTS)
    rows = iota(square, 0)
    cols = iota(square, 1)
    link_b = jnp.broadcast_to(link, square)
    far_b = jnp.broadcast_to(far, square)
    near = jnp.where(link_b == cols.astype(f32), 1.0, 0.0)
    link_row = jnp.sum(jnp.where(rows == cols, link_b, 0.0), 0, keepdims=True)
    far_row = jnp.sum(jnp.where(rows == cols, far_b, 0.0), 0, keepdims=True)
    rank = jnp.sum(jnp.where(link_row < link_b, jnp.broadcast_to(far_row, square), 0.0), 1, keepdims=True)
    order_row = jnp.sum(jnp.where(rows < cols, far_b, 0.0), 0, keepdims=True)
    place = jnp.where(
        (jnp.broadcast_to(rank, (SLOTS, MOVERS)) == iota((SLOTS, MOVERS), 1).astype(f32))
        & (jnp.broadcast_to(far, (SLOTS, MOVERS)) > 0.0),
        1.0,
        0.0,
    )
    pick = jnp.where(
        (jnp.broadcast_to(order_row, (MOVERS, SLOTS)) == iota((MOVERS, SLOTS), 0).astype(f32))
        & (jnp.broadcast_to(far_row, (MOVERS, SLOTS)) > 0.0),
        1.0,
        0.0,
    )
    exists = jnp.where(missing, 0.0, 1.0)
    return near, place, pick, exists


def halo_of(links, rows, message):
    near, place, _, _ = links
    return route(near, rows) + route(place, message)


def extract_kernel(moves, base, depth, discharge, bed, friction, frames, up_out, down_out, lo_acc, hi_acc, turned):
    g = pl.program_id(0)
    lane = iota((TILE, TILE), 1)

    def strip(f, k):
        return pl.ds((f * STRIPS + k) * TILE, TILE)

    sources = ((depth, 0, 1), (discharge, 0, 2), (discharge, 1, 2), (bed, 0, 1), (friction, 0, 1))
    home = pl.ds(pl.multiple_of(g * GROUP, GROUP), GROUP)
    for f, (ref, part, parts) in enumerate(sources):
        for k in range(STRIPS):
            row = k if k < DEPTH else TILE - STRIPS + k
            frames[home, strip(f, k)] = ref[pl.ds(part * TILE + row, GROUP, stride=parts * TILE), :]
        high = None
        low = None
        for t in range(GROUP):
            tile = ref[pl.ds((t * parts + part) * TILE, TILE), :]
            turn = pltpu.roll(tile, DEPTH * t + DEPTH, 1)
            high = turn if t == 0 else jnp.where(lane >= DEPTH * t, turn, high)
            low = turn if t == 0 else jnp.where(lane >= DEPTH * t + DEPTH, turn, low)
        shift = g * (GROUP * DEPTH)
        high = pltpu.roll(high, shift, 1)
        low = pltpu.roll(low, shift, 1)
        hi_acc[f] = jnp.where(lane // (GROUP * DEPTH) == g, high, hi_acc[f])
        lo_acc[f] = jnp.where(((lane + (TILE - DEPTH)) % TILE) // (GROUP * DEPTH) == g, low, lo_acc[f])

    @pl.when(g == pl.num_programs(0) - 1)
    def _():
        for f in range(5):
            to = (0, 2, 1, 3, 4)[f]
            for half in range(2):
                block = hi_acc[f] if half else pltpu.roll(lo_acc[f], TILE - DEPTH, 1)
                turned[...] = block.T
                for k in range(DEPTH):
                    frames[pl.ds(SLOTS, SLOTS), strip(to, half * DEPTH + k)] = turned[pl.ds(k, SLOTS, stride=DEPTH), :]
        shape = (2 * MOVERS, SLOTS)
        pick = jnp.zeros(shape, f32)
        for m in range(MOVERS):
            for way in range(2):
                leaver = moves[way, m, 0] - base[0]
                spot = (iota(shape, 0) == (1 - way) * MOVERS + m) & (iota(shape, 1) == leaver)
                pick = jnp.where(spot, 1.0, pick)
        width = FIELD
        for axis in range(2):
            for c in range(5):
                got = route(pick, frames[pl.ds(axis * SLOTS, SLOTS), pl.ds(c * width, width)])
                to = pl.ds((axis * 5 + c) * width, width)
                up_out[:, to] = got[:MOVERS]
                down_out[:, to] = got[MOVERS:]


def start_chunk(index, moves, base, tiles, box, sem):
    depth, discharge, bed, friction = tiles
    for way in range(2):
        for i in range(PER_ROUND):
            slot = jnp.clip(moves[1 - way, index * PER_ROUND + i, 0] - base[0], 0, SLOTS - 1)
            at = (way * PER_ROUND + i) * 5 * TILE
            one = pl.ds(pl.multiple_of(slot * TILE, TILE), TILE)
            two = pl.ds(pl.multiple_of(slot * (2 * TILE), TILE), 2 * TILE)
            pltpu.make_async_copy(depth.at[one], box.at[pl.ds(at, TILE)], sem).start()
            pltpu.make_async_copy(discharge.at[two], box.at[pl.ds(at + TILE, 2 * TILE)], sem).start()
            pltpu.make_async_copy(bed.at[one], box.at[pl.ds(at + 3 * TILE, TILE)], sem).start()
            pltpu.make_async_copy(friction.at[one], box.at[pl.ds(at + 4 * TILE, TILE)], sem).start()


def forward_chunk(box, up_out, down_out, sem, out_sem):
    pltpu.make_async_copy(box, box, sem).wait()
    body = pl.ds(0, CHUNK_ROWS)
    for way, out in enumerate((up_out, down_out)):
        pltpu.make_async_copy(box.at[pl.ds(way * CHUNK_ROWS, CHUNK_ROWS)], out.at[body], out_sem.at[way]).start()


def finish_chunk(extra_up, extra_down, up_out, down_out, out_sem):
    edge = pl.ds(CHUNK_ROWS, extra_up.shape[0])
    pltpu.make_async_copy(extra_up, up_out.at[edge], out_sem.at[2]).start()
    pltpu.make_async_copy(extra_down, down_out.at[edge], out_sem.at[3]).start()
    body = pl.ds(0, CHUNK_ROWS)
    for way, out in enumerate((up_out, down_out)):
        pltpu.make_async_copy(out.at[body], out.at[body], out_sem.at[way]).wait()
        pltpu.make_async_copy(out.at[edge], out.at[edge], out_sem.at[2 + way]).wait()


def settle_kernel(
    moves, base, nb, frames, from_low, from_high, depth, discharge, bed, friction,
    dyn, fixed, x_up, x_down, y_up, y_down, edge_up, edge_down, box, sem, out_sem,
):
    start_chunk(0, moves, base, (depth, discharge, bed, friction), box, sem)
    shape = (SLOTS, 2 * MOVERS)
    land = jnp.zeros(shape, f32)
    left = jnp.zeros((SLOTS, TILE), f32)
    for m in range(MOVERS):
        for way in range(2):
            lander = moves[way, m, 1] - base[0]
            leaver = moves[way, m, 0] - base[0]
            spot = (iota(shape, 0) == lander) & (iota(shape, 1) == way * MOVERS + m)
            land = jnp.where(spot, 1.0, land)
            row = iota((SLOTS, TILE), 0)
            left = jnp.where((row == leaver) | (row == lander), 1.0, left)
    for axis in range(2):
        home = pl.ds(axis * SLOTS, SLOTS)
        for f in range(5):
            part = pl.ds(f * FIELD, FIELD)
            came = pl.ds((axis * 5 + f) * FIELD, FIELD)
            fresh = route(land, jnp.concatenate([from_low[:, came], from_high[:, came]], 0))
            for k in range(STRIPS):
                sub = pl.ds(f * FIELD + k * TILE, TILE)
                value = jnp.where(left > 0.0, 0.0, frames[home, sub]) + fresh[:, k * TILE : (k + 1) * TILE]
                if f < 3:
                    dyn[home, sub] = value
                else:
                    fixed[home, pl.ds((f - 3) * FIELD + k * TILE, TILE)] = value

    forward_chunk(box, y_up, y_down, sem, out_sem)

    def edge(ref, axis, f, k):
        return ref[pl.ds(axis * SLOTS, SLOTS), pl.ds(f * FIELD + k * TILE, TILE)]

    last = STRIPS - 1
    for axis, up, down in ((0, x_up, x_down), (1, edge_up, edge_down)):
        lower = side_links(nb, base[0], 2 * axis)
        higher = side_links(nb, base[0], 2 * axis + 1)
        ups = (edge(dyn, axis, 0, last), edge(fixed, axis, 0, last), edge(fixed, axis, 1, last), edge(dyn, axis, 1, last))
        downs = (edge(dyn, axis, 0, 0), edge(fixed, axis, 0, 0), edge(fixed, axis, 1, 0))
        for f, rows in enumerate(ups):
            up[pl.ds(f * MOVERS, MOVERS), :] = route(higher[2], rows)
        for f, rows in enumerate(downs):
            down[pl.ds(f * MOVERS, MOVERS), :] = route(lower[2], rows)
        down[pl.ds(3 * MOVERS, MOVERS), :] = jnp.zeros((MOVERS, TILE), f32)
    finish_chunk(edge_up, edge_down, y_up, y_down, out_sem)


def other_axis(x):
    return jnp.concatenate([x[SLOTS:], x[:SLOTS]], 0)


def gather_halos(nb, base, dyn, fixed, messages, first):
    last = STRIPS - 1
    out = {}
    parts = {name: [] for name in ("h_lo", "h_hi", "z_lo", "n_lo", "q_lo", "z_hi", "n_hi", "lo", "hi")}
    picks = []
    for axis in range(2):
        home = pl.ds(axis * SLOTS, SLOTS)
        lower = side_links(nb, base, 2 * axis)
        higher = side_links(nb, base, 2 * axis + 1)
        picks.append((lower[2], higher[2]))
        from_lower, from_higher = messages[axis]

        def strip(ref, f, k):
            return ref[home, pl.ds(f * FIELD + k * TILE, TILE)]

        def low(f, rows):
            return halo_of(lower, rows, from_lower[pl.ds(f * MOVERS, MOVERS), :])

        def high(f, rows):
            return halo_of(higher, rows, from_higher[pl.ds(f * MOVERS, MOVERS), :])

        parts["h_lo"].append(low(0, strip(dyn, 0, last)))
        parts["h_hi"].append(high(0, strip(dyn, 0, 0)))
        if first:
            parts["z_lo"].append(low(1, strip(fixed, 0, last)))
            parts["n_lo"].append(low(2, strip(fixed, 1, last)))
            parts["q_lo"].append(low(3, strip(dyn, 1, last)))
            parts["z_hi"].append(high(1, strip(fixed, 0, 0)))
            parts["n_hi"].append(high(2, strip(fixed, 1, 0)))
        parts["lo"].append(jnp.broadcast_to(lower[3], (SLOTS, TILE)))
        parts["hi"].append(jnp.broadcast_to(higher[3], (SLOTS, TILE)))
    for name, pieces in parts.items():
        if pieces:
            out[name] = jnp.concatenate(pieces, 0)
    return out, picks


def step_kernel(turn, moves, base, nb, dyn, fixed, *rest):
    first = turn == 0
    if first:
        still = None
        (xl, xh, yl, yh), rest = rest[:4], rest[4:]
    else:
        still = rest[0]
        (xl, xh, yl, yh), rest = rest[1:5], rest[5:]
    depth, discharge, bed, friction = rest[:4]
    (dyn_out, still_out, trail, x_up, x_down, y_up, y_down, edge_up, edge_down, box, sem, out_sem) = rest[4:]
    start_chunk(turn + 1, moves, base, (depth, discharge, bed, friction), box, sem)
    halo, picks = gather_halos(nb, base[0], dyn, fixed, ((xl, xh), (yl, yh)), first)
    names = ("z_lo", "n_lo", "z_hi", "n_hi", "q_lo")
    if not first:
        for j, name in enumerate(names):
            halo[name] = still[:, pl.ds(j * TILE, TILE)]

    def get(ref, f, k):
        return ref[:, pl.ds(f * FIELD + k * TILE, TILE)]

    last = STRIPS - 1
    h = [get(dyn, 0, k) for k in range(STRIPS)]
    z = [get(fixed, 0, k) for k in range(STRIPS)]
    n = [get(fixed, 1, k) for k in range(STRIPS)]
    low_face = flux(halo["q_lo"], halo["h_lo"], h[0], z[0] - halo["z_lo"], RUB * (halo["n_lo"] + n[0]))
    low_face = jnp.where(halo["lo"] > 0.0, low_face, 0.0)
    high_face = flux(get(dyn, 1, last), h[last], halo["h_hi"], halo["z_hi"] - z[last], RUB * (n[last] + halo["n_hi"]))
    high_face = jnp.where(halo["hi"] > 0.0, high_face, 0.0)
    for j, name in enumerate(names[:4]):
        still_out[:, pl.ds(j * TILE, TILE)] = halo[name]
    still_out[:, pl.ds(4 * TILE, TILE)] = low_face
    trail[:, pl.ds(0, TILE)] = low_face
    trail[:, pl.ds(TILE, TILE)] = halo["h_hi"]

    forward_chunk(box, y_up, y_down, sem, out_sem)
    lane = iota((2 * SLOTS, TILE), 1)
    side_h = other_axis(halo["h_hi"])
    side_z = other_axis(halo["z_hi"])
    side_n = other_axis(halo["n_hi"])
    side_wall = other_axis(halo["hi"]) <= 0.0
    side_in = other_axis(low_face)

    def cell(x, k):
        at = k if k < DEPTH else TILE - STRIPS + k
        return jnp.broadcast_to(x[:, at : at + 1], x.shape)

    def ahead(x, k, side):
        return jnp.where(lane == TILE - 1, cell(side, k), pltpu.roll(x, TILE - 1, 1))

    reach = DEPTH - 1 - turn
    low_keep = list(range(reach))
    high_keep = list(range(STRIPS - reach, STRIPS))
    face = {-1: low_face, last: high_face}
    for k in low_keep + [x - 1 for x in high_keep]:
        face[k] = flux(get(dyn, 1, k), h[k], h[k + 1], z[k + 1] - z[k], RUB * (n[k] + n[k + 1]))
    new = {}
    for k in low_keep + high_keep:
        side = flux(
            get(dyn, 2, k), h[k], ahead(h[k], k, side_h), ahead(z[k], k, side_z) - z[k],
            RUB * (n[k] + ahead(n[k], k, side_n)),
        )
        side = jnp.where((lane == TILE - 1) & side_wall, 0.0, side)
        before = jnp.where(lane == 0, cell(side_in, k), pltpu.roll(side, 1, 1))
        new[k] = h[k] + GAIN * ((face[k - 1] - face[k]) + (before - side))
        dyn_out[:, pl.ds(2 * FIELD + k * TILE, TILE)] = side
    blank = jnp.zeros((2 * SLOTS, TILE), f32)
    for k in range(STRIPS):
        dyn_out[:, pl.ds(k * TILE, TILE)] = new[k] if k in new else blank
        dyn_out[:, pl.ds(FIELD + k * TILE, TILE)] = face[k] if k in face else blank
        if k not in new:
            dyn_out[:, pl.ds(2 * FIELD + k * TILE, TILE)] = blank
    for axis, up, down in ((0, x_up, x_down), (1, edge_up, edge_down)):
        home = slice(axis * SLOTS, (axis + 1) * SLOTS)
        up[...] = route(picks[axis][1], new[last][home])
        down[...] = route(picks[axis][0], new[0][home])
    finish_chunk(edge_up, edge_down, y_up, y_down, out_sem)


def tile_kernel(
    moves, base, ids, nb_s, nb, dyn, fixed, still, xl, xh, yl, yh, t0, t1, t2,
    depth, discharge, bed, friction, l0, l1, l2, l3, u0, u1, u2, u3,
    depth_out, flow_out,
    inbox, outbox, zeros, edges, columns, turned, water, stream_x, stream_y, slope_x, slope_y, rub_x, rub_y, origin,
    in_sem, out_sem, zero_sem,
):
    lows = (l0, l1, l2, l3)
    highs = (u0, u1, u2, u3)

    def count_live(t, total):
        origin[t] = 0
        return total + jnp.where(ids[t] >= 0, 1, 0)

    live = lax.fori_loop(0, SLOTS, count_live, 0)
    for m in range(MOVERS):
        for way in range(2):
            lander = moves[way, m, 1]

            @pl.when(lander >= 0)
            def _():
                origin[lander - base[0]] = 1 + way * MOVERS + m

    def fetch(t):
        buf = t % BUFFERS
        sem = in_sem.at[buf]
        box = inbox.at[buf]
        kind = origin[t]

        @pl.when(kind == 0)
        def _():
            one = pl.ds(pl.multiple_of(t * TILE, TILE), TILE)
            two = pl.ds(pl.multiple_of(t * (2 * TILE), TILE), 2 * TILE)
            pltpu.make_async_copy(depth.at[one], box.at[pl.ds(0, TILE)], sem).start()
            pltpu.make_async_copy(discharge.at[two], box.at[pl.ds(TILE, 2 * TILE)], sem).start()
            pltpu.make_async_copy(bed.at[one], box.at[pl.ds(3 * TILE, TILE)], sem).start()
            pltpu.make_async_copy(friction.at[one], box.at[pl.ds(4 * TILE, TILE)], sem).start()

        for way, chunks in ((0, lows), (1, highs)):
            for m in range(MOVERS):

                @pl.when(kind == 1 + way * MOVERS + m)
                def _():
                    src = chunks[m // PER_ROUND].at[pl.ds((m % PER_ROUND) * 5 * TILE, 5 * TILE)]
                    pltpu.make_async_copy(src, box, sem).start()

    def arrived(buf):
        box = inbox.at[buf]
        pltpu.make_async_copy(box, box, in_sem.at[buf]).wait()

    def send(t, buf):
        box = outbox.at[buf]
        one = pl.ds(pl.multiple_of(t * TILE, TILE), TILE)
        two = pl.ds(pl.multiple_of(t * (2 * TILE), TILE), 2 * TILE)
        pltpu.make_async_copy(box.at[pl.ds(0, TILE)], depth_out.at[one], out_sem.at[buf]).start()
        pltpu.make_async_copy(box.at[pl.ds(TILE, 2 * TILE)], flow_out.at[two], out_sem.at[buf]).start()

    def sent(buf):
        box = outbox.at[buf]
        pltpu.make_async_copy(box, box, out_sem.at[buf]).wait()

    for t in range(BUFFERS - 1):

        @pl.when(t < live)
        def _():
            fetch(t)

    zeros[...] = jnp.zeros(zeros.shape, f32)

    def blank(t, carry):
        one = pl.ds(pl.multiple_of(t * TILE, TILE), TILE)
        two = pl.ds(pl.multiple_of(t * (2 * TILE), TILE), 2 * TILE)
        pltpu.make_async_copy(zeros.at[pl.ds(0, TILE)], depth_out.at[one], zero_sem).start()
        pltpu.make_async_copy(zeros.at[pl.ds(TILE, 2 * TILE)], flow_out.at[two], zero_sem).start()
        return carry

    lax.fori_loop(live, SLOTS, blank, 0)

    last = STRIPS - 1
    halo, _ = gather_halos(nb, base[0], dyn, fixed, ((xl, xh), (yl, yh)), False)

    def kept(j):
        return still[:, pl.ds(j * TILE, TILE)]

    n_first = fixed[:, pl.ds(FIELD, TILE)]
    z_first = fixed[:, pl.ds(0, TILE)]
    low_face = flux(
        kept(4), halo["h_lo"], dyn[:, pl.ds(0, TILE)], z_first - kept(0), RUB * (kept(1) + n_first)
    )
    low_face = jnp.where(halo["lo"] > 0.0, low_face, 0.0)
    trails = [(t[:, pl.ds(0, TILE)], t[:, pl.ds(TILE, TILE)]) for t in (t0, t1, t2)]
    trails.append((low_face, halo["h_hi"]))
    for s, (inflow, ahead_h) in enumerate(trails):
        edges[s] = inflow[:SLOTS]
        edges[4 + s] = ahead_h[:SLOTS]
        turned[pl.ds(64 * (s % 2), SLOTS, stride=2), :] = ahead_h[SLOTS:]
        turned[pl.ds(64 * (s % 2) + 1, SLOTS, stride=2), :] = inflow[SLOTS:]
        if s % 2:
            columns[s // 2] = turned[...].T
    edges[8] = kept(2)[:SLOTS]
    edges[9] = kept(3)[:SLOTS]
    turned[pl.ds(0, SLOTS), :] = kept(2)[SLOTS:]
    turned[pl.ds(SLOTS, SLOTS), :] = kept(3)[SLOTS:]
    columns[2] = turned[...].T

    part_rows = 32
    parts = TILE // part_rows
    lane = iota((part_rows, TILE), 1)
    row = iota((part_rows, TILE), 0)
    at_first = lane == 0
    at_last = lane == TILE - 1
    bottom = row == part_rows - 1

    def one_tile(t, carry):
        buf = t % BUFFERS

        @pl.when(t + BUFFERS - 1 < live)
        def _():
            fetch(t + BUFFERS - 1)

        arrived(buf)

        @pl.when(t >= BUFFERS)
        def _():
            sent(buf)

        box = inbox.at[buf]
        out = outbox.at[buf]
        wall_x = nb_s[t, 1] < 0
        wall_y = nb_s[t, 3] < 0

        def edge_row(j):
            return edges[j, pl.ds(t, 1), :]

        z_next = edge_row(8)
        n_next = edge_row(9)
        for p in range(parts):
            rows = pl.ds(p * part_rows, part_rows)
            zr = pl.ds(3 * TILE + p * part_rows, part_rows)
            nr = pl.ds(4 * TILE + p * part_rows, part_rows)
            z = box[zr, :]
            n = box[nr, :]
            if p < parts - 1:
                z_dn = box[pl.ds(3 * TILE + p * part_rows + 1, part_rows), :]
                n_dn = box[pl.ds(4 * TILE + p * part_rows + 1, part_rows), :]
            else:
                z_dn = jnp.where(bottom, z_next, pltpu.roll(z, part_rows - 1, 0))
                n_dn = jnp.where(bottom, n_next, pltpu.roll(n, part_rows - 1, 0))
            side = columns[2, rows, :]
            z_rt = jnp.where(at_last, pltpu.roll(side, TILE - 1 - t, 1), pltpu.roll(z, TILE - 1, 1))
            n_rt = jnp.where(at_last, pltpu.roll(side, TILE - 1 - SLOTS - t, 1), pltpu.roll(n, TILE - 1, 1))
            slope_x[rows, :] = z_dn - z
            slope_y[rows, :] = z_rt - z
            rub_x[rows, :] = RUB * (n + n_dn)
            rub_y[rows, :] = RUB * (n + n_rt)
            water[pl.ds(p * part_rows, part_rows), :] = box[rows, :]
        for s in range(4):
            water[pl.ds(TILE, 1), :] = edge_row(4 + s)
            stream_x[pl.ds(7, 1), :] = edge_row(s)
            for p in range(parts):
                rows = pl.ds(p * part_rows, part_rows)
                h = water[rows, :]
                h_dn = water[pl.ds(p * part_rows + 1, part_rows), :]
                side = pltpu.roll(columns[s // 2, rows, :], TILE - 1 - 64 * (s % 2) - 2 * t, 1)
                h_rt = jnp.where(at_last, side, pltpu.roll(h, TILE - 1, 1))
                if s == 0:
                    flow_x = box[pl.ds(TILE + p * part_rows, part_rows), :]
                    flow_y = box[pl.ds(2 * TILE + p * part_rows, part_rows), :]
                else:
                    flow_x = stream_x[pl.ds(8 + p * part_rows, part_rows), :]
                    flow_y = stream_y[rows, :]
                new_x = flux(flow_x, h, h_dn, slope_x[rows, :], rub_x[rows, :])
                if p == parts - 1:
                    new_x = jnp.where(bottom & wall_x, 0.0, new_x)
                new_y = flux(flow_y, h, h_rt, slope_y[rows, :], rub_y[rows, :])
                new_y = jnp.where(at_last & wall_y, 0.0, new_y)
                if s < 3:
                    stream_y[rows, :] = new_y
                else:
                    out[pl.ds(TILE + p * part_rows, part_rows), :] = new_x
                    out[pl.ds(2 * TILE + p * part_rows, part_rows), :] = new_y
                in_y = jnp.where(at_first, side, pltpu.roll(new_y, 1, 1))
                stream_x[pl.ds(8 + p * part_rows, part_rows), :] = new_x
                in_x = stream_x[pl.ds(7 + p * part_rows, part_rows), :]
                h_new = h + GAIN * ((in_x - new_x) + (in_y - new_y))
                if s < 3:
                    water[rows, :] = h_new
                else:
                    out[rows, :] = h_new
        send(t, buf)
        return carry

    lax.fori_loop(0, live, one_tile, 0)
    for b in range(BUFFERS):

        @pl.when(b < live)
        def _():
            sent(b)

    def blanked(t, carry):
        pltpu.make_async_copy(zeros, zeros, zero_sem).wait()
        return carry

    lax.fori_loop(live, SLOTS, blanked, 0)


SMEM = pl.BlockSpec(memory_space=pltpu.SMEM)
VMEM = pl.BlockSpec(memory_space=pltpu.VMEM)
ANY = pl.BlockSpec(memory_space=pl.ANY)


def shifted(block, axis, distance):
    devices = range(lax.axis_size(axis))
    route_pairs = [(i - distance, i) for i in devices if i - distance in devices]
    return lax.ppermute(block, axis, route_pairs)


def exchange(x_up, x_down, y_up, y_down):
    got_y = shifted(y_up, "gy", 1), shifted(y_down, "gy", -1)
    got_x = shifted(x_up, "gx", 1), shifted(x_down, "gx", -1)
    return got_x[0], got_x[1], got_y[0], got_y[1]


def struct(*shape):
    return jax.ShapeDtypeStruct(shape, f32)


def shards(depth, discharge, bed, friction, tile_ids, neighbors, moves):
    base = (lax.axis_index(("gx", "gy")) * SLOTS).astype(i32).reshape(1)
    plan = moves[0]
    tiles = (
        depth.reshape(SLOTS * TILE, TILE),
        discharge.reshape(SLOTS * 2 * TILE, TILE),
        bed.reshape(SLOTS * TILE, TILE),
        friction.reshape(SLOTS * TILE, TILE),
    )
    one = pl.BlockSpec((GROUP * TILE, TILE), lambda g: (g, 0))
    two = pl.BlockSpec((GROUP * 2 * TILE, TILE), lambda g: (g, 0))

    def whole(*shape):
        return pl.BlockSpec(shape, lambda g: (0,) * len(shape))

    frames, up, down = pl.pallas_call(
        extract_kernel,
        grid=(SLOTS // GROUP,),
        in_specs=[SMEM, SMEM, one, two, one, one],
        out_specs=[whole(2 * SLOTS, 5 * FIELD), whole(MOVERS, 10 * FIELD), whole(MOVERS, 10 * FIELD)],
        out_shape=[struct(2 * SLOTS, 5 * FIELD), struct(MOVERS, 10 * FIELD), struct(MOVERS, 10 * FIELD)],
        scratch_shapes=[
            pltpu.VMEM((5, TILE, TILE), f32),
            pltpu.VMEM((5, TILE, TILE), f32),
            pltpu.VMEM((TILE, TILE), f32),
        ],
        name="extract",
    )(plan, base, *tiles)
    from_low = shifted(up, "gy", 1)
    from_high = shifted(down, "gy", -1)

    def chunk_scratch(rows):
        return [
            pltpu.VMEM((rows, TILE), f32),
            pltpu.VMEM((rows, TILE), f32),
            pltpu.VMEM((2 * CHUNK_ROWS, TILE), f32),
            pltpu.SemaphoreType.DMA,
            pltpu.SemaphoreType.DMA((4,)),
        ]

    first_rows = 4 * MOVERS
    dyn, fixed, *sends = pl.pallas_call(
        settle_kernel,
        in_specs=[SMEM, SMEM, VMEM, VMEM, VMEM, VMEM, ANY, ANY, ANY, ANY],
        out_specs=[VMEM, VMEM, VMEM, VMEM, ANY, ANY],
        out_shape=[
            struct(2 * SLOTS, 3 * FIELD),
            struct(2 * SLOTS, 2 * FIELD),
            struct(first_rows, TILE),
            struct(first_rows, TILE),
            struct(CHUNK_ROWS + first_rows, TILE),
            struct(CHUNK_ROWS + first_rows, TILE),
        ],
        scratch_shapes=chunk_scratch(first_rows),
        name="settle",
    )(plan, base, neighbors, frames, from_low, from_high, *tiles)
    got = exchange(*sends)
    lows = [got[2]]
    highs = [got[3]]
    still = []
    trails = []

    def edge_specs(rows):
        at = CHUNK_ROWS // rows
        return [VMEM, VMEM] + [pl.BlockSpec((rows, TILE), lambda i: (at, 0))] * 2

    def flat(spec, shape):
        return spec

    rows = first_rows
    for turn in range(3):

        def body(*refs, turn=turn):
            step_kernel(turn, *refs)

        at = CHUNK_ROWS // rows
        full = [pl.BlockSpec(a.shape, lambda i: (0, 0)) for a in (neighbors, dyn, fixed, *still)]
        sides = [pl.BlockSpec(got[0].shape, lambda i: (0, 0)), pl.BlockSpec(got[1].shape, lambda i: (0, 0))]
        ends = [pl.BlockSpec((rows, TILE), lambda i, at=at: (at, 0))] * 2
        shapes = [
            (2 * SLOTS, 3 * FIELD),
            (2 * SLOTS, 5 * TILE),
            (2 * SLOTS, 2 * TILE),
            (MOVERS, TILE),
            (MOVERS, TILE),
        ]
        dyn, kept, trail, *sends = pl.pallas_call(
            body,
            grid=(1,),
            in_specs=[SMEM, SMEM, *full, *sides, *ends, ANY, ANY, ANY, ANY],
            out_specs=[pl.BlockSpec(s, lambda i: (0, 0)) for s in shapes] + [ANY, ANY],
            out_shape=[struct(*s) for s in shapes] + [struct(CHUNK_ROWS + MOVERS, TILE)] * 2,
            scratch_shapes=chunk_scratch(MOVERS),
            name="edge_step",
        )(plan, base, neighbors, dyn, fixed, *still, *got, *tiles)
        still = [kept]
        trails.append(trail)
        got = exchange(*sends)
        lows.append(got[2])
        highs.append(got[3])
        rows = MOVERS

    at = CHUNK_ROWS // rows
    full = [pl.BlockSpec(a.shape, lambda i: (0, 0)) for a in (neighbors, dyn, fixed, *still)]
    sides = [pl.BlockSpec(got[0].shape, lambda i: (0, 0)), pl.BlockSpec(got[1].shape, lambda i: (0, 0))]
    ends = [pl.BlockSpec((rows, TILE), lambda i: (at, 0))] * 2
    trail_specs = [pl.BlockSpec(t.shape, lambda i: (0, 0)) for t in trails]
    new_depth, new_flow = pl.pallas_call(
        tile_kernel,
        grid=(1,),
        in_specs=[SMEM, SMEM, SMEM, SMEM, *full, *sides, *ends, *trail_specs, *([ANY] * 12)],
        out_specs=[ANY, ANY],
        out_shape=[struct(SLOTS * TILE, TILE), struct(SLOTS * 2 * TILE, TILE)],
        scratch_shapes=[
            pltpu.VMEM((BUFFERS, 5 * TILE, TILE), f32),
            pltpu.VMEM((BUFFERS, 3 * TILE, TILE), f32),
            pltpu.VMEM((3 * TILE, TILE), f32),
            pltpu.VMEM((10, SLOTS, TILE), f32),
            pltpu.VMEM((3, TILE, TILE), f32),
            pltpu.VMEM((TILE, TILE), f32),
            pltpu.VMEM((TILE + 8, TILE), f32),
            pltpu.VMEM((TILE + 8, TILE), f32),
            pltpu.VMEM((TILE, TILE), f32),
            pltpu.VMEM((TILE, TILE), f32),
            pltpu.VMEM((TILE, TILE), f32),
            pltpu.VMEM((TILE, TILE), f32),
            pltpu.VMEM((TILE, TILE), f32),
            pltpu.SMEM((SLOTS,), i32),
            pltpu.SemaphoreType.DMA((BUFFERS,)),
            pltpu.SemaphoreType.DMA((BUFFERS,)),
            pltpu.SemaphoreType.DMA,
        ],
        name="tiles",
    )(plan, base, tile_ids, neighbors, neighbors, dyn, fixed, *still, *got, *trails, *tiles, *lows, *highs)
    return (
        new_depth.reshape(SLOTS, TILE, TILE),
        new_flow.reshape(SLOTS, 2, TILE, TILE),
    )


def solution(mesh):
    return jax.shard_map(
        shards,
        mesh=mesh,
        in_specs=(
            P(("gx", "gy"), None, None),
            P(("gx", "gy"), None, None, None),
            P(("gx", "gy"), None, None),
            P(("gx", "gy"), None, None),
            P(("gx", "gy")),
            P(("gx", "gy"), None),
            P(("gx", "gy"), None, None, None),
        ),
        out_specs=(P(("gx", "gy"), None, None), P(("gx", "gy"), None, None, None)),
        check_vma=False,
    )
```

time: 357 us -> 163 us (0.46)
  local copies, waits for them, and re-layouts: 139 us -> 6.17 us
  other arithmetic: 106 us -> 0 us
  Pallas kernels: 0 us -> 56.3 us
  waiting for transfers between devices: 53.1 us -> 46.8 us
    select_n x39 -> x0, other arithmetic: 60.9 us -> none  [the longest x3 22.9 us: shards(): jnp.where(inside_y | exists[:, 3][:, None, None], face_flux(qy, h, h_rt,...]
    slice x41 -> x0, local copies, waits for them, and re-layouts: 60.3 us -> none  [the longest x12 23.7 us: shards(): h_rt = jnp.where(inside_y, jnp.roll(h, -1, 2), right[:, 0, :][:, :, None])]
    pallas_call x0 -> x6, Pallas kernels: none -> 56.3 us  [the longest x1 27.4 us: shards(): pl.pallas_call(tile_kernel, grid=(1,), in_specs=[SMEM, SMEM, SMEM, SMEM,...]
    gather x56 -> x0, local copies, waits for them, and re-layouts: 48.3 us -> none  [the longest x16 9.45 us: place_rows(): near_rows = jnp.take(rows, jnp.clip(link - base, 0, slots - 1), axis=0)]
    another operation x15 -> x0, other arithmetic: 19.8 us -> none  [the longest x3 19.1 us: shards(): jnp.stack([jnp.where(live, qx, 0.0), jnp.where(live, qy, 0.0)], 1)]
    add x3 -> x0, other arithmetic: 16.6 us -> none  [shards(): h = h + step_time / spacing * (in_x - qx_new + (in_y - qy_new))]
    scatter x4 -> x0, local copies, waits for them, and re-layouts: 12.3 us -> none  [settle(): return kept.at[landing].set(fresh, mode='drop')]
    unnamed x50 -> x39, local copies, waits for them, and re-layouts: 14.5 us -> 4.82 us
  transfers between devices with their start and end apart: 18 -> 18, of which waited for: 6 -> 14; matrix products, arithmetic and copies ran while one was open for 32% -> 0% of each run, Pallas kernels for 0% -> 0%
where the time goes in v1:
time: 163 us; the launch traced here: 162 us
  Pallas kernels  56.3 us (35%)
  starting transfers between devices  51.4 us (32%)
  waiting for transfers between devices  46.8 us (29%)
  local copies, waits for them, and re-layouts  6.17 us (4%)
    ppermute x18, starting transfers between devices, shifted(): return lax.ppermute(block, axis, route_pairs)  51.4 us
    ppermute x18, waiting for transfers between devices, shifted(): return lax.ppermute(block, axis, route_pairs)  46.8 us
    pallas_call x1, Pallas kernels, shards(): pl.pallas_call(tile_kernel, grid=(1,), in_specs=[SMEM, SMEM, SMEM, SMEM,...  27.4 us
    pallas_call x3, Pallas kernels, shards(): pl.pallas_call(body, grid=(1,), in_specs=[SMEM, SMEM, *full, *sides, *end...  14.7 us
    pallas_call x1, Pallas kernels, shards(): pl.pallas_call(extract_kernel, grid=(SLOTS // GROUP,), in_specs=[SMEM, SM...  9.03 us
    pallas_call x1, Pallas kernels, shards(): pl.pallas_call(settle_kernel, in_specs=[SMEM, SMEM, VMEM, VMEM, VMEM, VME...  5.2 us
    unnamed x39, local copies, waits for them, and re-layouts  4.82 us
  transfers between devices with their start and end apart: 18, of which 14 were waited for; matrix products, arithmetic and copies ran while one was open for 0% of the time, Pallas kernels for 0%

profile of v1, /device:TPU:56, one launch (start us, length us, event | category | flops | bytes accessed | tf_op | source)
XLA Modules:
  0.0 161.6 jit_solution(11399250295073981864)
XLA Ops:
  2.0 9.0 %extract.1 = (f32[64,5120]{1,0:T(8,128)}, f32[8,10240]{1,0:T(8,128)}, f32[8,10240]{1,0:T(8,128)}) custom-call(s32[2,8,2]{2,1,0:T(8,128)} %copy.18.moves.refs_0_, s32[1]{0:T(128)} %bitcast.1.base.refs_1_, f32[4096,128]{1,0:T(8,128)} %bitcast.14, f32[8192,128]{1,0:T(8,128)} %bitcast.8, f32[4096,128]{1,0:T(8,128)} %bitcast.20, f32[4096,128]{1,0:T(8,128)} %bitcast.26), custom_call_target="tpu_custom_call" | custom-call | tf_op jit(solution)/shard_map/extract/pallas_call | solution.py:585
  11.0 3.0 %collective-permute-start = (f32[8,10240]{1,0:T(8,128)}, f32[8,10240]{1,0:T(8,128)S(1)}, u32[]{:S(2)}, u32[]{:S(2)}) collective-permute-start(f32[8,10240]{1,0:T(8,128)} %get-tuple-element.35), channel_id=1, source_target_pairs={{0,1},{1,2},{2,3},{3,4},{4,5},{5,6},{6,7},{7,8},{8,9},{9,10},{10,1... | collective-permute-start | bytes 983048 | tf_op jit(solution)/shard_map/ppermute | solution.py:557
  17.6 5.0 %collective-permute-done.from_low = f32[8,10240]{1,0:T(8,128)S(1)} collective-permute-done((f32[8,10240]{1,0:T(8,128)}, f32[8,10240]{1,0:T(8,128)S(1)}, u32[]{:S(2)}, u32[]{:S(2)}) %collective-permute-start) | collective-permute-done | bytes 327712 | tf_op jit(solution)/shard_map/ppermute | solution.py:557
  22.6 4.9 %collective-permute-done.1.from_high = f32[8,10240]{1,0:T(8,128)S(1)} collective-permute-done((f32[8,10240]{1,0:T(8,128)}, f32[8,10240]{1,0:T(8,128)S(1)}, u32[]{:S(2)}, u32[]{:S(2)}) %collective-permute-start.1) | collective-permute-done | bytes 327712 | tf_op jit(solution)/shard_map/ppermute | solution.py:557
  28.2 5.2 %settle.1 = (f32[64,3072]{1,0:T(8,128)}, f32[64,2048]{1,0:T(8,128)}, f32[32,128]{1,0:T(8,128)}, f32[32,128]{1,0:T(8,128)}, f32[1312,128]{1,0:T(8,128)}, /*index=5*/f32[1312,128]{1,0:T(8,128)}) custom-call(s32[2,8,2]{2,1,0:T(8,128)} %copy.18.moves.refs_0_, s32[1]{0:T(128)} %bitcast.1.base.refs_1_, s32[32,4]{1,0:T(8,128)} %copy.19.nb.refs_2_.nb_s, ...), custom_call_target="tpu_custom_call" | custom-call | tf_op jit(solution)/shard_map/settle/pallas_call | solution.py:611
  35.3 3.9 %collective-permute-start.5 = (f32[1312,128]{1,0:T(8,128)}, f32[1312,128]{1,0:T(8,128)S(1)}, u32[]{:S(2)}, u32[]{:S(2)}) collective-permute-start(f32[1312,128]{1,0:T(8,128)} %get-tuple-element.42), channel_id=1, source_target_pairs={{1,0},{2,1},{3,2},{4,3},{5,4},{6,5},{7,6},{8,7},{9,8},{10,9},{11,1... | collective-permute-start | bytes 2015240 | tf_op jit(solution)/shard_map/ppermute | solution.py:557
  41.2 3.6 %collective-permute-start.3 = (f32[32,128]{1,0:T(8,128)}, f32[32,128]{1,0:T(8,128)S(1)}, u32[]{:S(2)}, u32[]{:S(2)}) collective-permute-start(f32[32,128]{1,0:T(8,128)} %get-tuple-element.40), channel_id=1, source_target_pairs={{16,0},{32,16},{48,32},{64,48},{80,64},{96,80},{112,96},{17,1},{33... | collective-permute-start | bytes 49160 | tf_op jit(solution)/shard_map/ppermute | solution.py:557
  46.4 4.7 %collective-permute-done.4.refs_7_.l0 = f32[1312,128]{1,0:T(8,128)S(1)} collective-permute-done((f32[1312,128]{1,0:T(8,128)}, f32[1312,128]{1,0:T(8,128)S(1)}, u32[]{:S(2)}, u32[]{:S(2)}) %collective-permute-start.4) | collective-permute-done | bytes 671776 | tf_op jit(solution)/shard_map/ppermute | solution.py:557
  51.1 4.0 %collective-permute-done.5.refs_8_.u0 = f32[1312,128]{1,0:T(8,128)S(1)} collective-permute-done((f32[1312,128]{1,0:T(8,128)}, f32[1312,128]{1,0:T(8,128)S(1)}, u32[]{:S(2)}, u32[]{:S(2)}) %collective-permute-start.5) | collective-permute-done | bytes 671776 | tf_op jit(solution)/shard_map/ppermute | solution.py:557
  56.0 5.0 %edge_step.3 = (f32[64,3072]{1,0:T(8,128)}, f32[64,640]{1,0:T(8,128)}, f32[64,256]{1,0:T(8,128)}, f32[8,128]{1,0:T(8,128)}, f32[8,128]{1,0:T(8,128)}, /*index=5*/f32[1288,128]{1,0:T(8,128)}, f32[1288,128]{1,0:T(8,128)}) custom-call(s32[2,8,2]{2,1,0:T(8,128)} %copy.18.moves.refs_0_, s32[1]{0:T(128)} %bitcast.1.base.refs_1_, s32[32,4]{1,0:T(8,128)} %copy.19.nb.refs_2_.nb_s, ...), custom_call_target="tpu_custom_call" | custom-call | tf_op jit(solution)/shard_map/edge_step/pallas_call | solution.py:656
  63.0 3.9 %collective-permute-start.9 = (f32[1288,128]{1,0:T(8,128)}, f32[1288,128]{1,0:T(8,128)S(1)}, u32[]{:S(2)}, u32[]{:S(2)}) collective-permute-start(f32[1288,128]{1,0:T(8,128)} %get-tuple-element.48), channel_id=1, source_target_pairs={{1,0},{2,1},{3,2},{4,3},{5,4},{6,5},{7,6},{8,7},{9,8},{10,9},{11,1... | collective-permute-start | bytes 1978376 | tf_op jit(solution)/shard_map/ppermute | solution.py:557
  68.8 3.6 %collective-permute-start.7 = (f32[8,128]{1,0:T(8,128)}, f32[8,128]{1,0:T(8,128)S(1)}, u32[]{:S(2)}, u32[]{:S(2)}) collective-permute-start(f32[8,128]{1,0:T(8,128)} %get-tuple-element.46), channel_id=1, source_target_pairs={{16,0},{32,16},{48,32},{64,48},{80,64},{96,80},{112,96},{17,1},{33... | collective-permute-start | bytes 12296 | tf_op jit(solution)/shard_map/ppermute | solution.py:557
  74.0 3.7 %collective-permute-done.8.refs_8_.l1 = f32[1288,128]{1,0:T(8,128)S(1)} collective-permute-done((f32[1288,128]{1,0:T(8,128)}, f32[1288,128]{1,0:T(8,128)S(1)}, u32[]{:S(2)}, u32[]{:S(2)}) %collective-permute-start.8) | collective-permute-done | bytes 659488 | tf_op jit(solution)/shard_map/ppermute | solution.py:557
  77.7 4.0 %collective-permute-done.9.refs_9_.u1 = f32[1288,128]{1,0:T(8,128)S(1)} collective-permute-done((f32[1288,128]{1,0:T(8,128)}, f32[1288,128]{1,0:T(8,128)S(1)}, u32[]{:S(2)}, u32[]{:S(2)}) %collective-permute-start.9) | collective-permute-done | bytes 659488 | tf_op jit(solution)/shard_map/ppermute | solution.py:557
  82.6 4.8 %edge_step.4 = (f32[64,3072]{1,0:T(8,128)}, f32[64,640]{1,0:T(8,128)}, f32[64,256]{1,0:T(8,128)}, f32[8,128]{1,0:T(8,128)}, f32[8,128]{1,0:T(8,128)}, /*index=5*/f32[1288,128]{1,0:T(8,128)}, f32[1288,128]{1,0:T(8,128)}) custom-call(s32[2,8,2]{2,1,0:T(8,128)} %copy.18.moves.refs_0_, s32[1]{0:T(128)} %bitcast.1.base.refs_1_, s32[32,4]{1,0:T(8,128)} %copy.19.nb.refs_2_.nb_s, ...), custom_call_target="tpu_custom_call" | custom-call | tf_op jit(solution)/shard_map/edge_step/pallas_call | solution.py:656
  89.4 3.9 %collective-permute-start.13 = (f32[1288,128]{1,0:T(8,128)}, f32[1288,128]{1,0:T(8,128)S(1)}, u32[]{:S(2)}, u32[]{:S(2)}) collective-permute-start(f32[1288,128]{1,0:T(8,128)} %get-tuple-element.54), channel_id=1, source_target_pairs={{1,0},{2,1},{3,2},{4,3},{5,4},{6,5},{7,6},{8,7},{9,8},{10,9},{11,1... | collective-permute-start | bytes 1978376 | tf_op jit(solution)/shard_map/ppermute | solution.py:557
  95.2 3.6 %collective-permute-start.11 = (f32[8,128]{1,0:T(8,128)}, f32[8,128]{1,0:T(8,128)S(1)}, u32[]{:S(2)}, u32[]{:S(2)}) collective-permute-start(f32[8,128]{1,0:T(8,128)} %get-tuple-element.52), channel_id=1, source_target_pairs={{16,0},{32,16},{48,32},{64,48},{80,64},{96,80},{112,96},{17,1},{33... | collective-permute-start | bytes 12296 | tf_op jit(solution)/shard_map/ppermute | solution.py:557
  100.4 2.8 %collective-permute-done.12.refs_8_.l2 = f32[1288,128]{1,0:T(8,128)S(1)} collective-permute-done((f32[1288,128]{1,0:T(8,128)}, f32[1288,128]{1,0:T(8,128)S(1)}, u32[]{:S(2)}, u32[]{:S(2)}) %collective-permute-start.12) | collective-permute-done | bytes 659488 | tf_op jit(solution)/shard_map/ppermute | solution.py:557
  103.3 4.0 %collective-permute-done.13.refs_9_.u2 = f32[1288,128]{1,0:T(8,128)S(1)} collective-permute-done((f32[1288,128]{1,0:T(8,128)}, f32[1288,128]{1,0:T(8,128)S(1)}, u32[]{:S(2)}, u32[]{:S(2)}) %collective-permute-start.13) | collective-permute-done | bytes 659488 | tf_op jit(solution)/shard_map/ppermute | solution.py:557
  108.1 4.8 %edge_step.5 = (f32[64,3072]{1,0:T(8,128)}, f32[64,640]{1,0:T(8,128)}, f32[64,256]{1,0:T(8,128)}, f32[8,128]{1,0:T(8,128)}, f32[8,128]{1,0:T(8,128)}, /*index=5*/f32[1288,128]{1,0:T(8,128)}, f32[1288,128]{1,0:T(8,128)}) custom-call(s32[2,8,2]{2,1,0:T(8,128)} %copy.18.moves.refs_0_, s32[1]{0:T(128)} %bitcast.1.base.refs_1_, s32[32,4]{1,0:T(8,128)} %copy.19.nb.refs_2_.nb_s, ...), custom_call_target="tpu_custom_call" | custom-call | tf_op jit(solution)/shard_map/edge_step/pallas_call | solution.py:656
  114.9 3.9 %collective-permute-start.17 = (f32[1288,128]{1,0:T(8,128)}, f32[1288,128]{1,0:T(8,128)S(1)}, u32[]{:S(2)}, u32[]{:S(2)}) collective-permute-start(f32[1288,128]{1,0:T(8,128)} %get-tuple-element.60), channel_id=1, source_target_pairs={{1,0},{2,1},{3,2},{4,3},{5,4},{6,5},{7,6},{8,7},{9,8},{10,9},{11,1... | collective-permute-start | bytes 1978376 | tf_op jit(solution)/shard_map/ppermute | solution.py:557
  120.8 3.6 %collective-permute-start.15 = (f32[8,128]{1,0:T(8,128)}, f32[8,128]{1,0:T(8,128)S(1)}, u32[]{:S(2)}, u32[]{:S(2)}) collective-permute-start(f32[8,128]{1,0:T(8,128)} %get-tuple-element.58), channel_id=1, source_target_pairs={{16,0},{32,16},{48,32},{64,48},{80,64},{96,80},{112,96},{17,1},{33... | collective-permute-start | bytes 12296 | tf_op jit(solution)/shard_map/ppermute | solution.py:557
  127.9 5.4 %collective-permute-done.17.yh.u3 = f32[1288,128]{1,0:T(8,128)S(1)} collective-permute-done((f32[1288,128]{1,0:T(8,128)}, f32[1288,128]{1,0:T(8,128)S(1)}, u32[]{:S(2)}, u32[]{:S(2)}) %collective-permute-start.17) | collective-permute-done | bytes 659488 | tf_op jit(solution)/shard_map/ppermute | solution.py:557
  134.2 27.4 %tiles.1 = (f32[4096,128]{1,0:T(8,128)}, f32[8192,128]{1,0:T(8,128)}) custom-call(s32[2,8,2]{2,1,0:T(8,128)} %copy.18.moves.refs_0_, s32[1]{0:T(128)} %bitcast.1.base.refs_1_, s32[32]{0:T(128)} %ids.1, s32[32,4]{1,0:T(8,128)} %copy.19.nb.refs_2_.nb_s, s32[32,4]{1,0:T(8,128)} %copy.19.nb.refs_2_.nb_s, f32[64,3072]{1,0:T(8,128)} %get-tuple-element.55.dyn, ...), custom_call_target="tpu_custom_call" | custom-call | tf_op jit(solution)/shard_map/tiles/pallas_call | solution.py:677
  (58 shorter events, 32.4 us)
Async XLA Ops:
  2.0 14.9 %copy-start.18 = (s32[32,4]{0,1:T(4,128)S(1)}, s32[32,4]{0,1:T(4,128)}, u32[]{:S(2)}) copy-start(s32[32,4]{0,1:T(4,128)} %param.12) | copy-start | bytes 1540
  11.0 11.5 %collective-permute-start = (f32[8,10240]{1,0:T(8,128)}, f32[8,10240]{1,0:T(8,128)S(1)}, u32[]{:S(2)}, u32[]{:S(2)}) collective-permute-start(f32[8,10240]{1,0:T(8,128)} %get-tuple-element.35), channel_id=1, source_target_pairs={{0,1},{1,2},{2,3},{3,4},{4,5},{5,6},{6,7},{7,8},{8,9},{9,10},{10,1... | collective-permute-start | bytes 983048 | tf_op jit(solution)/shard_map/ppermute | solution.py:557
  14.1 13.4 %collective-permute-start.1 = (f32[8,10240]{1,0:T(8,128)}, f32[8,10240]{1,0:T(8,128)S(1)}, u32[]{:S(2)}, u32[]{:S(2)}) collective-permute-start(f32[8,10240]{1,0:T(8,128)} %get-tuple-element.36), channel_id=1, source_target_pairs={{1,0},{2,1},{3,2},{4,3},{5,4},{6,5},{7,6},{8,7},{9,8},{10,9},{11,1... | collective-permute-start | bytes 983048 | tf_op jit(solution)/shard_map/ppermute | solution.py:557
  33.4 17.8 %collective-permute-start.4 = (f32[1312,128]{1,0:T(8,128)}, f32[1312,128]{1,0:T(8,128)S(1)}, u32[]{:S(2)}, u32[]{:S(2)}) collective-permute-start(f32[1312,128]{1,0:T(8,128)} %get-tuple-element.41), channel_id=1, source_target_pairs={{0,1},{1,2},{2,3},{3,4},{4,5},{5,6},{6,7},{7,8},{8,9},{9,10},{10,1... | collective-permute-start | bytes 2015240 | tf_op jit(solution)/shard_map/ppermute | solution.py:557
  35.3 19.9 %collective-permute-start.5 = (f32[1312,128]{1,0:T(8,128)}, f32[1312,128]{1,0:T(8,128)S(1)}, u32[]{:S(2)}, u32[]{:S(2)}) collective-permute-start(f32[1312,128]{1,0:T(8,128)} %get-tuple-element.42), channel_id=1, source_target_pairs={{1,0},{2,1},{3,2},{4,3},{5,4},{6,5},{7,6},{8,7},{9,8},{10,9},{11,1... | collective-permute-start | bytes 2015240 | tf_op jit(solution)/shard_map/ppermute | solution.py:557
  39.2 5.6 %collective-permute-start.2 = (f32[32,128]{1,0:T(8,128)}, f32[32,128]{1,0:T(8,128)S(1)}, u32[]{:S(2)}, u32[]{:S(2)}) collective-permute-start(f32[32,128]{1,0:T(8,128)} %get-tuple-element.39), channel_id=1, source_target_pairs={{0,16},{16,32},{32,48},{48,64},{64,80},{80,96},{96,112},{1,17},{17... | collective-permute-start | bytes 49160 | tf_op jit(solution)/shard_map/ppermute | solution.py:557
  41.2 5.3 %collective-permute-start.3 = (f32[32,128]{1,0:T(8,128)}, f32[32,128]{1,0:T(8,128)S(1)}, u32[]{:S(2)}, u32[]{:S(2)}) collective-permute-start(f32[32,128]{1,0:T(8,128)} %get-tuple-element.40), channel_id=1, source_target_pairs={{16,0},{32,16},{48,32},{64,48},{80,64},{96,80},{112,96},{17,1},{33... | collective-permute-start | bytes 49160 | tf_op jit(solution)/shard_map/ppermute | solution.py:557
  44.8 10.4 %copy-start.10 = (f32[32,128]{1,0:T(8,128)}, f32[32,128]{1,0:T(8,128)S(1)}, u32[]{:S(2)}) copy-start(f32[32,128]{1,0:T(8,128)S(1)} %collective-permute-done.2.refs_5_) | copy-start | bytes 49156
  46.4 8.8 %copy-start.11 = (f32[32,128]{1,0:T(8,128)}, f32[32,128]{1,0:T(8,128)S(1)}, u32[]{:S(2)}) copy-start(f32[32,128]{1,0:T(8,128)S(1)} %collective-permute-done.3.refs_6_) | copy-start | bytes 49156
  61.1 16.7 %collective-permute-start.8 = (f32[1288,128]{1,0:T(8,128)}, f32[1288,128]{1,0:T(8,128)S(1)}, u32[]{:S(2)}, u32[]{:S(2)}) collective-permute-start(f32[1288,128]{1,0:T(8,128)} %get-tuple-element.47), channel_id=1, source_target_pairs={{0,1},{1,2},{2,3},{3,4},{4,5},{5,6},{6,7},{7,8},{8,9},{9,10},{10,1... | collective-permute-start | bytes 1978376 | tf_op jit(solution)/shard_map/ppermute | solution.py:557
  63.0 18.8 %collective-permute-start.9 = (f32[1288,128]{1,0:T(8,128)}, f32[1288,128]{1,0:T(8,128)S(1)}, u32[]{:S(2)}, u32[]{:S(2)}) collective-permute-start(f32[1288,128]{1,0:T(8,128)} %get-tuple-element.48), channel_id=1, source_target_pairs={{1,0},{2,1},{3,2},{4,3},{5,4},{6,5},{7,6},{8,7},{9,8},{10,9},{11,1... | collective-permute-start | bytes 1978376 | tf_op jit(solution)/shard_map/ppermute | solution.py:557
  66.9 5.6 %collective-permute-start.6 = (f32[8,128]{1,0:T(8,128)}, f32[8,128]{1,0:T(8,128)S(1)}, u32[]{:S(2)}, u32[]{:S(2)}) collective-permute-start(f32[8,128]{1,0:T(8,128)} %get-tuple-element.45), channel_id=1, source_target_pairs={{0,16},{16,32},{32,48},{48,64},{64,80},{80,96},{96,112},{1,17},{17... | collective-permute-start | bytes 12296 | tf_op jit(solution)/shard_map/ppermute | solution.py:557
  68.8 5.2 %collective-permute-start.7 = (f32[8,128]{1,0:T(8,128)}, f32[8,128]{1,0:T(8,128)S(1)}, u32[]{:S(2)}, u32[]{:S(2)}) collective-permute-start(f32[8,128]{1,0:T(8,128)} %get-tuple-element.46), channel_id=1, source_target_pairs={{16,0},{32,16},{48,32},{64,48},{80,64},{96,80},{112,96},{17,1},{33... | collective-permute-start | bytes 12296 | tf_op jit(solution)/shard_map/ppermute | solution.py:557
  72.5 9.3 %copy-start.12 = (f32[8,128]{1,0:T(8,128)}, f32[8,128]{1,0:T(8,128)S(1)}, u32[]{:S(2)}) copy-start(f32[8,128]{1,0:T(8,128)S(1)} %collective-permute-done.6.refs_6_) | copy-start | bytes 12292
  87.5 15.8 %collective-permute-start.12 = (f32[1288,128]{1,0:T(8,128)}, f32[1288,128]{1,0:T(8,128)S(1)}, u32[]{:S(2)}, u32[]{:S(2)}) collective-permute-start(f32[1288,128]{1,0:T(8,128)} %get-tuple-element.53), channel_id=1, source_target_pairs={{0,1},{1,2},{2,3},{3,4},{4,5},{5,6},{6,7},{7,8},{8,9},{9,10},{10,1... | collective-permute-start | bytes 1978376 | tf_op jit(solution)/shard_map/ppermute | solution.py:557
  89.4 17.9 %collective-permute-start.13 = (f32[1288,128]{1,0:T(8,128)}, f32[1288,128]{1,0:T(8,128)S(1)}, u32[]{:S(2)}, u32[]{:S(2)}) collective-permute-start(f32[1288,128]{1,0:T(8,128)} %get-tuple-element.54), channel_id=1, source_target_pairs={{1,0},{2,1},{3,2},{4,3},{5,4},{6,5},{7,6},{8,7},{9,8},{10,9},{11,1... | collective-permute-start | bytes 1978376 | tf_op jit(solution)/shard_map/ppermute | solution.py:557
  93.3 5.6 %collective-permute-start.10 = (f32[8,128]{1,0:T(8,128)}, f32[8,128]{1,0:T(8,128)S(1)}, u32[]{:S(2)}, u32[]{:S(2)}) collective-permute-start(f32[8,128]{1,0:T(8,128)} %get-tuple-element.51), channel_id=1, source_target_pairs={{0,16},{16,32},{32,48},{48,64},{64,80},{80,96},{96,112},{1,17},{17... | collective-permute-start | bytes 12296 | tf_op jit(solution)/shard_map/ppermute | solution.py:557
  95.2 5.2 %collective-permute-start.11 = (f32[8,128]{1,0:T(8,128)}, f32[8,128]{1,0:T(8,128)S(1)}, u32[]{:S(2)}, u32[]{:S(2)}) collective-permute-start(f32[8,128]{1,0:T(8,128)} %get-tuple-element.52), channel_id=1, source_target_pairs={{16,0},{32,16},{48,32},{64,48},{80,64},{96,80},{112,96},{17,1},{33... | collective-permute-start | bytes 12296 | tf_op jit(solution)/shard_map/ppermute | solution.py:557
  98.9 8.4 %copy-start.13 = (f32[8,128]{1,0:T(8,128)}, f32[8,128]{1,0:T(8,128)S(1)}, u32[]{:S(2)}) copy-start(f32[8,128]{1,0:T(8,128)S(1)} %collective-permute-done.10.refs_6_) | copy-start | bytes 12292
  113.0 14.9 %collective-permute-start.16 = (f32[1288,128]{1,0:T(8,128)}, f32[1288,128]{1,0:T(8,128)S(1)}, u32[]{:S(2)}, u32[]{:S(2)}) collective-permute-start(f32[1288,128]{1,0:T(8,128)} %get-tuple-element.59), channel_id=1, source_target_pairs={{0,1},{1,2},{2,3},{3,4},{4,5},{5,6},{6,7},{7,8},{8,9},{9,10},{10,1... | collective-permute-start | bytes 1978376 | tf_op jit(solution)/shard_map/ppermute | solution.py:557
  114.9 18.4 %collective-permute-start.17 = (f32[1288,128]{1,0:T(8,128)}, f32[1288,128]{1,0:T(8,128)S(1)}, u32[]{:S(2)}, u32[]{:S(2)}) collective-permute-start(f32[1288,128]{1,0:T(8,128)} %get-tuple-element.60), channel_id=1, source_target_pairs={{1,0},{2,1},{3,2},{4,3},{5,4},{6,5},{7,6},{8,7},{9,8},{10,9},{11,1... | collective-permute-start | bytes 1978376 | tf_op jit(solution)/shard_map/ppermute | solution.py:557
  118.9 5.6 %collective-permute-start.14 = (f32[8,128]{1,0:T(8,128)}, f32[8,128]{1,0:T(8,128)S(1)}, u32[]{:S(2)}, u32[]{:S(2)}) collective-permute-start(f32[8,128]{1,0:T(8,128)} %get-tuple-element.57), channel_id=1, source_target_pairs={{0,16},{16,32},{32,48},{48,64},{64,80},{80,96},{96,112},{1,17},{17... | collective-permute-start | bytes 12296 | tf_op jit(solution)/shard_map/ppermute | solution.py:557
  120.8 5.2 %collective-permute-start.15 = (f32[8,128]{1,0:T(8,128)}, f32[8,128]{1,0:T(8,128)S(1)}, u32[]{:S(2)}, u32[]{:S(2)}) collective-permute-start(f32[8,128]{1,0:T(8,128)} %get-tuple-element.58), channel_id=1, source_target_pairs={{16,0},{32,16},{48,32},{64,48},{80,64},{96,80},{112,96},{17,1},{33... | collective-permute-start | bytes 12296 | tf_op jit(solution)/shard_map/ppermute | solution.py:557
  124.4 8.9 %copy-start.16 = (f32[8,128]{1,0:T(8,128)}, f32[8,128]{1,0:T(8,128)S(1)}, u32[]{:S(2)}) copy-start(f32[8,128]{1,0:T(8,128)S(1)} %collective-permute-done.14.xl) | copy-start | bytes 12292
  (13 other events, 48.6 us)

commit v2 on v1

v2 whole, which is shorter than its diff:
```python
import jax
import jax.numpy as jnp
from jax import lax
from jax.experimental import pallas as pl
from jax.experimental.pallas import tpu as pltpu
from jax.sharding import PartitionSpec as P


TILE = 128
SLOTS = 32
MOVERS = 8
DEPTH = 4
STRIPS = 2 * DEPTH
FIELD = STRIPS * TILE
STATE = 5 * TILE
EARLY = (0, 1)
RIDERS = (2, 3, 4, 5)
LATE = (6, 7)
GROUP = 8
GY = 16
BUFFERS = 4

gravity = 9.81
step_time = 0.25
spacing = 2.0
min_depth = 0.15
PULL = gravity * step_time / spacing
RUB = gravity * step_time * 0.5
GAIN = step_time / spacing

f32 = jnp.float32
bf16 = jnp.bfloat16
i32 = jnp.int32


def flux(flow, h_lo, h_hi, slope, rub):
    depth_face = jnp.maximum(0.5 * (h_lo + h_hi), min_depth)
    drive = flow - (PULL * depth_face) * ((h_hi - h_lo) + slope)
    loss = jnp.exp2(jnp.log2(depth_face) * (-7.0 / 3.0))
    return drive / (1.0 + (rub * jnp.abs(flow)) * loss)


def iota(shape, dim):
    return lax.broadcasted_iota(i32, shape, dim)


def route(onehot, rows):
    a = rows.astype(bf16)
    rest = rows - a.astype(f32)
    b = rest.astype(bf16)
    c = (rest - b.astype(f32)).astype(bf16)
    take = onehot.astype(bf16)

    def part(x):
        return jnp.dot(take, x, preferred_element_type=f32)

    return part(a) + part(b) + part(c)


def side_links(nb_ref, base, side):
    square = (SLOTS, SLOTS)
    rows = iota(square, 0)
    cols = iota(square, 1)
    link_row = jnp.broadcast_to(nb_ref[side : side + 1, :].astype(f32), square)
    diagonal = rows == cols

    def column(x):
        return jnp.broadcast_to(jnp.sum(jnp.where(diagonal, x, 0.0), 1, keepdims=True), square)

    first = base.astype(f32)

    def remote(link):
        return jnp.where((link >= 0.0) & ((link < first) | (link >= first + SLOTS)), 1.0, 0.0)

    link_b = column(link_row)
    missing = link_b[:, :1] < 0.0
    far_b = remote(link_b)
    far = far_b[:, :1]
    far_row = remote(link_row)
    near = jnp.where(link_b - first == cols.astype(f32), 1.0, 0.0)
    rank = jnp.sum(jnp.where(link_row < link_b, far_row, 0.0), 1, keepdims=True)
    order_row = jnp.sum(jnp.where(rows < cols, far_b, 0.0), 0, keepdims=True)
    far_row = far_row[:1]
    place = jnp.where(
        (jnp.broadcast_to(rank, (SLOTS, MOVERS)) == iota((SLOTS, MOVERS), 1).astype(f32))
        & (jnp.broadcast_to(far, (SLOTS, MOVERS)) > 0.0),
        1.0,
        0.0,
    )
    pick = jnp.where(
        (jnp.broadcast_to(order_row, (MOVERS, SLOTS)) == iota((MOVERS, SLOTS), 0).astype(f32))
        & (jnp.broadcast_to(far_row, (MOVERS, SLOTS)) > 0.0),
        1.0,
        0.0,
    )
    exists = jnp.where(missing, 0.0, 1.0)
    return near, place, pick, exists


def halo_of(links, rows, message):
    near, place, _, _ = links
    return route(near, rows) + route(place, message)


def extract_kernel(
    moves, base, depth, discharge, bed, friction, frames, up_out, down_out, early_up, early_down,
    depth_v, flow_v, bed_v, rough_v, lo_acc, hi_acc, turned, load_sem, sem,
):
    lane = iota((TILE, TILE), 1)
    groups = SLOTS // GROUP
    loads = []
    for g in range(groups):
        one = pl.ds(g * GROUP * TILE, GROUP * TILE)
        two = pl.ds(g * GROUP * 2 * TILE, GROUP * 2 * TILE)
        pairs = ((depth, depth_v, one), (discharge, flow_v, two), (bed, bed_v, one), (friction, rough_v, one))
        copies = [pltpu.make_async_copy(a.at[r], b.at[r], load_sem.at[g, i]) for i, (a, b, r) in enumerate(pairs)]
        for c in copies:
            c.start()
        loads.append(copies)
    start_chunk(EARLY, moves, base, (depth, discharge, bed, friction), early_up, early_down, sem)

    def strip(f, k):
        return pl.ds((f * STRIPS + k) * TILE, TILE)

    sources = ((depth_v, 0, 1), (flow_v, 0, 2), (flow_v, 1, 2), (bed_v, 0, 1), (rough_v, 0, 1))
    for g in range(groups):
        for c in loads[g]:
            c.wait()
        home = pl.ds(g * GROUP, GROUP)
        for f, (ref, part, parts) in enumerate(sources):
            top = (g * GROUP * parts + part) * TILE
            for k in range(STRIPS):
                row = k if k < DEPTH else TILE - STRIPS + k
                frames[home, strip(f, k)] = ref[pl.ds(top + row, GROUP, stride=parts * TILE), :]
            high = hi_acc[f] if g else None
            low = lo_acc[f] if g else None
            for t in range(GROUP):
                tile = ref[pl.ds(top + t * parts * TILE, TILE), :]
                at = g * GROUP * DEPTH + DEPTH * t
                turn = pltpu.roll(tile, (at + DEPTH) % TILE, 1)
                high = turn if high is None else jnp.where(lane >= at, turn, high)
                if low is None:
                    low = turn
                elif at + DEPTH < TILE:
                    low = jnp.where(lane >= at + DEPTH, turn, low)
                else:
                    low = jnp.where(lane < DEPTH, turn, low)
            hi_acc[f] = high
            lo_acc[f] = low

    for f in range(5):
        to = (0, 2, 1, 3, 4)[f]
        for half in range(2):
            block = hi_acc[f] if half else pltpu.roll(lo_acc[f], TILE - DEPTH, 1)
            turned[...] = block.T
            for k in range(DEPTH):
                frames[pl.ds(SLOTS, SLOTS), strip(to, half * DEPTH + k)] = turned[pl.ds(k, SLOTS, stride=DEPTH), :]
    shape = (2 * MOVERS, SLOTS)
    pick = jnp.zeros(shape, f32)
    for m in range(MOVERS):
        for way in range(2):
            leaver = moves[way, 0, m] - base[0]
            spot = (iota(shape, 0) == (1 - way) * MOVERS + m) & (iota(shape, 1) == leaver)
            pick = jnp.where(spot, 1.0, pick)
    for axis in range(2):
        for c in range(5):
            got = route(pick, frames[pl.ds(axis * SLOTS, SLOTS), pl.ds(c * FIELD, FIELD)])
            to = pl.ds((axis * 5 + c) * FIELD, FIELD)
            up_out[:, to] = got[:MOVERS]
            down_out[:, to] = got[MOVERS:]
    finish_chunk(EARLY, early_up, early_down, sem)


def start_chunk(entries, moves, base, tiles, up_out, down_out, sem):
    depth, discharge, bed, friction = tiles
    for way, out in ((1, up_out), (0, down_out)):
        for i, m in enumerate(entries):
            slot = jnp.clip(moves[way, 0, m] - base[0], 0, SLOTS - 1)
            at = i * STATE
            one = pl.ds(pl.multiple_of(slot * TILE, TILE), TILE)
            two = pl.ds(pl.multiple_of(slot * (2 * TILE), TILE), 2 * TILE)
            pltpu.make_async_copy(depth.at[one], out.at[pl.ds(at, TILE)], sem.at[way]).start()
            pltpu.make_async_copy(discharge.at[two], out.at[pl.ds(at + TILE, 2 * TILE)], sem.at[way]).start()
            pltpu.make_async_copy(bed.at[one], out.at[pl.ds(at + 3 * TILE, TILE)], sem.at[way]).start()
            pltpu.make_async_copy(friction.at[one], out.at[pl.ds(at + 4 * TILE, TILE)], sem.at[way]).start()


def finish_chunk(entries, up_out, down_out, sem):
    body = pl.ds(0, len(entries) * STATE)
    for way, out in ((1, up_out), (0, down_out)):
        pltpu.make_async_copy(out.at[body], out.at[body], sem.at[way]).wait()


def is_odd(base):
    return ((base[0] // (SLOTS * GY)) % 2) == 1


def swap(odd, a, b):
    return jnp.where(odd, b, a), jnp.where(odd, a, b)


def settle_kernel(
    moves, base, nb, frames, from_low, from_high, depth, discharge, bed, friction,
    dyn, fixed, x_0, x_1, y_up, y_down, sem,
):
    ride = RIDERS[:1]
    start_chunk(ride, moves, base, (depth, discharge, bed, friction), y_up, y_down, sem)
    shape = (SLOTS, 2 * MOVERS)
    land = jnp.zeros(shape, f32)
    left = jnp.zeros((SLOTS, TILE), f32)
    for m in range(MOVERS):
        for way in range(2):
            lander = moves[way, 1, m] - base[0]
            leaver = moves[way, 0, m] - base[0]
            spot = (iota(shape, 0) == lander) & (iota(shape, 1) == way * MOVERS + m)
            land = jnp.where(spot, 1.0, land)
            row = iota((SLOTS, TILE), 0)
            left = jnp.where((row == leaver) | (row == lander), 1.0, left)
    for axis in range(2):
        home = pl.ds(axis * SLOTS, SLOTS)
        for f in range(5):
            part = pl.ds(f * FIELD, FIELD)
            came = pl.ds((axis * 5 + f) * FIELD, FIELD)
            fresh = route(land, jnp.concatenate([from_low[:, came], from_high[:, came]], 0))
            for k in range(STRIPS):
                sub = pl.ds(f * FIELD + k * TILE, TILE)
                value = jnp.where(left > 0.0, 0.0, frames[home, sub]) + fresh[:, k * TILE : (k + 1) * TILE]
                if f < 3:
                    dyn[home, sub] = value
                else:
                    fixed[home, pl.ds((f - 3) * FIELD + k * TILE, TILE)] = value

    def edge(ref, axis, f, k):
        return ref[pl.ds(axis * SLOTS, SLOTS), pl.ds(f * FIELD + k * TILE, TILE)]

    last = STRIPS - 1
    blank = jnp.zeros((MOVERS, TILE), f32)
    for axis in range(2):
        lower = side_links(nb, base[0], 2 * axis)
        higher = side_links(nb, base[0], 2 * axis + 1)
        ups = (edge(dyn, axis, 0, last), edge(fixed, axis, 0, last), edge(fixed, axis, 1, last), edge(dyn, axis, 1, last))
        downs = (edge(dyn, axis, 0, 0), edge(fixed, axis, 0, 0), edge(fixed, axis, 1, 0))
        for f in range(4):
            up = route(higher[2], ups[f])
            down = route(lower[2], downs[f]) if f < 3 else blank
            if axis == 0:
                up, down = swap(is_odd(base), up, down)
                x_0[pl.ds(f * MOVERS, MOVERS), :] = up
                x_1[pl.ds(f * MOVERS, MOVERS), :] = down
            else:
                y_up[pl.ds(STATE + f * MOVERS, MOVERS), :] = up
                y_down[pl.ds(STATE + f * MOVERS, MOVERS), :] = down
    finish_chunk(ride, y_up, y_down, sem)


def other_axis(x):
    return jnp.concatenate([x[SLOTS:], x[:SLOTS]], 0)


def gather_halos(nb, base_ref, dyn, fixed, messages, first):
    last = STRIPS - 1
    out = {}
    parts = {name: [] for name in ("h_lo", "h_hi", "z_lo", "n_lo", "q_lo", "z_hi", "n_hi", "lo", "hi")}
    picks = []
    for axis in range(2):
        home = pl.ds(axis * SLOTS, SLOTS)
        lower = side_links(nb, base_ref[0], 2 * axis)
        higher = side_links(nb, base_ref[0], 2 * axis + 1)
        picks.append((lower[2], higher[2]))

        def message(f):
            if axis == 0:
                rows = pl.ds(f * MOVERS, MOVERS)
                from_higher, from_lower = swap(is_odd(base_ref), messages[0][0][rows, :], messages[0][1][rows, :])
                return from_lower, from_higher
            rows = pl.ds(STATE + f * MOVERS, MOVERS)
            return messages[1][0][rows, :], messages[1][1][rows, :]

        def strip(ref, f, k):
            return ref[home, pl.ds(f * FIELD + k * TILE, TILE)]

        def low(f, rows):
            return halo_of(lower, rows, message(f)[0])

        def high(f, rows):
            return halo_of(higher, rows, message(f)[1])

        parts["h_lo"].append(low(0, strip(dyn, 0, last)))
        parts["h_hi"].append(high(0, strip(dyn, 0, 0)))
        if first:
            parts["z_lo"].append(low(1, strip(fixed, 0, last)))
            parts["n_lo"].append(low(2, strip(fixed, 1, last)))
            parts["q_lo"].append(low(3, strip(dyn, 1, last)))
            parts["z_hi"].append(high(1, strip(fixed, 0, 0)))
            parts["n_hi"].append(high(2, strip(fixed, 1, 0)))
        parts["lo"].append(jnp.broadcast_to(lower[3], (SLOTS, TILE)))
        parts["hi"].append(jnp.broadcast_to(higher[3], (SLOTS, TILE)))
    for name, pieces in parts.items():
        if pieces:
            out[name] = jnp.concatenate(pieces, 0)
    return out, picks


def step_kernel(turn, moves, base, nb, dyn, fixed, *rest):
    first = turn == 0
    if first:
        still = None
        (xl, xh, yl, yh), rest = rest[:4], rest[4:]
    else:
        still = rest[0]
        (xl, xh, yl, yh), rest = rest[1:5], rest[5:]
    depth, discharge, bed, friction = rest[:4]
    tiles = (depth, discharge, bed, friction)
    final = turn == 2
    if final:
        (dyn_out, still_out, trail, x_0, x_1, y_up, y_down, late_up, late_down, sem) = rest[4:]
    else:
        (dyn_out, still_out, trail, x_0, x_1, y_up, y_down, sem) = rest[4:]
    ride = RIDERS[turn + 1 : turn + 2]
    start_chunk(ride, moves, base, tiles, y_up, y_down, sem.at[0])
    if final:
        start_chunk(LATE, moves, base, tiles, late_up, late_down, sem.at[1])
    halo, picks = gather_halos(nb, base, dyn, fixed, ((xl, xh), (yl, yh)), first)
    names = ("z_lo", "n_lo", "z_hi", "n_hi", "q_lo")
    if not first:
        for j, name in enumerate(names):
            halo[name] = still[:, pl.ds(j * TILE, TILE)]

    def get(ref, f, k):
        return ref[:, pl.ds(f * FIELD + k * TILE, TILE)]

    last = STRIPS - 1
    h = [get(dyn, 0, k) for k in range(STRIPS)]
    z = [get(fixed, 0, k) for k in range(STRIPS)]
    n = [get(fixed, 1, k) for k in range(STRIPS)]
    low_face = flux(halo["q_lo"], halo["h_lo"], h[0], z[0] - halo["z_lo"], RUB * (halo["n_lo"] + n[0]))
    low_face = jnp.where(halo["lo"] > 0.0, low_face, 0.0)
    high_face = flux(get(dyn, 1, last), h[last], halo["h_hi"], halo["z_hi"] - z[last], RUB * (n[last] + halo["n_hi"]))
    high_face = jnp.where(halo["hi"] > 0.0, high_face, 0.0)
    for j, name in enumerate(names[:4]):
        still_out[:, pl.ds(j * TILE, TILE)] = halo[name]
    still_out[:, pl.ds(4 * TILE, TILE)] = low_face
    trail[:, pl.ds(0, TILE)] = low_face
    trail[:, pl.ds(TILE, TILE)] = halo["h_hi"]

    lane = iota((2 * SLOTS, TILE), 1)
    side_h = other_axis(halo["h_hi"])
    side_z = other_axis(halo["z_hi"])
    side_n = other_axis(halo["n_hi"])
    side_wall = other_axis(halo["hi"]) <= 0.0
    side_in = other_axis(low_face)

    def cell(x, k):
        at = k if k < DEPTH else TILE - STRIPS + k
        return jnp.broadcast_to(x[:, at : at + 1], x.shape)

    def ahead(x, k, side):
        return jnp.where(lane == TILE - 1, cell(side, k), pltpu.roll(x, TILE - 1, 1))

    reach = DEPTH - 1 - turn
    low_keep = list(range(reach))
    high_keep = list(range(STRIPS - reach, STRIPS))
    face = {-1: low_face, last: high_face}
    for k in low_keep + [x - 1 for x in high_keep]:
        face[k] = flux(get(dyn, 1, k), h[k], h[k + 1], z[k + 1] - z[k], RUB * (n[k] + n[k + 1]))
    new = {}
    for k in low_keep + high_keep:
        side = flux(
            get(dyn, 2, k), h[k], ahead(h[k], k, side_h), ahead(z[k], k, side_z) - z[k],
            RUB * (n[k] + ahead(n[k], k, side_n)),
        )
        side = jnp.where((lane == TILE - 1) & side_wall, 0.0, side)
        before = jnp.where(lane == 0, cell(side_in, k), pltpu.roll(side, 1, 1))
        new[k] = h[k] + GAIN * ((face[k - 1] - face[k]) + (before - side))
        dyn_out[:, pl.ds(2 * FIELD + k * TILE, TILE)] = side
    blank = jnp.zeros((2 * SLOTS, TILE), f32)
    for k in range(STRIPS):
        dyn_out[:, pl.ds(k * TILE, TILE)] = new[k] if k in new else blank
        dyn_out[:, pl.ds(FIELD + k * TILE, TILE)] = face[k] if k in face else blank
        if k not in new:
            dyn_out[:, pl.ds(2 * FIELD + k * TILE, TILE)] = blank
    for axis in range(2):
        home = slice(axis * SLOTS, (axis + 1) * SLOTS)
        up = route(picks[axis][1], new[last][home])
        down = route(picks[axis][0], new[0][home])
        if axis == 0:
            x_0[...], x_1[...] = swap(is_odd(base), up, down)
        else:
            y_up[pl.ds(STATE, MOVERS), :] = up
            y_down[pl.ds(STATE, MOVERS), :] = down
    finish_chunk(ride, y_up, y_down, sem.at[0])
    if final:
        finish_chunk(LATE, late_up, late_down, sem.at[1])


def run_tiles(
    queue, origin, count, moves_sources, tiles, nb_s, edges, columns, outs, before_loop,
    inbox, outbox, water, stream_x, stream_y, slope_x, slope_y, rub_x, rub_y, in_sem, out_sem,
):
    depth, discharge, bed, friction = tiles
    depth_out, flow_out = outs

    def fetch(j):
        t = queue[j]
        buf = j % BUFFERS
        sem = in_sem.at[buf]
        box = inbox.at[buf]
        kind = origin[t]

        if depth is not None:

            @pl.when(kind == 0)
            def _():
                one = pl.ds(pl.multiple_of(t * TILE, TILE), TILE)
                two = pl.ds(pl.multiple_of(t * (2 * TILE), TILE), 2 * TILE)
                pltpu.make_async_copy(depth.at[one], box.at[pl.ds(0, TILE)], sem).start()
                pltpu.make_async_copy(discharge.at[two], box.at[pl.ds(TILE, 2 * TILE)], sem).start()
                pltpu.make_async_copy(bed.at[one], box.at[pl.ds(3 * TILE, TILE)], sem).start()
                pltpu.make_async_copy(friction.at[one], box.at[pl.ds(4 * TILE, TILE)], sem).start()

        for code, ref, at in moves_sources:

            @pl.when(kind == code)
            def _():
                pltpu.make_async_copy(ref.at[pl.ds(at, STATE)], box, sem).start()

    def arrived(buf):
        box = inbox.at[buf]
        pltpu.make_async_copy(box, box, in_sem.at[buf]).wait()

    def send(t, buf):
        box = outbox.at[buf]
        one = pl.ds(pl.multiple_of(t * TILE, TILE), TILE)
        two = pl.ds(pl.multiple_of(t * (2 * TILE), TILE), 2 * TILE)
        pltpu.make_async_copy(box.at[pl.ds(0, TILE)], depth_out.at[one], out_sem.at[buf]).start()
        pltpu.make_async_copy(box.at[pl.ds(TILE, 2 * TILE)], flow_out.at[two], out_sem.at[buf]).start()

    def sent(buf):
        box = outbox.at[buf]
        pltpu.make_async_copy(box, box, out_sem.at[buf]).wait()

    def prime():
        for j in range(BUFFERS - 1):

            @pl.when(j < count)
            def _():
                fetch(j)

    prime()
    before_loop()
    part_rows = 32
    parts = TILE // part_rows
    lane = iota((part_rows, TILE), 1)
    row = iota((part_rows, TILE), 0)
    at_first = lane == 0
    at_last = lane == TILE - 1
    bottom = row == part_rows - 1

    def one_tile(j, carry):
        t = queue[j]
        buf = j % BUFFERS

        @pl.when(j + BUFFERS - 1 < count)
        def _():
            fetch(j + BUFFERS - 1)

        arrived(buf)

        @pl.when(j >= BUFFERS)
        def _():
            sent(buf)

        box = inbox.at[buf]
        out = outbox.at[buf]
        wall_x = nb_s[1, t] < 0
        wall_y = nb_s[3, t] < 0

        def edge_row(j):
            return edges[j, pl.ds(t, 1), :]

        z_next = edge_row(8)
        n_next = edge_row(9)
        for p in range(parts):
            rows = pl.ds(p * part_rows, part_rows)
            zr = pl.ds(3 * TILE + p * part_rows, part_rows)
            nr = pl.ds(4 * TILE + p * part_rows, part_rows)
            z = box[zr, :]
            n = box[nr, :]
            if p < parts - 1:
                z_dn = box[pl.ds(3 * TILE + p * part_rows + 1, part_rows), :]
                n_dn = box[pl.ds(4 * TILE + p * part_rows + 1, part_rows), :]
            else:
                z_dn = jnp.where(bottom, z_next, pltpu.roll(z, part_rows - 1, 0))
                n_dn = jnp.where(bottom, n_next, pltpu.roll(n, part_rows - 1, 0))
            side = columns[2, rows, :]
            z_rt = jnp.where(at_last, pltpu.roll(side, TILE - 1 - t, 1), pltpu.roll(z, TILE - 1, 1))
            n_rt = jnp.where(at_last, pltpu.roll(side, TILE - 1 - SLOTS - t, 1), pltpu.roll(n, TILE - 1, 1))
            slope_x[rows, :] = z_dn - z
            slope_y[rows, :] = z_rt - z
            rub_x[rows, :] = RUB * (n + n_dn)
            rub_y[rows, :] = RUB * (n + n_rt)
            water[pl.ds(p * part_rows, part_rows), :] = box[rows, :]
        for s in range(4):
            water[pl.ds(TILE, 1), :] = edge_row(4 + s)
            stream_x[pl.ds(7, 1), :] = edge_row(s)
            for p in range(parts):
                rows = pl.ds(p * part_rows, part_rows)
                h = water[rows, :]
                h_dn = water[pl.ds(p * part_rows + 1, part_rows), :]
                side = pltpu.roll(columns[s // 2, rows, :], TILE - 1 - 64 * (s % 2) - 2 * t, 1)
                h_rt = jnp.where(at_last, side, pltpu.roll(h, TILE - 1, 1))
                if s == 0:
                    flow_x = box[pl.ds(TILE + p * part_rows, part_rows), :]
                    flow_y = box[pl.ds(2 * TILE + p * part_rows, part_rows), :]
                else:
                    flow_x = stream_x[pl.ds(8 + p * part_rows, part_rows), :]
                    flow_y = stream_y[rows, :]
                new_x = flux(flow_x, h, h_dn, slope_x[rows, :], rub_x[rows, :])
                if p == parts - 1:
                    new_x = jnp.where(bottom & wall_x, 0.0, new_x)
                new_y = flux(flow_y, h, h_rt, slope_y[rows, :], rub_y[rows, :])
                new_y = jnp.where(at_last & wall_y, 0.0, new_y)
                if s < 3:
                    stream_y[rows, :] = new_y
                else:
                    out[pl.ds(TILE + p * part_rows, part_rows), :] = new_x
                    out[pl.ds(2 * TILE + p * part_rows, part_rows), :] = new_y
                in_y = jnp.where(at_first, side, pltpu.roll(new_y, 1, 1))
                stream_x[pl.ds(8 + p * part_rows, part_rows), :] = new_x
                in_x = stream_x[pl.ds(7 + p * part_rows, part_rows), :]
                h_new = h + GAIN * ((in_x - new_x) + (in_y - new_y))
                if s < 3:
                    water[rows, :] = h_new
                else:
                    out[rows, :] = h_new
        send(t, buf)
        return carry

    lax.fori_loop(0, count, one_tile, 0)
    for b in range(BUFFERS):

        @pl.when(b < count)
        def _():
            sent(b)


def chunk_sources(entries, low, high):
    found = []
    for way, ref in ((0, low), (1, high)):
        for i, m in enumerate(entries):
            found.append((1 + way * MOVERS + m, ref, i * STATE))
    return found


def note_arrivals(entries, moves, base, visit):
    for m in entries:
        for way in range(2):
            lander = moves[way, 1, m]

            @pl.when(lander >= 0)
            def _():
                visit(lander - base[0], 1 + way * MOVERS + m)


def tile_kernel(
    moves, base, ids, nb_s, nb, dyn, fixed, still, x_0, x_1, l3, u3, t0, t1, t2,
    l0, l1, l2, u0, u1, u2, early_low, early_high, depth, discharge, bed, friction,
    depth_out, flow_out, edges, columns,
    zeros, turned, queue, origin, zero_sem, *scratch,
):
    def clear(t, total):
        origin[t] = 0
        return total + jnp.where(ids[t] >= 0, 1, 0)

    live = lax.fori_loop(0, SLOTS, clear, 0)

    def mark(t, code):
        origin[t] = code

    note_arrivals(EARLY + RIDERS, moves, base, mark)
    note_arrivals(LATE, moves, base, lambda t, code: mark(t, -1))

    def enqueue(t, size):
        keep = origin[t] >= 0
        queue[size] = t
        return size + jnp.where(keep, 1, 0)

    count = lax.fori_loop(0, live, enqueue, 0)
    zeros[...] = jnp.zeros(zeros.shape, f32)

    def blank(t, carry):
        one = pl.ds(pl.multiple_of(t * TILE, TILE), TILE)
        two = pl.ds(pl.multiple_of(t * (2 * TILE), TILE), 2 * TILE)
        pltpu.make_async_copy(zeros.at[pl.ds(0, TILE)], depth_out.at[one], zero_sem).start()
        pltpu.make_async_copy(zeros.at[pl.ds(TILE, 2 * TILE)], flow_out.at[two], zero_sem).start()
        return carry

    def before_loop():
        lax.fori_loop(live, SLOTS, blank, 0)
        halo, _ = gather_halos(nb, base, dyn, fixed, ((x_0, x_1), (l3, u3)), False)

        def kept(j):
            return still[:, pl.ds(j * TILE, TILE)]

        n_first = fixed[:, pl.ds(FIELD, TILE)]
        z_first = fixed[:, pl.ds(0, TILE)]
        low_face = flux(
            kept(4), halo["h_lo"], dyn[:, pl.ds(0, TILE)], z_first - kept(0), RUB * (kept(1) + n_first)
        )
        low_face = jnp.where(halo["lo"] > 0.0, low_face, 0.0)
        trails = [(t[:, pl.ds(0, TILE)], t[:, pl.ds(TILE, TILE)]) for t in (t0, t1, t2)]
        trails.append((low_face, halo["h_hi"]))
        for s, (inflow, ahead_h) in enumerate(trails):
            edges[s] = inflow[:SLOTS]
            edges[4 + s] = ahead_h[:SLOTS]
            turned[pl.ds(64 * (s % 2), SLOTS, stride=2), :] = ahead_h[SLOTS:]
            turned[pl.ds(64 * (s % 2) + 1, SLOTS, stride=2), :] = inflow[SLOTS:]
            if s % 2:
                columns[s // 2] = turned[...].T
        edges[8] = kept(2)[:SLOTS]
        edges[9] = kept(3)[:SLOTS]
        turned[pl.ds(0, SLOTS), :] = kept(2)[SLOTS:]
        turned[pl.ds(SLOTS, SLOTS), :] = kept(3)[SLOTS:]
        columns[2] = turned[...].T

    sources = chunk_sources(EARLY, early_low, early_high)
    for m, low, high in zip(RIDERS, (l0, l1, l2, l3), (u0, u1, u2, u3)):
        sources += chunk_sources((m,), low, high)
    run_tiles(
        queue, origin, count, sources, (depth, discharge, bed, friction), nb_s, edges, columns,
        (depth_out, flow_out), before_loop, *scratch,
    )

    def blanked(t, carry):
        pltpu.make_async_copy(zeros, zeros, zero_sem).wait()
        return carry

    lax.fori_loop(live, SLOTS, blanked, 0)


def late_kernel(
    moves, base, nb_s, edges, columns, late_low, late_high, depth_in, flow_in,
    depth_out, flow_out, queue, origin, size, *scratch,
):
    size[0] = 0

    def enqueue(t, code):
        queue[size[0]] = t
        origin[t] = code
        size[0] = size[0] + 1

    note_arrivals(LATE, moves, base, enqueue)
    run_tiles(
        queue, origin, size[0], chunk_sources(LATE, late_low, late_high), (None,) * 4, nb_s, edges, columns,
        (depth_out, flow_out), lambda: None, *scratch,
    )


SMEM = pl.BlockSpec(memory_space=pltpu.SMEM)
VMEM = pl.BlockSpec(memory_space=pltpu.VMEM)
HBM = pl.BlockSpec(memory_space=pltpu.HBM)


def ride_up(block, axis, distance):
    devices = range(lax.axis_size(axis))
    route_pairs = [(i - distance, i) for i in devices if i - distance in devices]
    return lax.ppermute(block, axis, route_pairs)


def trade(block, pairing):
    size = lax.axis_size("gx")
    pairs = []
    for i in range(size):
        other = i ^ 1 if pairing == 0 else ((i + 1) ^ 1) - 1
        if 0 <= other < size:
            pairs.append((i, other))
    return lax.ppermute(block, "gx", pairs)


def both_ways(up, down):
    low = ride_up(up, "gy", 1)
    high = ride_up(down, "gy", -1)
    return low, high


def exchange(x_0, x_1, y_up, y_down):
    got_y = both_ways(y_up, y_down)
    return trade(x_0, 0), trade(x_1, 1), got_y[0], got_y[1]


def held(*shape):
    return pltpu.VMEM(shape, f32)


def on_core(*arrays):
    return [pltpu.with_memory_space_constraint(a, pltpu.VMEM) for a in arrays]


def call(kernel, **settings):
    return pl.pallas_call(kernel, **settings)


def struct(*shape):
    return jax.ShapeDtypeStruct(shape, f32)


def loop_scratch():
    return [
        pltpu.VMEM((BUFFERS, STATE, TILE), f32),
        pltpu.VMEM((BUFFERS, 3 * TILE, TILE), f32),
        pltpu.VMEM((TILE + 8, TILE), f32),
        pltpu.VMEM((TILE + 8, TILE), f32),
        pltpu.VMEM((TILE, TILE), f32),
        pltpu.VMEM((TILE, TILE), f32),
        pltpu.VMEM((TILE, TILE), f32),
        pltpu.VMEM((TILE, TILE), f32),
        pltpu.VMEM((TILE, TILE), f32),
        pltpu.SemaphoreType.DMA((BUFFERS,)),
        pltpu.SemaphoreType.DMA((BUFFERS,)),
    ]


def shards(depth, discharge, bed, friction, tile_ids, neighbors, moves):
    base = (lax.axis_index(("gx", "gy")) * SLOTS).astype(i32).reshape(1)
    plan = moves[0].transpose(0, 2, 1)
    nb = neighbors.T
    tiles = [
        pltpu.with_memory_space_constraint(a, pltpu.HBM)
        for a in (
            depth.reshape(SLOTS * TILE, TILE),
            discharge.reshape(SLOTS * 2 * TILE, TILE),
            bed.reshape(SLOTS * TILE, TILE),
            friction.reshape(SLOTS * TILE, TILE),
        )
    ]
    early_rows = len(EARLY) * STATE
    frames, up, down, early_up, early_down = pl.pallas_call(
        extract_kernel,
        in_specs=[SMEM, SMEM] + [HBM] * 4,
        out_specs=[VMEM] * 5,
        out_shape=[
            held(2 * SLOTS, 5 * FIELD),
            held(MOVERS, 10 * FIELD),
            held(MOVERS, 10 * FIELD),
            held(early_rows, TILE),
            held(early_rows, TILE),
        ],
        scratch_shapes=[
            pltpu.VMEM((SLOTS * TILE, TILE), f32),
            pltpu.VMEM((SLOTS * 2 * TILE, TILE), f32),
            pltpu.VMEM((SLOTS * TILE, TILE), f32),
            pltpu.VMEM((SLOTS * TILE, TILE), f32),
            pltpu.VMEM((5, TILE, TILE), f32),
            pltpu.VMEM((5, TILE, TILE), f32),
            pltpu.VMEM((TILE, TILE), f32),
            pltpu.SemaphoreType.DMA((SLOTS // GROUP, 4)),
            pltpu.SemaphoreType.DMA((2,)),
        ],
        compiler_params=pltpu.CompilerParams(vmem_limit_bytes=20 * 2**20),
        name="extract",
    )(plan, base, *tiles)
    from_low, from_high = both_ways(up, down)
    early_low, early_high = both_ways(early_up, early_down)

    first_rows = 4 * MOVERS
    dyn, fixed, *sends = call(
        settle_kernel,
        in_specs=[SMEM, SMEM] + [VMEM] * 4 + [HBM] * 4,
        out_specs=[VMEM] * 6,
        out_shape=[
            held(2 * SLOTS, 3 * FIELD),
            held(2 * SLOTS, 2 * FIELD),
            held(first_rows, TILE),
            held(first_rows, TILE),
            held(STATE + first_rows, TILE),
            held(STATE + first_rows, TILE),
        ],
        scratch_shapes=[pltpu.SemaphoreType.DMA((2,))],
        compiler_params=pltpu.CompilerParams(vmem_limit_bytes=12 * 2**20),
    )(plan, base, *on_core(nb, frames, from_low, from_high), *tiles)
    got = exchange(*sends)
    lows = [got[2]]
    highs = [got[3]]
    still = []
    trails = []
    late = []
    for turn in range(3):

        def body(*refs, turn=turn):
            step_kernel(turn, *refs)

        shapes = [
            (2 * SLOTS, 3 * FIELD),
            (2 * SLOTS, 5 * TILE),
            (2 * SLOTS, 2 * TILE),
            (MOVERS, TILE),
            (MOVERS, TILE),
            (STATE + MOVERS, TILE),
            (STATE + MOVERS, TILE),
        ]
        if turn == 2:
            shapes += [(len(LATE) * STATE, TILE)] * 2
        dyn, kept, trail, *sends = call(
            body,
            in_specs=[SMEM, SMEM] + [VMEM] * (7 + len(still)) + [HBM] * 4,
            out_specs=[VMEM] * len(shapes),
            out_shape=[held(*s) for s in shapes],
            scratch_shapes=[pltpu.SemaphoreType.DMA((2, 2))],
            compiler_params=pltpu.CompilerParams(vmem_limit_bytes=12 * 2**20),
        )(plan, base, *on_core(nb, dyn, fixed, *still, *got), *tiles)
        still = [kept]
        trails.append(trail)
        late = sends[4:]
        got = exchange(*sends[:4])
        lows.append(got[2])
        highs.append(got[3])

    late_low, late_high = both_ways(*late)
    kept_inputs = on_core(
        nb, dyn, fixed, *still, *got, *trails, *lows[:3], *highs[:3], early_low, early_high
    )
    new_depth, new_flow, edges, columns = call(
        tile_kernel,
        in_specs=[SMEM] * 4 + [VMEM] * len(kept_inputs) + [HBM] * 4,
        out_specs=[HBM, HBM, VMEM, VMEM],
        out_shape=[
            struct(SLOTS * TILE, TILE),
            struct(SLOTS * 2 * TILE, TILE),
            held(10, SLOTS, TILE),
            held(3, TILE, TILE),
        ],
        scratch_shapes=[
            pltpu.VMEM((3 * TILE, TILE), f32),
            pltpu.VMEM((TILE, TILE), f32),
            pltpu.SMEM((SLOTS,), i32),
            pltpu.SMEM((SLOTS,), i32),
            pltpu.SemaphoreType.DMA,
            *loop_scratch(),
        ],
        compiler_params=pltpu.CompilerParams(vmem_limit_bytes=12 * 2**20),
    )(plan, base, tile_ids, nb, *kept_inputs, *tiles)
    new_depth, new_flow = pl.pallas_call(
        late_kernel,
        in_specs=[SMEM] * 3 + [VMEM] * 4 + [HBM] * 2,
        out_specs=[HBM, HBM],
        out_shape=[struct(SLOTS * TILE, TILE), struct(SLOTS * 2 * TILE, TILE)],
        input_output_aliases={7: 0, 8: 1},
        scratch_shapes=[
            pltpu.SMEM((SLOTS,), i32),
            pltpu.SMEM((SLOTS,), i32),
            pltpu.SMEM((1,), i32),
            *loop_scratch(),
        ],
        compiler_params=pltpu.CompilerParams(vmem_limit_bytes=12 * 2**20),
        name="late_tiles",
    )(plan, base, nb, *on_core(edges, columns, late_low, late_high), new_depth, new_flow)
    return (
        new_depth.reshape(SLOTS, TILE, TILE),
        new_flow.reshape(SLOTS, 2, TILE, TILE),
    )


def solution(mesh):
    return jax.shard_map(
        shards,
        mesh=mesh,
        in_specs=(
            P(("gx", "gy"), None, None),
            P(("gx", "gy"), None, None, None),
            P(("gx", "gy"), None, None),
            P(("gx", "gy"), None, None),
            P(("gx", "gy")),
            P(("gx", "gy"), None),
            P(("gx", "gy"), None, None, None),
        ),
        out_specs=(P(("gx", "gy"), None, None), P(("gx", "gy"), None, None, None)),
        check_vma=False,
    )
```

time: 163 us -> 147 us (0.902)
  the two profiles are of different devices: /device:TPU:56 before, /device:TPU:60 now
where the time goes in v2:
time: 147 us; the launch traced here: 146 us
  starting transfers between devices  55.5 us (38%)
  Pallas kernels  48.9 us (33%)
  waiting for transfers between devices  40.3 us (27%)
    ppermute x14, starting transfers between devices, ride_up(): return lax.ppermute(block, axis, route_pairs)  44.9 us
    ppermute x14, waiting for transfers between devices, ride_up(): return lax.ppermute(block, axis, route_pairs)  30.1 us
    pallas_call x1, Pallas kernels, shards(): call(tile_kernel, in_specs=[SMEM] * 4 + [VMEM] * len(kept_inputs) + [HBM]...  27 us
    ppermute x8, starting transfers between devices, trade(): return lax.ppermute(block, 'gx', pairs)  10.6 us
    ppermute x8, waiting for transfers between devices, trade(): return lax.ppermute(block, 'gx', pairs)  10.2 us
    pallas_call x3, Pallas kernels, shards(): call(body, in_specs=[SMEM, SMEM] + [VMEM] * (7 + len(still)) + [HBM] * 4,...  8.19 us
    pallas_call x1, Pallas kernels, shards(): pl.pallas_call(extract_kernel, in_specs=[SMEM, SMEM] + [HBM] * 4, out_spe...  7.13 us
    pallas_call x1, Pallas kernels, shards(): pl.pallas_call(late_kernel, in_specs=[SMEM] * 3 + [VMEM] * 4 + [HBM] * 2,...  4.11 us
  transfers between devices with their start and end apart: 22, of which 12 were waited for; matrix products, arithmetic and copies ran while one was open for 0% of the time, Pallas kernels for 22%

profile of v2, /device:TPU:60, one launch (start us, length us, event | category | flops | bytes accessed | tf_op | source)
XLA Modules:
  0.0 146.4 jit_solution(1199106301607897130)
XLA Ops:
  1.3 7.1 %extract.1 = (f32[64,5120]{1,0:T(8,128)S(1)}, f32[8,10240]{1,0:T(8,128)S(1)}, f32[8,10240]{1,0:T(8,128)S(1)}, f32[1280,128]{1,0:T(8,128)S(1)}, f32[1280,128]{1,0:T(8,128)S(1)}) custom-call(s32[2,2,8]{2,1,0:T(2,128)S(1)} %bitcast.11, s32[1]{0:T(128)} %bitcast.2.base.refs_1_, f32[4096,128]{1,0:T(8,128)} %bitcast.31, f32[8192,128]{1,0:T(8,128)} %bitcast.25, ...), custom_call_target="tpu_custom_call" | custom-call | tf_op jit(solution)/shard_map/extract/pallas_call | solution.py:737
  8.5 2.7 %collective-permute-start = (f32[8,10240]{1,0:T(8,128)S(1)}, f32[8,10240]{1,0:T(8,128)S(1)}, u32[]{:S(2)}, u32[]{:S(2)}) collective-permute-start(f32[8,10240]{1,0:T(8,128)S(1)} %get-tuple-element.43), channel_id=1, source_target_pairs={{0,1},{1,2},{2,3},{3,4},{4,5},{5,6},{6,7},{7,8},{8,9},{9,10},{10,1... | collective-permute-start | bytes 983048 | tf_op jit(solution)/shard_map/ppermute | solution.py:667
  11.2 3.1 %collective-permute-start.1 = (f32[8,10240]{1,0:T(8,128)S(1)}, f32[8,10240]{1,0:T(8,128)S(1)}, u32[]{:S(2)}, u32[]{:S(2)}) collective-permute-start(f32[8,10240]{1,0:T(8,128)S(1)} %get-tuple-element.44), channel_id=1, source_target_pairs={{1,0},{2,1},{3,2},{4,3},{5,4},{6,5},{7,6},{8,7},{9,8},{10,9},{11,1... | collective-permute-start | bytes 983048 | tf_op jit(solution)/shard_map/ppermute | solution.py:667
  14.3 5.5 %collective-permute-done.from_low = f32[8,10240]{1,0:T(8,128)S(1)} collective-permute-done((f32[8,10240]{1,0:T(8,128)S(1)}, f32[8,10240]{1,0:T(8,128)S(1)}, u32[]{:S(2)}, u32[]{:S(2)}) %collective-permute-start) | collective-permute-done | bytes 327712 | tf_op jit(solution)/shard_map/ppermute | solution.py:667
  19.8 4.4 %collective-permute-done.1.from_high = f32[8,10240]{1,0:T(8,128)S(1)} collective-permute-done((f32[8,10240]{1,0:T(8,128)S(1)}, f32[8,10240]{1,0:T(8,128)S(1)}, u32[]{:S(2)}, u32[]{:S(2)}) %collective-permute-start.1) | collective-permute-done | bytes 327712 | tf_op jit(solution)/shard_map/ppermute | solution.py:667
  24.2 2.4 %shard_map.86 = (f32[64,3072]{1,0:T(8,128)S(1)}, f32[64,2048]{1,0:T(8,128)S(1)}, f32[32,128]{1,0:T(8,128)S(1)}, f32[32,128]{1,0:T(8,128)S(1)}, f32[672,128]{1,0:T(8,128)S(1)}, /*index=5*/f32[672,128]{1,0:T(8,128)S(1)}) custom-call(s32[2,2,8]{2,1,0:T(2,128)S(1)} %bitcast.12, s32[1]{0:T(128)} %bitcast.2.base.refs_1_, s32[4,32]{1,0:T(4,128)S(1)} %bitcast.18, ...), custom_call_target="tpu_custom_call" | custom-call | tf_op jit(solution)/shard_map/pallas_call | solution.py:766
  28.5 3.9 %collective-permute-start.5 = (f32[672,128]{1,0:T(8,128)S(1)}, f32[672,128]{1,0:T(8,128)S(1)}, u32[]{:S(2)}, u32[]{:S(2)}) collective-permute-start(f32[672,128]{1,0:T(8,128)S(1)} %get-tuple-element.50), channel_id=1, source_target_pairs={{1,0},{2,1},{3,2},{4,3},{5,4},{6,5},{7,6},{8,7},{9,8},{10,9},{11,1... | collective-permute-start | bytes 1032200 | tf_op jit(solution)/shard_map/ppermute | solution.py:667
  35.0 2.7 %collective-permute-done.3.refs_6_ = f32[32,128]{1,0:T(8,128)S(1)} collective-permute-done((f32[32,128]{1,0:T(8,128)S(1)}, f32[32,128]{1,0:T(8,128)S(1)}, u32[]{:S(2)}, u32[]{:S(2)}) %collective-permute-start.3) | collective-permute-done | bytes 16416 | tf_op jit(solution)/shard_map/ppermute | solution.py:677
  37.6 3.4 %collective-permute-done.5.refs_8_.u0 = f32[672,128]{1,0:T(8,128)S(1)} collective-permute-done((f32[672,128]{1,0:T(8,128)S(1)}, f32[672,128]{1,0:T(8,128)S(1)}, u32[]{:S(2)}, u32[]{:S(2)}) %collective-permute-start.5) | collective-permute-done | bytes 344096 | tf_op jit(solution)/shard_map/ppermute | solution.py:667
  41.0 2.7 %shard_map.87 = (f32[64,3072]{1,0:T(8,128)S(1)}, f32[64,640]{1,0:T(8,128)S(1)}, f32[64,256]{1,0:T(8,128)S(1)}, f32[8,128]{1,0:T(8,128)S(1)}, f32[8,128]{1,0:T(8,...) custom-call(s32[2,2,8]{2,1,0:T(2,128)S(1)} %bitcast.13, s32[1]{0:T(128)} %bitcast.2.base.refs_1_, ...), custom_call_target="tpu_custom_call" | custom-call | tf_op jit(solution)/shard_map/pallas_call | solution.py:803
  45.6 3.9 %collective-permute-start.9 = (f32[648,128]{1,0:T(8,128)S(1)}, f32[648,128]{1,0:T(8,128)S(1)}, u32[]{:S(2)}, u32[]{:S(2)}) collective-permute-start(f32[648,128]{1,0:T(8,128)S(1)} %get-tuple-element.56), channel_id=1, source_target_pairs={{1,0},{2,1},{3,2},{4,3},{5,4},{6,5},{7,6},{8,7},{9,8},{10,9},{11,1... | collective-permute-start | bytes 995336 | tf_op jit(solution)/shard_map/ppermute | solution.py:667
  49.6 3.3 %collective-permute-start.7 = (f32[8,128]{1,0:T(8,128)S(1)}, f32[8,128]{1,0:T(8,128)S(1)}, u32[]{:S(2)}, u32[]{:S(2)}) collective-permute-start(f32[8,128]{1,0:T(8,128)S(1)} %get-tuple-element.54), channel_id=1, source_target_pairs={{16,32},{32,16},{48,64},{64,48},{80,96},{96,80},{17,33},{33,17},{4... | collective-permute-start | bytes 12296 | tf_op jit(solution)/shard_map/ppermute | solution.py:677
  53.0 4.0 %collective-permute-start.18 = (f32[1280,128]{1,0:T(8,128)S(1)}, f32[1280,128]{1,0:T(8,128)S(1)}, u32[]{:S(2)}, u32[]{:S(2)}) collective-permute-start(f32[1280,128]{1,0:T(8,128)S(1)} %get-tuple-element.72), channel_id=1, source_target_pairs={{0,1},{1,2},{2,3},{3,4},{4,5},{5,6},{6,7},{7,8},{8,9},{9,10},{10,1... | collective-permute-start | bytes 1966088 | tf_op jit(solution)/shard_map/ppermute | solution.py:667
  62.6 3.9 %collective-permute-start.13 = (f32[648,128]{1,0:T(8,128)S(1)}, f32[648,128]{1,0:T(8,128)S(1)}, u32[]{:S(2)}, u32[]{:S(2)}) collective-permute-start(f32[648,128]{1,0:T(8,128)S(1)} %get-tuple-element.62), channel_id=1, source_target_pairs={{1,0},{2,1},{3,2},{4,3},{5,4},{6,5},{7,6},{8,7},{9,8},{10,9},{11,1... | collective-permute-start | bytes 995336 | tf_op jit(solution)/shard_map/ppermute | solution.py:667
  69.7 2.6 %collective-permute-start.11 = (f32[8,128]{1,0:T(8,128)S(1)}, f32[8,128]{1,0:T(8,128)S(1)}, u32[]{:S(2)}, u32[]{:S(2)}) collective-permute-start(f32[8,128]{1,0:T(8,128)S(1)} %get-tuple-element.60), channel_id=1, source_target_pairs={{16,32},{32,16},{48,64},{64,48},{80,96},{96,80},{17,33},{33,17},{4... | collective-permute-start | bytes 12296 | tf_op jit(solution)/shard_map/ppermute | solution.py:677
  74.6 4.3 %collective-permute-done.12.refs_8_.l2 = f32[648,128]{1,0:T(8,128)S(1)} collective-permute-done((f32[648,128]{1,0:T(8,128)S(1)}, f32[648,128]{1,0:T(8,128)S(1)}, u32[]{:S(2)}, u32[]{:S(2)}) %collective-permute-start.12) | collective-permute-done | bytes 331808 | tf_op jit(solution)/shard_map/ppermute | solution.py:667
  79.0 3.1 %shard_map.89 = (f32[64,3072]{1,0:T(8,128)S(1)}, f32[64,640]{1,0:T(8,128)S(1)}, f32[64,256]{1,0:T(8,128)S(1)}, f32[8,128]{1,0:T(8,128)S(1)}, f32[8,128]{1,0:T(8,...) custom-call(s32[2,2,8]{2,1,0:T(2,128)S(1)} %bitcast.15, ...), custom_call_target="tpu_custom_call" | custom-call | tf_op jit(solution)/shard_map/pallas_call | solution.py:803
  82.1 5.8 %collective-permute-start.20 = (f32[1280,128]{1,0:T(8,128)S(1)}, f32[1280,128]{1,0:T(8,128)S(1)}, u32[]{:S(2)}, u32[]{:S(2)}) collective-permute-start(f32[1280,128]{1,0:T(8,128)S(1)} %get-tuple-element.76), channel_id=1, source_target_pairs={{0,1},{1,2},{2,3},{3,4},{4,5},{5,6},{6,7},{7,8},{8,9},{9,10},{10,1... | collective-permute-start | bytes 1966088 | tf_op jit(solution)/shard_map/ppermute | solution.py:667
  89.8 6.0 %collective-permute-start.16 = (f32[648,128]{1,0:T(8,128)S(1)}, f32[648,128]{1,0:T(8,128)S(1)}, u32[]{:S(2)}, u32[]{:S(2)}) collective-permute-start(f32[648,128]{1,0:T(8,128)S(1)} %get-tuple-element.67), channel_id=1, source_target_pairs={{0,1},{1,2},{2,3},{3,4},{4,5},{5,6},{6,7},{7,8},{8,9},{9,10},{10,1... | collective-permute-start | bytes 995336 | tf_op jit(solution)/shard_map/ppermute | solution.py:667
  100.9 3.0 %collective-permute-done.15.x_1 = f32[8,128]{1,0:T(8,128)S(1)} collective-permute-done((f32[8,128]{1,0:T(8,128)S(1)}, f32[8,128]{1,0:T(8,128)S(1)}, u32[]{:S(2)}, u32[]{:S(2)}) %collective-permute-start.15) | collective-permute-done | bytes 4128 | tf_op jit(solution)/shard_map/ppermute | solution.py:677
  103.9 5.1 %collective-permute-done.16.l3 = f32[648,128]{1,0:T(8,128)S(1)} collective-permute-done((f32[648,128]{1,0:T(8,128)S(1)}, f32[648,128]{1,0:T(8,128)S(1)}, u32[]{:S(2)}, u32[]{:S(2)}) %collective-permute-start.16) | collective-permute-done | bytes 331808 | tf_op jit(solution)/shard_map/ppermute | solution.py:667
  109.0 6.2 %collective-permute-done.17.u3 = f32[648,128]{1,0:T(8,128)S(1)} collective-permute-done((f32[648,128]{1,0:T(8,128)S(1)}, f32[648,128]{1,0:T(8,128)S(1)}, u32[]{:S(2)}, u32[]{:S(2)}) %collective-permute-start.17) | collective-permute-done | bytes 331808 | tf_op jit(solution)/shard_map/ppermute | solution.py:667
  115.2 27.0 %shard_map.90 = (f32[4096,128]{1,0:T(8,128)}, f32[8192,128]{1,0:T(8,128)}, f32[10,32,128]{2,1,0:T(8,128)S(1)}, f32[3,128,128]{2,1,0:T(8,128)S(1)}) custom-call(s32[2,2,8]{2,1,0:T(2,128)S(1)} %bitcast.16, s32[1]{0:T(128)} %bitcast.2.base.refs_1_, s32[32]{0:T(128)S(1)} %copy-done.3, s32[4,32]{1,0:T(4,128)S(1)} %bitcast.22, s32[4,32]{1,0:T(4,128)S(1)} %bitcast.23, ...), custom_call_target="tpu_custom_call" | custom-call | tf_op jit(solution)/shard_map/pallas_call | solution.py:822
  142.3 4.1 %late_tiles.1 = (f32[4096,128]{1,0:T(8,128)}, f32[8192,128]{1,0:T(8,128)}) custom-call(s32[2,2,8]{2,1,0:T(2,128)S(1)} %bitcast.17, s32[1]{0:T(128)} %bitcast.2.base.refs_1_, s32[4,32]{1,0:T(4,128)S(1)} %bitcast.24, f32[10,32,128]{2,1,0:T(8,128)S(1)} %get-tuple-element.74.edges, ...), custom_call_target="tpu_custom_call", output_to_operand_aliasing={{0}: (7, {}), {1}: (8, {})} | custom-call | tf_op jit(solution)/shard_map/late_tiles/pallas_call | solution.py:842
  (35 shorter events, 25.1 us)
Async XLA Ops:
  1.3 22.9 %copy-start.2 = (s32[32,4]{0,1:T(4,128)S(1)}, s32[32,4]{0,1:T(4,128)}, u32[]{:S(2)}) copy-start(s32[32,4]{0,1:T(4,128)} %param.12) | copy-start | bytes 1540
  8.5 11.4 %collective-permute-start = (f32[8,10240]{1,0:T(8,128)S(1)}, f32[8,10240]{1,0:T(8,128)S(1)}, u32[]{:S(2)}, u32[]{:S(2)}) collective-permute-start(f32[8,10240]{1,0:T(8,128)S(1)} %get-tuple-element.43), channel_id=1, source_target_pairs={{0,1},{1,2},{2,3},{3,4},{4,5},{5,6},{6,7},{7,8},{8,9},{9,10},{10,1... | collective-permute-start | bytes 983048 | tf_op jit(solution)/shard_map/ppermute | solution.py:667
  11.2 13.0 %collective-permute-start.1 = (f32[8,10240]{1,0:T(8,128)S(1)}, f32[8,10240]{1,0:T(8,128)S(1)}, u32[]{:S(2)}, u32[]{:S(2)}) collective-permute-start(f32[8,10240]{1,0:T(8,128)S(1)} %get-tuple-element.44), channel_id=1, source_target_pairs={{1,0},{2,1},{3,2},{4,3},{5,4},{6,5},{7,6},{8,7},{9,8},{10,9},{11,1... | collective-permute-start | bytes 983048 | tf_op jit(solution)/shard_map/ppermute | solution.py:667
  26.6 11.0 %collective-permute-start.4 = (f32[672,128]{1,0:T(8,128)S(1)}, f32[672,128]{1,0:T(8,128)S(1)}, u32[]{:S(2)}, u32[]{:S(2)}) collective-permute-start(f32[672,128]{1,0:T(8,128)S(1)} %get-tuple-element.49), channel_id=1, source_target_pairs={{0,1},{1,2},{2,3},{3,4},{4,5},{5,6},{6,7},{7,8},{8,9},{9,10},{10,1... | collective-permute-start | bytes 1032200 | tf_op jit(solution)/shard_map/ppermute | solution.py:667
  28.5 12.5 %collective-permute-start.5 = (f32[672,128]{1,0:T(8,128)S(1)}, f32[672,128]{1,0:T(8,128)S(1)}, u32[]{:S(2)}, u32[]{:S(2)}) collective-permute-start(f32[672,128]{1,0:T(8,128)S(1)} %get-tuple-element.50), channel_id=1, source_target_pairs={{1,0},{2,1},{3,2},{4,3},{5,4},{6,5},{7,6},{8,7},{9,8},{10,9},{11,1... | collective-permute-start | bytes 1032200 | tf_op jit(solution)/shard_map/ppermute | solution.py:667
  32.5 2.5 %collective-permute-start.2 = (f32[32,128]{1,0:T(8,128)S(1)}, f32[32,128]{1,0:T(8,128)S(1)}, u32[]{:S(2)}, u32[]{:S(2)}) collective-permute-start(f32[32,128]{1,0:T(8,128)S(1)} %get-tuple-element.47), channel_id=1, source_target_pairs={{0,16},{16,0},{32,48},{48,32},{64,80},{80,64},{96,112},{112,96},{1... | collective-permute-start | bytes 49160 | tf_op jit(solution)/shard_map/ppermute | solution.py:677
  32.6 5.1 %collective-permute-start.3 = (f32[32,128]{1,0:T(8,128)S(1)}, f32[32,128]{1,0:T(8,128)S(1)}, u32[]{:S(2)}, u32[]{:S(2)}) collective-permute-start(f32[32,128]{1,0:T(8,128)S(1)} %get-tuple-element.48), channel_id=1, source_target_pairs={{16,32},{32,16},{48,64},{64,48},{80,96},{96,80},{17,33},{33,17},{4... | collective-permute-start | bytes 49160 | tf_op jit(solution)/shard_map/ppermute | solution.py:677
  43.7 13.3 %collective-permute-start.8 = (f32[648,128]{1,0:T(8,128)S(1)}, f32[648,128]{1,0:T(8,128)S(1)}, u32[]{:S(2)}, u32[]{:S(2)}) collective-permute-start(f32[648,128]{1,0:T(8,128)S(1)} %get-tuple-element.55), channel_id=1, source_target_pairs={{0,1},{1,2},{2,3},{3,4},{4,5},{5,6},{6,7},{7,8},{8,9},{9,10},{10,1... | collective-permute-start | bytes 995336 | tf_op jit(solution)/shard_map/ppermute | solution.py:667
  45.6 12.6 %collective-permute-start.9 = (f32[648,128]{1,0:T(8,128)S(1)}, f32[648,128]{1,0:T(8,128)S(1)}, u32[]{:S(2)}, u32[]{:S(2)}) collective-permute-start(f32[648,128]{1,0:T(8,128)S(1)} %get-tuple-element.56), channel_id=1, source_target_pairs={{1,0},{2,1},{3,2},{4,3},{5,4},{6,5},{7,6},{8,7},{9,8},{10,9},{11,1... | collective-permute-start | bytes 995336 | tf_op jit(solution)/shard_map/ppermute | solution.py:667
  49.5 7.5 %collective-permute-start.6 = (f32[8,128]{1,0:T(8,128)S(1)}, f32[8,128]{1,0:T(8,128)S(1)}, u32[]{:S(2)}, u32[]{:S(2)}) collective-permute-start(f32[8,128]{1,0:T(8,128)S(1)} %get-tuple-element.53), channel_id=1, source_target_pairs={{0,16},{16,0},{32,48},{48,32},{64,80},{80,64},{96,112},{112,96},{1... | collective-permute-start | bytes 12296 | tf_op jit(solution)/shard_map/ppermute | solution.py:677
  49.6 7.4 %collective-permute-start.7 = (f32[8,128]{1,0:T(8,128)S(1)}, f32[8,128]{1,0:T(8,128)S(1)}, u32[]{:S(2)}, u32[]{:S(2)}) collective-permute-start(f32[8,128]{1,0:T(8,128)S(1)} %get-tuple-element.54), channel_id=1, source_target_pairs={{16,32},{32,16},{48,64},{64,48},{80,96},{96,80},{17,33},{33,17},{4... | collective-permute-start | bytes 12296 | tf_op jit(solution)/shard_map/ppermute | solution.py:677
  53.0 42.9 %collective-permute-start.18 = (f32[1280,128]{1,0:T(8,128)S(1)}, f32[1280,128]{1,0:T(8,128)S(1)}, u32[]{:S(2)}, u32[]{:S(2)}) collective-permute-start(f32[1280,128]{1,0:T(8,128)S(1)} %get-tuple-element.72), channel_id=1, source_target_pairs={{0,1},{1,2},{2,3},{3,4},{4,5},{5,6},{6,7},{7,8},{8,9},{9,10},{10,1... | collective-permute-start | bytes 1966088 | tf_op jit(solution)/shard_map/ppermute | solution.py:667
  60.7 18.3 %collective-permute-start.12 = (f32[648,128]{1,0:T(8,128)S(1)}, f32[648,128]{1,0:T(8,128)S(1)}, u32[]{:S(2)}, u32[]{:S(2)}) collective-permute-start(f32[648,128]{1,0:T(8,128)S(1)} %get-tuple-element.61), channel_id=1, source_target_pairs={{0,1},{1,2},{2,3},{3,4},{4,5},{5,6},{6,7},{7,8},{8,9},{9,10},{10,1... | collective-permute-start | bytes 995336 | tf_op jit(solution)/shard_map/ppermute | solution.py:667
  62.6 16.4 %collective-permute-start.13 = (f32[648,128]{1,0:T(8,128)S(1)}, f32[648,128]{1,0:T(8,128)S(1)}, u32[]{:S(2)}, u32[]{:S(2)}) collective-permute-start(f32[648,128]{1,0:T(8,128)S(1)} %get-tuple-element.62), channel_id=1, source_target_pairs={{1,0},{2,1},{3,2},{4,3},{5,4},{6,5},{7,6},{8,7},{9,8},{10,9},{11,1... | collective-permute-start | bytes 995336 | tf_op jit(solution)/shard_map/ppermute | solution.py:667
  66.5 31.2 %collective-permute-start.19 = (f32[1280,128]{1,0:T(8,128)S(1)}, f32[1280,128]{1,0:T(8,128)S(1)}, u32[]{:S(2)}, u32[]{:S(2)}) collective-permute-start(f32[1280,128]{1,0:T(8,128)S(1)} %get-tuple-element.73), channel_id=1, source_target_pairs={{1,0},{2,1},{3,2},{4,3},{5,4},{6,5},{7,6},{8,7},{9,8},{10,9},{11,1... | collective-permute-start | bytes 1966088 | tf_op jit(solution)/shard_map/ppermute | solution.py:667
  68.5 1.2 collective-permute-start.10
  69.7 4.9 %collective-permute-start.11 = (f32[8,128]{1,0:T(8,128)S(1)}, f32[8,128]{1,0:T(8,128)S(1)}, u32[]{:S(2)}, u32[]{:S(2)}) collective-permute-start(f32[8,128]{1,0:T(8,128)S(1)} %get-tuple-element.60), channel_id=1, source_target_pairs={{16,32},{32,16},{48,64},{64,48},{80,96},{96,80},{17,33},{33,17},{4... | collective-permute-start | bytes 12296 | tf_op jit(solution)/shard_map/ppermute | solution.py:677
  79.0 36.2 %copy-start.3 = (s32[32]{0:T(128)S(1)}, s32[32]{0:T(128)}, u32[]{:S(2)}) copy-start(s32[32]{0:T(128)} %ids.1) | copy-start | bytes 388
  82.1 60.1 %collective-permute-start.20 = (f32[1280,128]{1,0:T(8,128)S(1)}, f32[1280,128]{1,0:T(8,128)S(1)}, u32[]{:S(2)}, u32[]{:S(2)}) collective-permute-start(f32[1280,128]{1,0:T(8,128)S(1)} %get-tuple-element.76), channel_id=1, source_target_pairs={{0,1},{1,2},{2,3},{3,4},{4,5},{5,6},{6,7},{7,8},{8,9},{9,10},{10,1... | collective-permute-start | bytes 1966088 | tf_op jit(solution)/shard_map/ppermute | solution.py:667
  87.9 54.4 %collective-permute-start.21 = (f32[1280,128]{1,0:T(8,128)S(1)}, f32[1280,128]{1,0:T(8,128)S(1)}, u32[]{:S(2)}, u32[]{:S(2)}) collective-permute-start(f32[1280,128]{1,0:T(8,128)S(1)} %get-tuple-element.77), channel_id=1, source_target_pairs={{1,0},{2,1},{3,2},{4,3},{5,4},{6,5},{7,6},{8,7},{9,8},{10,9},{11,1... | collective-permute-start | bytes 1966088 | tf_op jit(solution)/shard_map/ppermute | solution.py:667
  89.8 19.2 %collective-permute-start.16 = (f32[648,128]{1,0:T(8,128)S(1)}, f32[648,128]{1,0:T(8,128)S(1)}, u32[]{:S(2)}, u32[]{:S(2)}) collective-permute-start(f32[648,128]{1,0:T(8,128)S(1)} %get-tuple-element.67), channel_id=1, source_target_pairs={{0,1},{1,2},{2,3},{3,4},{4,5},{5,6},{6,7},{7,8},{8,9},{9,10},{10,1... | collective-permute-start | bytes 995336 | tf_op jit(solution)/shard_map/ppermute | solution.py:667
  95.8 19.4 %collective-permute-start.17 = (f32[648,128]{1,0:T(8,128)S(1)}, f32[648,128]{1,0:T(8,128)S(1)}, u32[]{:S(2)}, u32[]{:S(2)}) collective-permute-start(f32[648,128]{1,0:T(8,128)S(1)} %get-tuple-element.68), channel_id=1, source_target_pairs={{1,0},{2,1},{3,2},{4,3},{5,4},{6,5},{7,6},{8,7},{9,8},{10,9},{11,1... | collective-permute-start | bytes 995336 | tf_op jit(solution)/shard_map/ppermute | solution.py:667
  97.8 1.2 collective-permute-start.14
  99.0 4.9 %collective-permute-start.15 = (f32[8,128]{1,0:T(8,128)S(1)}, f32[8,128]{1,0:T(8,128)S(1)}, u32[]{:S(2)}, u32[]{:S(2)}) collective-permute-start(f32[8,128]{1,0:T(8,128)S(1)} %get-tuple-element.66), channel_id=1, source_target_pairs={{16,32},{32,16},{48,64},{64,48},{80,96},{96,80},{17,33},{33,17},{4... | collective-permute-start | bytes 12296 | tf_op jit(solution)/shard_map/ppermute | solution.py:677
  (2 other events, 21.4 us)

commit v3 on v2

--- a/solution.py
+++ b/solution.py
@@ -27,6 +27,10 @@
 PULL = gravity * step_time / spacing
 RUB = gravity * step_time * 0.5
 GAIN = step_time / spacing
+UNIT_H = 2.0 / (GAIN * PULL)
+UNIT_Q = UNIT_H / GAIN
+FLOOR = 2.0 * min_depth / UNIT_H
+DRAG = RUB * UNIT_Q * (0.5 * UNIT_H) ** (-7.0 / 3.0)
 
 f32 = jnp.float32
 bf16 = jnp.bfloat16
@@ -37,6 +41,13 @@
     depth_face = jnp.maximum(0.5 * (h_lo + h_hi), min_depth)
     drive = flow - (PULL * depth_face) * ((h_hi - h_lo) + slope)
     loss = jnp.exp2(jnp.log2(depth_face) * (-7.0 / 3.0))
+    return drive / (1.0 + (rub * jnp.abs(flow)) * loss)
+
+
+def unit_flux(flow, h_lo, h_hi, slope, rub):
+    depth_sum = jnp.maximum(h_lo + h_hi, FLOOR)
+    drive = flow - depth_sum * ((h_hi - h_lo) + slope)
+    loss = jnp.exp2(jnp.log2(depth_sum) * (-7.0 / 3.0))
     return drive / (1.0 + (rub * jnp.abs(flow)) * loss)
 
 
@@ -103,7 +114,7 @@
 
 
 def extract_kernel(
-    moves, base, depth, discharge, bed, friction, frames, up_out, down_out, early_up, early_down,
+    moves, base, depth, discharge, bed, friction, frames, out_0, out_1, early_0, early_1,
     depth_v, flow_v, bed_v, rough_v, lo_acc, hi_acc, turned, load_sem, sem,
 ):
     lane = iota((TILE, TILE), 1)
@@ -117,7 +128,7 @@
         for c in copies:
             c.start()
         loads.append(copies)
-    start_chunk(EARLY, moves, base, (depth, discharge, bed, friction), early_up, early_down, sem)
+    start_chunk(EARLY, moves, base, (depth, discharge, bed, friction), early_0, early_1, sem)
 
     def strip(f, k):
         return pl.ds((f * STRIPS + k) * TILE, TILE)
@@ -158,41 +169,47 @@
     shape = (2 * MOVERS, SLOTS)
     pick = jnp.zeros(shape, f32)
     for m in range(MOVERS):
-        for way in range(2):
-            leaver = moves[way, 0, m] - base[0]
-            spot = (iota(shape, 0) == (1 - way) * MOVERS + m) & (iota(shape, 1) == leaver)
+        for pairing in range(2):
+            leaver = moves[way_of(base, pairing), 0, m] - base[0]
+            spot = (iota(shape, 0) == pairing * MOVERS + m) & (iota(shape, 1) == leaver)
             pick = jnp.where(spot, 1.0, pick)
     for axis in range(2):
         for c in range(5):
             got = route(pick, frames[pl.ds(axis * SLOTS, SLOTS), pl.ds(c * FIELD, FIELD)])
             to = pl.ds((axis * 5 + c) * FIELD, FIELD)
-            up_out[:, to] = got[:MOVERS]
-            down_out[:, to] = got[MOVERS:]
-    finish_chunk(EARLY, early_up, early_down, sem)
-
-
-def start_chunk(entries, moves, base, tiles, up_out, down_out, sem):
+            out_0[:, to] = got[:MOVERS]
+            out_1[:, to] = got[MOVERS:]
+    finish_chunk(EARLY, early_0, early_1, sem)
+
+
+def start_chunk(entries, moves, base, tiles, out_0, out_1, sem):
     depth, discharge, bed, friction = tiles
-    for way, out in ((1, up_out), (0, down_out)):
+    for pairing, out in enumerate((out_0, out_1)):
+        way = way_of(base, pairing)
         for i, m in enumerate(entries):
             slot = jnp.clip(moves[way, 0, m] - base[0], 0, SLOTS - 1)
             at = i * STATE
             one = pl.ds(pl.multiple_of(slot * TILE, TILE), TILE)
             two = pl.ds(pl.multiple_of(slot * (2 * TILE), TILE), 2 * TILE)
-            pltpu.make_async_copy(depth.at[one], out.at[pl.ds(at, TILE)], sem.at[way]).start()
-            pltpu.make_async_copy(discharge.at[two], out.at[pl.ds(at + TILE, 2 * TILE)], sem.at[way]).start()
-            pltpu.make_async_copy(bed.at[one], out.at[pl.ds(at + 3 * TILE, TILE)], sem.at[way]).start()
-            pltpu.make_async_copy(friction.at[one], out.at[pl.ds(at + 4 * TILE, TILE)], sem.at[way]).start()
-
-
-def finish_chunk(entries, up_out, down_out, sem):
+            pltpu.make_async_copy(depth.at[one], out.at[pl.ds(at, TILE)], sem.at[pairing]).start()
+            pltpu.make_async_copy(discharge.at[two], out.at[pl.ds(at + TILE, 2 * TILE)], sem.at[pairing]).start()
+            pltpu.make_async_copy(bed.at[one], out.at[pl.ds(at + 3 * TILE, TILE)], sem.at[pairing]).start()
+            pltpu.make_async_copy(friction.at[one], out.at[pl.ds(at + 4 * TILE, TILE)], sem.at[pairing]).start()
+
+
+def finish_chunk(entries, out_0, out_1, sem):
     body = pl.ds(0, len(entries) * STATE)
-    for way, out in ((1, up_out), (0, down_out)):
-        pltpu.make_async_copy(out.at[body], out.at[body], sem.at[way]).wait()
-
-
-def is_odd(base):
-    return ((base[0] // (SLOTS * GY)) % 2) == 1
+    for pairing, out in enumerate((out_0, out_1)):
+        pltpu.make_async_copy(out.at[body], out.at[body], sem.at[pairing]).wait()
+
+
+def is_odd(base, axis):
+    return ((base[0] // (SLOTS * (GY if axis == 0 else 1))) % 2) == 1
+
+
+def way_of(base, pairing):
+    odd = (base[0] // SLOTS) % 2
+    return odd if pairing else 1 - odd
 
 
 def swap(odd, a, b):
@@ -200,19 +217,20 @@
 
 
 def settle_kernel(
-    moves, base, nb, frames, from_low, from_high, depth, discharge, bed, friction,
-    dyn, fixed, x_0, x_1, y_up, y_down, sem,
+    moves, base, nb, frames, from_0, from_1, depth, discharge, bed, friction,
+    dyn, fixed, x_0, x_1, y_0, y_1, sem,
 ):
     ride = RIDERS[:1]
-    start_chunk(ride, moves, base, (depth, discharge, bed, friction), y_up, y_down, sem)
+    start_chunk(ride, moves, base, (depth, discharge, bed, friction), y_0, y_1, sem)
     shape = (SLOTS, 2 * MOVERS)
     land = jnp.zeros(shape, f32)
     left = jnp.zeros((SLOTS, TILE), f32)
     for m in range(MOVERS):
-        for way in range(2):
+        for pairing in range(2):
+            way = way_of(base, pairing)
             lander = moves[way, 1, m] - base[0]
             leaver = moves[way, 0, m] - base[0]
-            spot = (iota(shape, 0) == lander) & (iota(shape, 1) == way * MOVERS + m)
+            spot = (iota(shape, 0) == lander) & (iota(shape, 1) == pairing * MOVERS + m)
             land = jnp.where(spot, 1.0, land)
             row = iota((SLOTS, TILE), 0)
             left = jnp.where((row == leaver) | (row == lander), 1.0, left)
@@ -221,7 +239,7 @@
         for f in range(5):
             part = pl.ds(f * FIELD, FIELD)
             came = pl.ds((axis * 5 + f) * FIELD, FIELD)
-            fresh = route(land, jnp.concatenate([from_low[:, came], from_high[:, came]], 0))
+            fresh = route(land, jnp.concatenate([from_0[:, came], from_1[:, came]], 0))
             for k in range(STRIPS):
                 sub = pl.ds(f * FIELD + k * TILE, TILE)
                 value = jnp.where(left > 0.0, 0.0, frames[home, sub]) + fresh[:, k * TILE : (k + 1) * TILE]
@@ -243,14 +261,14 @@
         for f in range(4):
             up = route(higher[2], ups[f])
             down = route(lower[2], downs[f]) if f < 3 else blank
+            up, down = swap(is_odd(base, axis), up, down)
             if axis == 0:
-                up, down = swap(is_odd(base), up, down)
                 x_0[pl.ds(f * MOVERS, MOVERS), :] = up
                 x_1[pl.ds(f * MOVERS, MOVERS), :] = down
             else:
-                y_up[pl.ds(STATE + f * MOVERS, MOVERS), :] = up
-                y_down[pl.ds(STATE + f * MOVERS, MOVERS), :] = down
-    finish_chunk(ride, y_up, y_down, sem)
+                y_0[pl.ds(STATE + f * MOVERS, MOVERS), :] = up
+                y_1[pl.ds(STATE + f * MOVERS, MOVERS), :] = down
+    finish_chunk(ride, y_0, y_1, sem)
 
 
 def other_axis(x):
@@ -269,12 +287,10 @@
         picks.append((lower[2], higher[2]))
 
         def message(f):
-            if axis == 0:
-                rows = pl.ds(f * MOVERS, MOVERS)
-                from_higher, from_lower = swap(is_odd(base_ref), messages[0][0][rows, :], messages[0][1][rows, :])
-                return from_lower, from_higher
-            rows = pl.ds(STATE + f * MOVERS, MOVERS)
-            return messages[1][0][rows, :], messages[1][1][rows, :]
+            rows = pl.ds(axis * STATE + f * MOVERS, MOVERS)
+            pair = messages[axis]
+            from_higher, from_lower = swap(is_odd(base_ref, axis), pair[0][rows, :], pair[1][rows, :])
+            return from_lower, from_higher
 
         def strip(ref, f, k):
             return ref[home, pl.ds(f * FIELD + k * TILE, TILE)]
@@ -305,22 +321,22 @@
     first = turn == 0
     if first:
         still = None
-        (xl, xh, yl, yh), rest = rest[:4], rest[4:]
+        (x0, x1, y0, y1), rest = rest[:4], rest[4:]
     else:
         still = rest[0]
-        (xl, xh, yl, yh), rest = rest[1:5], rest[5:]
+        (x0, x1, y0, y1), rest = rest[1:5], rest[5:]
     depth, discharge, bed, friction = rest[:4]
     tiles = (depth, discharge, bed, friction)
     final = turn == 2
     if final:
-        (dyn_out, still_out, trail, x_0, x_1, y_up, y_down, late_up, late_down, sem) = rest[4:]
+        (dyn_out, still_out, trail, x_0, x_1, y_0, y_1, late_0, late_1, sem) = rest[4:]
     else:
-        (dyn_out, still_out, trail, x_0, x_1, y_up, y_down, sem) = rest[4:]
+        (dyn_out, still_out, trail, x_0, x_1, y_0, y_1, sem) = rest[4:]
     ride = RIDERS[turn + 1 : turn + 2]
-    start_chunk(ride, moves, base, tiles, y_up, y_down, sem.at[0])
+    start_chunk(ride, moves, base, tiles, y_0, y_1, sem.at[0])
     if final:
-        start_chunk(LATE, moves, base, tiles, late_up, late_down, sem.at[1])
-    halo, picks = gather_halos(nb, base, dyn, fixed, ((xl, xh), (yl, yh)), first)
+        start_chunk(LATE, moves, base, tiles, late_0, late_1, sem.at[1])
+    halo, picks = gather_halos(nb, base, dyn, fixed, ((x0, x1), (y0, y1)), first)
     names = ("z_lo", "n_lo", "z_hi", "n_hi", "q_lo")
     if not first:
         for j, name in enumerate(names):
@@ -383,14 +399,16 @@
         home = slice(axis * SLOTS, (axis + 1) * SLOTS)
         up = route(picks[axis][1], new[last][home])
         down = route(picks[axis][0], new[0][home])
+        up, down = swap(is_odd(base, axis), up, down)
         if axis == 0:
-            x_0[...], x_1[...] = swap(is_odd(base), up, down)
+            x_0[...] = up
+            x_1[...] = down
         else:
-            y_up[pl.ds(STATE, MOVERS), :] = up
-            y_down[pl.ds(STATE, MOVERS), :] = down
-    finish_chunk(ride, y_up, y_down, sem.at[0])
+            y_0[pl.ds(STATE, MOVERS), :] = up
+            y_1[pl.ds(STATE, MOVERS), :] = down
+    finish_chunk(ride, y_0, y_1, sem.at[0])
     if final:
-        finish_chunk(LATE, late_up, late_down, sem.at[1])
+        finish_chunk(LATE, late_0, late_1, sem.at[1])
 
 
 def run_tiles(
@@ -448,7 +466,7 @@
 
     prime()
     before_loop()
-    part_rows = 32
+    part_rows = 16
     parts = TILE // part_rows
     lane = iota((part_rows, TILE), 1)
     row = iota((part_rows, TILE), 0)
@@ -484,10 +502,10 @@
             rows = pl.ds(p * part_rows, part_rows)
             zr = pl.ds(3 * TILE + p * part_rows, part_rows)
             nr = pl.ds(4 * TILE + p * part_rows, part_rows)
-            z = box[zr, :]
+            z = box[zr, :] * (1.0 / UNIT_H)
             n = box[nr, :]
             if p < parts - 1:
-                z_dn = box[pl.ds(3 * TILE + p * part_rows + 1, part_rows), :]
+                z_dn = box[pl.ds(3 * TILE + p * part_rows + 1, part_rows), :] * (1.0 / UNIT_H)
                 n_dn = box[pl.ds(4 * TILE + p * part_rows + 1, part_rows), :]
             else:
                 z_dn = jnp.where(bottom, z_next, pltpu.roll(z, part_rows - 1, 0))
@@ -497,9 +515,9 @@
             n_rt = jnp.where(at_last, pltpu.roll(side, TILE - 1 - SLOTS - t, 1), pltpu.roll(n, TILE - 1, 1))
             slope_x[rows, :] = z_dn - z
             slope_y[rows, :] = z_rt - z
-            rub_x[rows, :] = RUB * (n + n_dn)
-            rub_y[rows, :] = RUB * (n + n_rt)
-            water[pl.ds(p * part_rows, part_rows), :] = box[rows, :]
+            rub_x[rows, :] = DRAG * (n + n_dn)
+            rub_y[rows, :] = DRAG * (n + n_rt)
+            water[rows, :] = box[rows, :] * (1.0 / UNIT_H)
         for s in range(4):
             water[pl.ds(TILE, 1), :] = edge_row(4 + s)
             stream_x[pl.ds(7, 1), :] = edge_row(s)
@@ -510,29 +528,29 @@
                 side = pltpu.roll(columns[s // 2, rows, :], TILE - 1 - 64 * (s % 2) - 2 * t, 1)
                 h_rt = jnp.where(at_last, side, pltpu.roll(h, TILE - 1, 1))
                 if s == 0:
-                    flow_x = box[pl.ds(TILE + p * part_rows, part_rows), :]
-                    flow_y = box[pl.ds(2 * TILE + p * part_rows, part_rows), :]
+                    flow_x = box[pl.ds(TILE + p * part_rows, part_rows), :] * (1.0 / UNIT_Q)
+                    flow_y = box[pl.ds(2 * TILE + p * part_rows, part_rows), :] * (1.0 / UNIT_Q)
                 else:
                     flow_x = stream_x[pl.ds(8 + p * part_rows, part_rows), :]
                     flow_y = stream_y[rows, :]
-                new_x = flux(flow_x, h, h_dn, slope_x[rows, :], rub_x[rows, :])
+                new_x = unit_flux(flow_x, h, h_dn, slope_x[rows, :], rub_x[rows, :])
                 if p == parts - 1:
                     new_x = jnp.where(bottom & wall_x, 0.0, new_x)
-                new_y = flux(flow_y, h, h_rt, slope_y[rows, :], rub_y[rows, :])
+                new_y = unit_flux(flow_y, h, h_rt, slope_y[rows, :], rub_y[rows, :])
                 new_y = jnp.where(at_last & wall_y, 0.0, new_y)
                 if s < 3:
                     stream_y[rows, :] = new_y
                 else:
-                    out[pl.ds(TILE + p * part_rows, part_rows), :] = new_x
-                    out[pl.ds(2 * TILE + p * part_rows, part_rows), :] = new_y
+                    out[pl.ds(TILE + p * part_rows, part_rows), :] = new_x * UNIT_Q
+                    out[pl.ds(2 * TILE + p * part_rows, part_rows), :] = new_y * UNIT_Q
                 in_y = jnp.where(at_first, side, pltpu.roll(new_y, 1, 1))
                 stream_x[pl.ds(8 + p * part_rows, part_rows), :] = new_x
                 in_x = stream_x[pl.ds(7 + p * part_rows, part_rows), :]
-                h_new = h + GAIN * ((in_x - new_x) + (in_y - new_y))
+                h_new = h + ((in_x - new_x) + (in_y - new_y))
                 if s < 3:
                     water[rows, :] = h_new
                 else:
-                    out[rows, :] = h_new
+                    out[rows, :] = h_new * UNIT_H
         send(t, buf)
         return carry
 
@@ -544,27 +562,27 @@
             sent(b)
 
 
-def chunk_sources(entries, low, high):
+def chunk_sources(entries, *chunks):
     found = []
-    for way, ref in ((0, low), (1, high)):
+    for pairing, ref in enumerate(chunks):
         for i, m in enumerate(entries):
-            found.append((1 + way * MOVERS + m, ref, i * STATE))
+            found.append((1 + pairing * MOVERS + m, ref, i * STATE))
     return found
 
 
 def note_arrivals(entries, moves, base, visit):
     for m in entries:
-        for way in range(2):
-            lander = moves[way, 1, m]
+        for pairing in range(2):
+            lander = moves[way_of(base, pairing), 1, m]
 
             @pl.when(lander >= 0)
             def _():
-                visit(lander - base[0], 1 + way * MOVERS + m)
+                visit(lander - base[0], 1 + pairing * MOVERS + m)
 
 
 def tile_kernel(
     moves, base, ids, nb_s, nb, dyn, fixed, still, x_0, x_1, l3, u3, t0, t1, t2,
-    l0, l1, l2, u0, u1, u2, early_low, early_high, depth, discharge, bed, friction,
+    l0, l1, l2, u0, u1, u2, early_0, early_1, depth, discharge, bed, friction,
     depth_out, flow_out, edges, columns,
     zeros, turned, queue, origin, zero_sem, *scratch,
 ):
@@ -611,21 +629,24 @@
         trails = [(t[:, pl.ds(0, TILE)], t[:, pl.ds(TILE, TILE)]) for t in (t0, t1, t2)]
         trails.append((low_face, halo["h_hi"]))
         for s, (inflow, ahead_h) in enumerate(trails):
+            inflow = inflow * (1.0 / UNIT_Q)
+            ahead_h = ahead_h * (1.0 / UNIT_H)
             edges[s] = inflow[:SLOTS]
             edges[4 + s] = ahead_h[:SLOTS]
             turned[pl.ds(64 * (s % 2), SLOTS, stride=2), :] = ahead_h[SLOTS:]
             turned[pl.ds(64 * (s % 2) + 1, SLOTS, stride=2), :] = inflow[SLOTS:]
             if s % 2:
                 columns[s // 2] = turned[...].T
-        edges[8] = kept(2)[:SLOTS]
+        z_ahead = kept(2) * (1.0 / UNIT_H)
+        edges[8] = z_ahead[:SLOTS]
         edges[9] = kept(3)[:SLOTS]
-        turned[pl.ds(0, SLOTS), :] = kept(2)[SLOTS:]
+        turned[pl.ds(0, SLOTS), :] = z_ahead[SLOTS:]
         turned[pl.ds(SLOTS, SLOTS), :] = kept(3)[SLOTS:]
         columns[2] = turned[...].T
 
-    sources = chunk_sources(EARLY, early_low, early_high)
-    for m, low, high in zip(RIDERS, (l0, l1, l2, l3), (u0, u1, u2, u3)):
-        sources += chunk_sources((m,), low, high)
+    sources = chunk_sources(EARLY, early_0, early_1)
+    for m, chunk_0, chunk_1 in zip(RIDERS, (l0, l1, l2, l3), (u0, u1, u2, u3)):
+        sources += chunk_sources((m,), chunk_0, chunk_1)
     run_tiles(
         queue, origin, count, sources, (depth, discharge, bed, friction), nb_s, edges, columns,
         (depth_out, flow_out), before_loop, *scratch,
@@ -639,7 +660,7 @@
 
 
 def late_kernel(
-    moves, base, nb_s, edges, columns, late_low, late_high, depth_in, flow_in,
+    moves, base, nb_s, edges, columns, late_0, late_1, depth_in, flow_in,
     depth_out, flow_out, queue, origin, size, *scratch,
 ):
     size[0] = 0
@@ -651,7 +672,7 @@
 
     note_arrivals(LATE, moves, base, enqueue)
     run_tiles(
-        queue, origin, size[0], chunk_sources(LATE, late_low, late_high), (None,) * 4, nb_s, edges, columns,
+        queue, origin, size[0], chunk_sources(LATE, late_0, late_1), (None,) * 4, nb_s, edges, columns,
         (depth_out, flow_out), lambda: None, *scratch,
     )
 
@@ -661,31 +682,26 @@
 HBM = pl.BlockSpec(memory_space=pltpu.HBM)
 
 
-def ride_up(block, axis, distance):
-    devices = range(lax.axis_size(axis))
-    route_pairs = [(i - distance, i) for i in devices if i - distance in devices]
-    return lax.ppermute(block, axis, route_pairs)
-
-
-def trade(block, pairing):
-    size = lax.axis_size("gx")
+def trade(block, axis, pairing):
+    size = lax.axis_size(axis)
     pairs = []
     for i in range(size):
         other = i ^ 1 if pairing == 0 else ((i + 1) ^ 1) - 1
         if 0 <= other < size:
             pairs.append((i, other))
-    return lax.ppermute(block, "gx", pairs)
-
-
-def both_ways(up, down):
-    low = ride_up(up, "gy", 1)
-    high = ride_up(down, "gy", -1)
-    return low, high
-
-
-def exchange(x_0, x_1, y_up, y_down):
-    got_y = both_ways(y_up, y_down)
-    return trade(x_0, 0), trade(x_1, 1), got_y[0], got_y[1]
+    return lax.ppermute(block, axis, pairs)
+
+
+def trade_both(block_0, block_1, axis):
+    got_1 = trade(block_1, axis, 1)
+    got_0 = trade(block_0, axis, 0)
+    return got_0, got_1
+
+
+def exchange(x_0, x_1, y_0, y_1):
+    got_y = trade_both(y_0, y_1, "gy")
+    got_x = trade_both(x_0, x_1, "gx")
+    return *got_x, *got_y
 
 
 def held(*shape):
@@ -734,7 +750,7 @@
         )
     ]
     early_rows = len(EARLY) * STATE
-    frames, up, down, early_up, early_down = pl.pallas_call(
+    frames, up, down, early_0, early_1 = pl.pallas_call(
         extract_kernel,
         in_specs=[SMEM, SMEM] + [HBM] * 4,
         out_specs=[VMEM] * 5,
@@ -759,8 +775,8 @@
         compiler_params=pltpu.CompilerParams(vmem_limit_bytes=20 * 2**20),
         name="extract",
     )(plan, base, *tiles)
-    from_low, from_high = both_ways(up, down)
-    early_low, early_high = both_ways(early_up, early_down)
+    from_0, from_1 = trade_both(up, down, "gy")
+    early_0, early_1 = trade_both(early_0, early_1, "gy")
 
     first_rows = 4 * MOVERS
     dyn, fixed, *sends = call(
@@ -777,7 +793,7 @@
         ],
         scratch_shapes=[pltpu.SemaphoreType.DMA((2,))],
         compiler_params=pltpu.CompilerParams(vmem_limit_bytes=12 * 2**20),
-    )(plan, base, *on_core(nb, frames, from_low, from_high), *tiles)
+    )(plan, base, *on_core(nb, frames, from_0, from_1), *tiles)
     got = exchange(*sends)
     lows = [got[2]]
     highs = [got[3]]
@@ -815,9 +831,9 @@
         lows.append(got[2])
         highs.append(got[3])
 
-    late_low, late_high = both_ways(*late)
+    late_0, late_1 = trade_both(*late, "gy")
     kept_inputs = on_core(
-        nb, dyn, fixed, *still, *got, *trails, *lows[:3], *highs[:3], early_low, early_high
+        nb, dyn, fixed, *still, *got, *trails, *lows[:3], *highs[:3], early_0, early_1
     )
     new_depth, new_flow, edges, columns = call(
         tile_kernel,
@@ -853,7 +869,7 @@
         ],
         compiler_params=pltpu.CompilerParams(vmem_limit_bytes=12 * 2**20),
         name="late_tiles",
-    )(plan, base, nb, *on_core(edges, columns, late_low, late_high), new_depth, new_flow)
+    )(plan, base, nb, *on_core(edges, columns, late_0, late_1), new_depth, new_flow)
     return (
         new_depth.reshape(SLOTS, TILE, TILE),
         new_flow.reshape(SLOTS, 2, TILE, TILE),

time: 147 us -> 137 us (0.932)
  the two profiles are of different devices: /device:TPU:60 before, /device:TPU:100 now
where the time goes in v3:
time: 137 us; the launch traced here: 136 us
  Pallas kernels  50.4 us (37%)
  waiting for transfers between devices  43.9 us (32%)
  starting transfers between devices  40.5 us (30%)
    ppermute x22, waiting for transfers between devices, trade(): return lax.ppermute(block, axis, pairs)  43.9 us
    ppermute x22, starting transfers between devices, trade(): return lax.ppermute(block, axis, pairs)  40.5 us
    pallas_call x1, Pallas kernels, shards(): call(tile_kernel, in_specs=[SMEM] * 4 + [VMEM] * len(kept_inputs) + [HBM]...  28.2 us
    pallas_call x3, Pallas kernels, shards(): call(body, in_specs=[SMEM, SMEM] + [VMEM] * (7 + len(still)) + [HBM] * 4,...  7.73 us
    pallas_call x1, Pallas kernels, shards(): pl.pallas_call(extract_kernel, in_specs=[SMEM, SMEM] + [HBM] * 4, out_spe...  7.12 us
    pallas_call x1, Pallas kernels, shards(): pl.pallas_call(late_kernel, in_specs=[SMEM] * 3 + [VMEM] * 4 + [HBM] * 2,...  5.07 us
  transfers between devices with their start and end apart: 22, of which 15 were waited for; matrix products, arithmetic and copies ran while one was open for 0% of the time, Pallas kernels for 24%

profile of v3, /device:TPU:100, one launch (start us, length us, event | category | flops | bytes accessed | tf_op | source)
XLA Modules:
  0.0 136.4 jit_solution(12686546068086810824)
XLA Ops:
  1.3 7.1 %extract.1 = (f32[64,5120]{1,0:T(8,128)S(1)}, f32[8,10240]{1,0:T(8,128)S(1)}, f32[8,10240]{1,0:T(8,128)S(1)}, f32[1280,128]{1,0:T(8,128)S(1)}, f32[1280,128]{1,0:T(8,128)S(1)}) custom-call(s32[2,2,8]{2,1,0:T(2,128)S(1)} %bitcast.11, s32[1]{0:T(128)} %bitcast.2.base.refs_1_, f32[4096,128]{1,0:T(8,128)} %bitcast.31, f32[8192,128]{1,0:T(8,128)} %bitcast.25, ...), custom_call_target="tpu_custom_call" | custom-call | tf_op jit(solution)/shard_map/extract/pallas_call | solution.py:753
  9.4 4.0 %collective-permute-start.1 = (f32[8,10240]{1,0:T(8,128)S(1)}, f32[8,10240]{1,0:T(8,128)S(1)}, u32[]{:S(2)}, u32[]{:S(2)}) collective-permute-start(f32[8,10240]{1,0:T(8,128)S(1)} %get-tuple-element.44), channel_id=1, source_target_pairs={{1,2},{2,1},{3,4},{4,3},{5,6},{6,5},{7,8},{8,7},{9,10},{10,9},{11,... | collective-permute-start | bytes 983048 | tf_op jit(solution)/shard_map/ppermute | solution.py:692
  13.5 4.5 %collective-permute-done.from_0 = f32[8,10240]{1,0:T(8,128)S(1)} collective-permute-done((f32[8,10240]{1,0:T(8,128)S(1)}, f32[8,10240]{1,0:T(8,128)S(1)}, u32[]{:S(2)}, u32[]{:S(2)}) %collective-permute-start) | collective-permute-done | bytes 327712 | tf_op jit(solution)/shard_map/ppermute | solution.py:692
  18.0 5.3 %collective-permute-done.1.from_1 = f32[8,10240]{1,0:T(8,128)S(1)} collective-permute-done((f32[8,10240]{1,0:T(8,128)S(1)}, f32[8,10240]{1,0:T(8,128)S(1)}, u32[]{:S(2)}, u32[]{:S(2)}) %collective-permute-start.1) | collective-permute-done | bytes 327712 | tf_op jit(solution)/shard_map/ppermute | solution.py:692
  23.3 2.3 %shard_map.86 = (f32[64,3072]{1,0:T(8,128)S(1)}, f32[64,2048]{1,0:T(8,128)S(1)}, f32[32,128]{1,0:T(8,128)S(1)}, f32[32,128]{1,0:T(8,128)S(1)}, f32[672,128]{1,0:T(8,128)S(1)}, /*index=5*/f32[672,128]{1,0:T(8,128)S(1)}) custom-call(s32[2,2,8]{2,1,0:T(2,128)S(1)} %bitcast.12, s32[1]{0:T(128)} %bitcast.2.base.refs_1_, s32[4,32]{1,0:T(4,128)S(1)} %bitcast.18, ...), custom_call_target="tpu_custom_call" | custom-call | tf_op jit(solution)/shard_map/pallas_call | solution.py:782
  25.7 4.1 %collective-permute-start.5 = (f32[672,128]{1,0:T(8,128)S(1)}, f32[672,128]{1,0:T(8,128)S(1)}, u32[]{:S(2)}, u32[]{:S(2)}) collective-permute-start(f32[672,128]{1,0:T(8,128)S(1)} %get-tuple-element.50), channel_id=1, source_target_pairs={{1,2},{2,1},{3,4},{4,3},{5,6},{6,5},{7,8},{8,7},{9,10},{10,9},{11,... | collective-permute-start | bytes 1032200 | tf_op jit(solution)/shard_map/ppermute | solution.py:692
  31.8 3.1 %collective-permute-done.3.refs_6_ = f32[32,128]{1,0:T(8,128)S(1)} collective-permute-done((f32[32,128]{1,0:T(8,128)S(1)}, f32[32,128]{1,0:T(8,128)S(1)}, u32[]{:S(2)}, u32[]{:S(2)}) %collective-permute-start.3) | collective-permute-done | bytes 16416 | tf_op jit(solution)/shard_map/ppermute | solution.py:692
  35.0 4.0 %collective-permute-done.5.refs_8_.u0 = f32[672,128]{1,0:T(8,128)S(1)} collective-permute-done((f32[672,128]{1,0:T(8,128)S(1)}, f32[672,128]{1,0:T(8,128)S(1)}, u32[]{:S(2)}, u32[]{:S(2)}) %collective-permute-start.5) | collective-permute-done | bytes 344096 | tf_op jit(solution)/shard_map/ppermute | solution.py:692
  39.1 2.6 %shard_map.87 = (f32[64,3072]{1,0:T(8,128)S(1)}, f32[64,640]{1,0:T(8,128)S(1)}, f32[64,256]{1,0:T(8,128)S(1)}, f32[8,128]{1,0:T(8,128)S(1)}, f32[8,128]{1,0:T(8,...) custom-call(s32[2,2,8]{2,1,0:T(2,128)S(1)} %bitcast.13, s32[1]{0:T(128)} %bitcast.2.base.refs_1_, ...), custom_call_target="tpu_custom_call" | custom-call | tf_op jit(solution)/shard_map/pallas_call | solution.py:819
  41.8 4.0 %collective-permute-start.9 = (f32[648,128]{1,0:T(8,128)S(1)}, f32[648,128]{1,0:T(8,128)S(1)}, u32[]{:S(2)}, u32[]{:S(2)}) collective-permute-start(f32[648,128]{1,0:T(8,128)S(1)} %get-tuple-element.56), channel_id=1, source_target_pairs={{1,2},{2,1},{3,4},{4,3},{5,6},{6,5},{7,8},{8,7},{9,10},{10,9},{11,... | collective-permute-start | bytes 995336 | tf_op jit(solution)/shard_map/ppermute | solution.py:692
  50.9 3.2 %collective-permute-done.9.refs_9_.u1 = f32[648,128]{1,0:T(8,128)S(1)} collective-permute-done((f32[648,128]{1,0:T(8,128)S(1)}, f32[648,128]{1,0:T(8,128)S(1)}, u32[]{:S(2)}, u32[]{:S(2)}) %collective-permute-start.9) | collective-permute-done | bytes 331808 | tf_op jit(solution)/shard_map/ppermute | solution.py:692
  54.0 2.4 %shard_map.88 = (f32[64,3072]{1,0:T(8,128)S(1)}, f32[64,640]{1,0:T(8,128)S(1)}, f32[64,256]{1,0:T(8,128)S(1)}, f32[8,128]{1,0:T(8,128)S(1)}, f32[8,128]{1,0:T(8,...) custom-call(s32[2,2,8]{2,1,0:T(2,128)S(1)} %bitcast.14, s32[1]{0:T(128)} %bitcast.2.base.refs_1_, ...), custom_call_target="tpu_custom_call" | custom-call | tf_op jit(solution)/shard_map/pallas_call | solution.py:819
  56.5 4.0 %collective-permute-start.13 = (f32[648,128]{1,0:T(8,128)S(1)}, f32[648,128]{1,0:T(8,128)S(1)}, u32[]{:S(2)}, u32[]{:S(2)}) collective-permute-start(f32[648,128]{1,0:T(8,128)S(1)} %get-tuple-element.62), channel_id=1, source_target_pairs={{1,2},{2,1},{3,4},{4,3},{5,6},{6,5},{7,8},{8,7},{9,10},{10,9},{11,... | collective-permute-start | bytes 995336 | tf_op jit(solution)/shard_map/ppermute | solution.py:692
  60.6 3.9 %collective-permute-start.19 = (f32[1280,128]{1,0:T(8,128)S(1)}, f32[1280,128]{1,0:T(8,128)S(1)}, u32[]{:S(2)}, u32[]{:S(2)}) collective-permute-start(f32[1280,128]{1,0:T(8,128)S(1)} %get-tuple-element.73), channel_id=1, source_target_pairs={{1,2},{2,1},{3,4},{4,3},{5,6},{6,5},{7,8},{8,7},{9,10},{10,9},{11,... | collective-permute-start | bytes 1966088 | tf_op jit(solution)/shard_map/ppermute | solution.py:692
  65.7 2.4 %collective-permute-start.11 = (f32[8,128]{1,0:T(8,128)S(1)}, f32[8,128]{1,0:T(8,128)S(1)}, u32[]{:S(2)}, u32[]{:S(2)}) collective-permute-start(f32[8,128]{1,0:T(8,128)S(1)} %get-tuple-element.60), channel_id=1, source_target_pairs={{16,32},{32,16},{48,64},{64,48},{80,96},{96,80},{17,33},{33,17},{4... | collective-permute-start | bytes 12296 | tf_op jit(solution)/shard_map/ppermute | solution.py:692
  68.2 2.5 %collective-permute-done.11.refs_7_ = f32[8,128]{1,0:T(8,128)S(1)} collective-permute-done((f32[8,128]{1,0:T(8,128)S(1)}, f32[8,128]{1,0:T(8,128)S(1)}, u32[]{:S(2)}, u32[]{:S(2)}) %collective-permute-start.11) | collective-permute-done | bytes 4128 | tf_op jit(solution)/shard_map/ppermute | solution.py:692
  71.2 2.7 %shard_map.89 = (f32[64,3072]{1,0:T(8,128)S(1)}, f32[64,640]{1,0:T(8,128)S(1)}, f32[64,256]{1,0:T(8,128)S(1)}, f32[8,128]{1,0:T(8,128)S(1)}, f32[8,128]{1,0:T(8,...) custom-call(s32[2,2,8]{2,1,0:T(2,128)S(1)} %bitcast.15, ...), custom_call_target="tpu_custom_call" | custom-call | tf_op jit(solution)/shard_map/pallas_call | solution.py:819
  74.3 4.2 %collective-permute-start.21 = (f32[1280,128]{1,0:T(8,128)S(1)}, f32[1280,128]{1,0:T(8,128)S(1)}, u32[]{:S(2)}, u32[]{:S(2)}) collective-permute-start(f32[1280,128]{1,0:T(8,128)S(1)} %get-tuple-element.77), channel_id=1, source_target_pairs={{1,2},{2,1},{3,4},{4,3},{5,6},{6,5},{7,8},{8,7},{9,10},{10,9},{11,... | collective-permute-start | bytes 1966088 | tf_op jit(solution)/shard_map/ppermute | solution.py:692
  85.7 2.4 %collective-permute-start.15 = (f32[8,128]{1,0:T(8,128)S(1)}, f32[8,128]{1,0:T(8,128)S(1)}, u32[]{:S(2)}, u32[]{:S(2)}) collective-permute-start(f32[8,128]{1,0:T(8,128)S(1)} %get-tuple-element.66), channel_id=1, source_target_pairs={{16,32},{32,16},{48,64},{64,48},{80,96},{96,80},{17,33},{33,17},{4... | collective-permute-start | bytes 12296 | tf_op jit(solution)/shard_map/ppermute | solution.py:692
  88.1 2.5 %collective-permute-done.15.x_1 = f32[8,128]{1,0:T(8,128)S(1)} collective-permute-done((f32[8,128]{1,0:T(8,128)S(1)}, f32[8,128]{1,0:T(8,128)S(1)}, u32[]{:S(2)}, u32[]{:S(2)}) %collective-permute-start.15) | collective-permute-done | bytes 4128 | tf_op jit(solution)/shard_map/ppermute | solution.py:692
  90.6 5.9 %collective-permute-done.16.l3 = f32[648,128]{1,0:T(8,128)S(1)} collective-permute-done((f32[648,128]{1,0:T(8,128)S(1)}, f32[648,128]{1,0:T(8,128)S(1)}, u32[]{:S(2)}, u32[]{:S(2)}) %collective-permute-start.16) | collective-permute-done | bytes 331808 | tf_op jit(solution)/shard_map/ppermute | solution.py:692
  96.5 6.6 %collective-permute-done.17.u3 = f32[648,128]{1,0:T(8,128)S(1)} collective-permute-done((f32[648,128]{1,0:T(8,128)S(1)}, f32[648,128]{1,0:T(8,128)S(1)}, u32[]{:S(2)}, u32[]{:S(2)}) %collective-permute-start.17) | collective-permute-done | bytes 331808 | tf_op jit(solution)/shard_map/ppermute | solution.py:692
  103.1 28.2 %shard_map.90 = (f32[4096,128]{1,0:T(8,128)}, f32[8192,128]{1,0:T(8,128)}, f32[10,32,128]{2,1,0:T(8,128)S(1)}, f32[3,128,128]{2,1,0:T(8,128)S(1)}) custom-call(s32[2,2,8]{2,1,0:T(2,128)S(1)} %bitcast.16, s32[1]{0:T(128)} %bitcast.2.base.refs_1_, s32[32]{0:T(128)S(1)} %copy-done.3, s32[4,32]{1,0:T(4,128)S(1)} %bitcast.22, s32[4,32]{1,0:T(4,128)S(1)} %bitcast.23, ...), custom_call_target="tpu_custom_call" | custom-call | tf_op jit(solution)/shard_map/pallas_call | solution.py:838
  131.3 5.1 %late_tiles.1 = (f32[4096,128]{1,0:T(8,128)}, f32[8192,128]{1,0:T(8,128)}) custom-call(s32[2,2,8]{2,1,0:T(2,128)S(1)} %bitcast.17, s32[1]{0:T(128)} %bitcast.2.base.refs_1_, s32[4,32]{1,0:T(4,128)S(1)} %bitcast.24, f32[10,32,128]{2,1,0:T(8,128)S(1)} %get-tuple-element.74.edges, ...), custom_call_target="tpu_custom_call", output_to_operand_aliasing={{0}: (7, {}), {1}: (8, {})} | custom-call | tf_op jit(solution)/shard_map/late_tiles/pallas_call | solution.py:858
  (35 shorter events, 18.4 us)
Async XLA Ops:
  1.3 22.0 %copy-start.2 = (s32[32,4]{0,1:T(4,128)S(1)}, s32[32,4]{0,1:T(4,128)}, u32[]{:S(2)}) copy-start(s32[32,4]{0,1:T(4,128)} %param.12) | copy-start | bytes 1540
  8.4 9.5 %collective-permute-start = (f32[8,10240]{1,0:T(8,128)S(1)}, f32[8,10240]{1,0:T(8,128)S(1)}, u32[]{:S(2)}, u32[]{:S(2)}) collective-permute-start(f32[8,10240]{1,0:T(8,128)S(1)} %get-tuple-element.43), channel_id=1, source_target_pairs={{0,1},{1,0},{2,3},{3,2},{4,5},{5,4},{6,7},{7,6},{8,9},{9,8},{10,11... | collective-permute-start | bytes 983048 | tf_op jit(solution)/shard_map/ppermute | solution.py:692
  9.4 13.9 %collective-permute-start.1 = (f32[8,10240]{1,0:T(8,128)S(1)}, f32[8,10240]{1,0:T(8,128)S(1)}, u32[]{:S(2)}, u32[]{:S(2)}) collective-permute-start(f32[8,10240]{1,0:T(8,128)S(1)} %get-tuple-element.44), channel_id=1, source_target_pairs={{1,2},{2,1},{3,4},{4,3},{5,6},{6,5},{7,8},{8,7},{9,10},{10,9},{11,... | collective-permute-start | bytes 983048 | tf_op jit(solution)/shard_map/ppermute | solution.py:692
  25.6 9.4 %collective-permute-start.4 = (f32[672,128]{1,0:T(8,128)S(1)}, f32[672,128]{1,0:T(8,128)S(1)}, u32[]{:S(2)}, u32[]{:S(2)}) collective-permute-start(f32[672,128]{1,0:T(8,128)S(1)} %get-tuple-element.49), channel_id=1, source_target_pairs={{0,1},{1,0},{2,3},{3,2},{4,5},{5,4},{6,7},{7,6},{8,9},{9,8},{10,11... | collective-permute-start | bytes 1032200 | tf_op jit(solution)/shard_map/ppermute | solution.py:692
  25.7 13.4 %collective-permute-start.5 = (f32[672,128]{1,0:T(8,128)S(1)}, f32[672,128]{1,0:T(8,128)S(1)}, u32[]{:S(2)}, u32[]{:S(2)}) collective-permute-start(f32[672,128]{1,0:T(8,128)S(1)} %get-tuple-element.50), channel_id=1, source_target_pairs={{1,2},{2,1},{3,4},{4,3},{5,6},{6,5},{7,8},{8,7},{9,10},{10,9},{11,... | collective-permute-start | bytes 1032200 | tf_op jit(solution)/shard_map/ppermute | solution.py:692
  29.8 2.0 %collective-permute-start.2 = (f32[32,128]{1,0:T(8,128)S(1)}, f32[32,128]{1,0:T(8,128)S(1)}, u32[]{:S(2)}, u32[]{:S(2)}) collective-permute-start(f32[32,128]{1,0:T(8,128)S(1)} %get-tuple-element.47), channel_id=1, source_target_pairs={{0,16},{16,0},{32,48},{48,32},{64,80},{80,64},{96,112},{112,96},{1... | collective-permute-start | bytes 49160 | tf_op jit(solution)/shard_map/ppermute | solution.py:692
  29.9 5.1 %collective-permute-start.3 = (f32[32,128]{1,0:T(8,128)S(1)}, f32[32,128]{1,0:T(8,128)S(1)}, u32[]{:S(2)}, u32[]{:S(2)}) collective-permute-start(f32[32,128]{1,0:T(8,128)S(1)} %get-tuple-element.48), channel_id=1, source_target_pairs={{16,32},{32,16},{48,64},{64,48},{80,96},{96,80},{17,33},{33,17},{4... | collective-permute-start | bytes 49160 | tf_op jit(solution)/shard_map/ppermute | solution.py:692
  41.7 9.2 %collective-permute-start.8 = (f32[648,128]{1,0:T(8,128)S(1)}, f32[648,128]{1,0:T(8,128)S(1)}, u32[]{:S(2)}, u32[]{:S(2)}) collective-permute-start(f32[648,128]{1,0:T(8,128)S(1)} %get-tuple-element.55), channel_id=1, source_target_pairs={{0,1},{1,0},{2,3},{3,2},{4,5},{5,4},{6,7},{7,6},{8,9},{9,8},{10,11... | collective-permute-start | bytes 995336 | tf_op jit(solution)/shard_map/ppermute | solution.py:692
  41.8 12.2 %collective-permute-start.9 = (f32[648,128]{1,0:T(8,128)S(1)}, f32[648,128]{1,0:T(8,128)S(1)}, u32[]{:S(2)}, u32[]{:S(2)}) collective-permute-start(f32[648,128]{1,0:T(8,128)S(1)} %get-tuple-element.56), channel_id=1, source_target_pairs={{1,2},{2,1},{3,4},{4,3},{5,6},{6,5},{7,8},{8,7},{9,10},{10,9},{11,... | collective-permute-start | bytes 995336 | tf_op jit(solution)/shard_map/ppermute | solution.py:692
  45.8 3.9 %collective-permute-start.6 = (f32[8,128]{1,0:T(8,128)S(1)}, f32[8,128]{1,0:T(8,128)S(1)}, u32[]{:S(2)}, u32[]{:S(2)}) collective-permute-start(f32[8,128]{1,0:T(8,128)S(1)} %get-tuple-element.53), channel_id=1, source_target_pairs={{0,16},{16,0},{32,48},{48,32},{64,80},{80,64},{96,112},{112,96},{1... | collective-permute-start | bytes 12296 | tf_op jit(solution)/shard_map/ppermute | solution.py:692
  45.9 4.9 %collective-permute-start.7 = (f32[8,128]{1,0:T(8,128)S(1)}, f32[8,128]{1,0:T(8,128)S(1)}, u32[]{:S(2)}, u32[]{:S(2)}) collective-permute-start(f32[8,128]{1,0:T(8,128)S(1)} %get-tuple-element.54), channel_id=1, source_target_pairs={{16,32},{32,16},{48,64},{64,48},{80,96},{96,80},{17,33},{33,17},{4... | collective-permute-start | bytes 12296 | tf_op jit(solution)/shard_map/ppermute | solution.py:692
  47.9 32.2 %collective-permute-start.18 = (f32[1280,128]{1,0:T(8,128)S(1)}, f32[1280,128]{1,0:T(8,128)S(1)}, u32[]{:S(2)}, u32[]{:S(2)}) collective-permute-start(f32[1280,128]{1,0:T(8,128)S(1)} %get-tuple-element.72), channel_id=1, source_target_pairs={{0,1},{1,0},{2,3},{3,2},{4,5},{5,4},{6,7},{7,6},{8,9},{9,8},{10,11... | collective-permute-start | bytes 1966088 | tf_op jit(solution)/shard_map/ppermute | solution.py:692
  56.4 14.7 %collective-permute-start.12 = (f32[648,128]{1,0:T(8,128)S(1)}, f32[648,128]{1,0:T(8,128)S(1)}, u32[]{:S(2)}, u32[]{:S(2)}) collective-permute-start(f32[648,128]{1,0:T(8,128)S(1)} %get-tuple-element.61), channel_id=1, source_target_pairs={{0,1},{1,0},{2,3},{3,2},{4,5},{5,4},{6,7},{7,6},{8,9},{9,8},{10,11... | collective-permute-start | bytes 995336 | tf_op jit(solution)/shard_map/ppermute | solution.py:692
  56.5 14.7 %collective-permute-start.13 = (f32[648,128]{1,0:T(8,128)S(1)}, f32[648,128]{1,0:T(8,128)S(1)}, u32[]{:S(2)}, u32[]{:S(2)}) collective-permute-start(f32[648,128]{1,0:T(8,128)S(1)} %get-tuple-element.62), channel_id=1, source_target_pairs={{1,2},{2,1},{3,4},{4,3},{5,6},{6,5},{7,8},{8,7},{9,10},{10,9},{11,... | collective-permute-start | bytes 995336 | tf_op jit(solution)/shard_map/ppermute | solution.py:692
  60.6 23.9 %collective-permute-start.19 = (f32[1280,128]{1,0:T(8,128)S(1)}, f32[1280,128]{1,0:T(8,128)S(1)}, u32[]{:S(2)}, u32[]{:S(2)}) collective-permute-start(f32[1280,128]{1,0:T(8,128)S(1)} %get-tuple-element.73), channel_id=1, source_target_pairs={{1,2},{2,1},{3,4},{4,3},{5,6},{6,5},{7,8},{8,7},{9,10},{10,9},{11,... | collective-permute-start | bytes 1966088 | tf_op jit(solution)/shard_map/ppermute | solution.py:692
  64.5 1.2 collective-permute-start.10
  65.7 4.9 %collective-permute-start.11 = (f32[8,128]{1,0:T(8,128)S(1)}, f32[8,128]{1,0:T(8,128)S(1)}, u32[]{:S(2)}, u32[]{:S(2)}) collective-permute-start(f32[8,128]{1,0:T(8,128)S(1)} %get-tuple-element.60), channel_id=1, source_target_pairs={{16,32},{32,16},{48,64},{64,48},{80,96},{96,80},{17,33},{33,17},{4... | collective-permute-start | bytes 12296 | tf_op jit(solution)/shard_map/ppermute | solution.py:692
  71.2 31.9 %copy-start.3 = (s32[32]{0:T(128)S(1)}, s32[32]{0:T(128)}, u32[]{:S(2)}) copy-start(s32[32]{0:T(128)} %ids.1) | copy-start | bytes 388
  73.9 57.4 %collective-permute-start.20 = (f32[1280,128]{1,0:T(8,128)S(1)}, f32[1280,128]{1,0:T(8,128)S(1)}, u32[]{:S(2)}, u32[]{:S(2)}) collective-permute-start(f32[1280,128]{1,0:T(8,128)S(1)} %get-tuple-element.76), channel_id=1, source_target_pairs={{0,1},{1,0},{2,3},{3,2},{4,5},{5,4},{6,7},{7,6},{8,9},{9,8},{10,11... | collective-permute-start | bytes 1966088 | tf_op jit(solution)/shard_map/ppermute | solution.py:692
  74.3 57.0 %collective-permute-start.21 = (f32[1280,128]{1,0:T(8,128)S(1)}, f32[1280,128]{1,0:T(8,128)S(1)}, u32[]{:S(2)}, u32[]{:S(2)}) collective-permute-start(f32[1280,128]{1,0:T(8,128)S(1)} %get-tuple-element.77), channel_id=1, source_target_pairs={{1,2},{2,1},{3,4},{4,3},{5,6},{6,5},{7,8},{8,7},{9,10},{10,9},{11,... | collective-permute-start | bytes 1966088 | tf_op jit(solution)/shard_map/ppermute | solution.py:692
  78.5 18.1 %collective-permute-start.16 = (f32[648,128]{1,0:T(8,128)S(1)}, f32[648,128]{1,0:T(8,128)S(1)}, u32[]{:S(2)}, u32[]{:S(2)}) collective-permute-start(f32[648,128]{1,0:T(8,128)S(1)} %get-tuple-element.67), channel_id=1, source_target_pairs={{0,1},{1,0},{2,3},{3,2},{4,5},{5,4},{6,7},{7,6},{8,9},{9,8},{10,11... | collective-permute-start | bytes 995336 | tf_op jit(solution)/shard_map/ppermute | solution.py:692
  80.1 23.0 %collective-permute-start.17 = (f32[648,128]{1,0:T(8,128)S(1)}, f32[648,128]{1,0:T(8,128)S(1)}, u32[]{:S(2)}, u32[]{:S(2)}) collective-permute-start(f32[648,128]{1,0:T(8,128)S(1)} %get-tuple-element.68), channel_id=1, source_target_pairs={{1,2},{2,1},{3,4},{4,3},{5,6},{6,5},{7,8},{8,7},{9,10},{10,9},{11,... | collective-permute-start | bytes 995336 | tf_op jit(solution)/shard_map/ppermute | solution.py:692
  84.5 1.2 collective-permute-start.14
  85.7 4.9 %collective-permute-start.15 = (f32[8,128]{1,0:T(8,128)S(1)}, f32[8,128]{1,0:T(8,128)S(1)}, u32[]{:S(2)}, u32[]{:S(2)}) collective-permute-start(f32[8,128]{1,0:T(8,128)S(1)} %get-tuple-element.66), channel_id=1, source_target_pairs={{16,32},{32,16},{48,64},{64,48},{80,96},{96,80},{17,33},{33,17},{4... | collective-permute-start | bytes 12296 | tf_op jit(solution)/shard_map/ppermute | solution.py:692
  (2 other events, 17.9 us)

commit v4 on v3

--- a/solution.py
+++ b/solution.py
@@ -14,11 +14,12 @@
 FIELD = STRIPS * TILE
 STATE = 5 * TILE
 EARLY = (0, 1)
-RIDERS = (2, 3, 4, 5)
-LATE = (6, 7)
+RIDERS = ((), (2,), (3,), (4,))
+LATE = (5, 6, 7)
 GROUP = 8
 GY = 16
-BUFFERS = 4
+BUFFERS = 6
+OUT_BUFFERS = 4
 
 gravity = 9.81
 step_time = 0.25
@@ -115,7 +116,7 @@
 
 def extract_kernel(
     moves, base, depth, discharge, bed, friction, frames, out_0, out_1, early_0, early_1,
-    depth_v, flow_v, bed_v, rough_v, lo_acc, hi_acc, turned, load_sem, sem,
+    depth_v, flow_v, bed_v, rough_v, acc, turned, load_sem, sem,
 ):
     lane = iota((TILE, TILE), 1)
     groups = SLOTS // GROUP
@@ -143,29 +144,24 @@
             for k in range(STRIPS):
                 row = k if k < DEPTH else TILE - STRIPS + k
                 frames[home, strip(f, k)] = ref[pl.ds(top + row, GROUP, stride=parts * TILE), :]
-            high = hi_acc[f] if g else None
-            low = lo_acc[f] if g else None
+            half = g * GROUP * STRIPS // TILE
+            packed = acc[half, f] if g * GROUP * STRIPS % TILE else None
             for t in range(GROUP):
                 tile = ref[pl.ds(top + t * parts * TILE, TILE), :]
-                at = g * GROUP * DEPTH + DEPTH * t
+                at = (g * GROUP + t) * STRIPS % TILE
                 turn = pltpu.roll(tile, (at + DEPTH) % TILE, 1)
-                high = turn if high is None else jnp.where(lane >= at, turn, high)
-                if low is None:
-                    low = turn
-                elif at + DEPTH < TILE:
-                    low = jnp.where(lane >= at + DEPTH, turn, low)
-                else:
-                    low = jnp.where(lane < DEPTH, turn, low)
-            hi_acc[f] = high
-            lo_acc[f] = low
-
+                packed = turn if packed is None else jnp.where(lane >= at, turn, packed)
+            acc[half, f] = packed
+
+    per = TILE // STRIPS
     for f in range(5):
         to = (0, 2, 1, 3, 4)[f]
-        for half in range(2):
-            block = hi_acc[f] if half else pltpu.roll(lo_acc[f], TILE - DEPTH, 1)
-            turned[...] = block.T
-            for k in range(DEPTH):
-                frames[pl.ds(SLOTS, SLOTS), strip(to, half * DEPTH + k)] = turned[pl.ds(k, SLOTS, stride=DEPTH), :]
+        for half in range(SLOTS // per):
+            turned[half] = acc[half, f].T
+            for k in range(STRIPS):
+                frames[pl.ds(SLOTS + half * per, per), strip(to, k)] = turned[
+                    half, pl.ds((k + DEPTH) % STRIPS, per, stride=STRIPS), :
+                ]
     shape = (2 * MOVERS, SLOTS)
     pick = jnp.zeros(shape, f32)
     for m in range(MOVERS):
@@ -198,6 +194,8 @@
 
 
 def finish_chunk(entries, out_0, out_1, sem):
+    if not entries:
+        return
     body = pl.ds(0, len(entries) * STATE)
     for pairing, out in enumerate((out_0, out_1)):
         pltpu.make_async_copy(out.at[body], out.at[body], sem.at[pairing]).wait()
@@ -220,7 +218,7 @@
     moves, base, nb, frames, from_0, from_1, depth, discharge, bed, friction,
     dyn, fixed, x_0, x_1, y_0, y_1, sem,
 ):
-    ride = RIDERS[:1]
+    ride = RIDERS[0]
     start_chunk(ride, moves, base, (depth, discharge, bed, friction), y_0, y_1, sem)
     shape = (SLOTS, 2 * MOVERS)
     land = jnp.zeros(shape, f32)
@@ -266,8 +264,8 @@
                 x_0[pl.ds(f * MOVERS, MOVERS), :] = up
                 x_1[pl.ds(f * MOVERS, MOVERS), :] = down
             else:
-                y_0[pl.ds(STATE + f * MOVERS, MOVERS), :] = up
-                y_1[pl.ds(STATE + f * MOVERS, MOVERS), :] = down
+                y_0[pl.ds(len(ride) * STATE + f * MOVERS, MOVERS), :] = up
+                y_1[pl.ds(len(ride) * STATE + f * MOVERS, MOVERS), :] = down
     finish_chunk(ride, y_0, y_1, sem)
 
 
@@ -275,7 +273,9 @@
     return jnp.concatenate([x[SLOTS:], x[:SLOTS]], 0)
 
 
-def gather_halos(nb, base_ref, dyn, fixed, messages, first):
+def gather_halos(nb, base_ref, dyn, fixed, messages, turn):
+    first = turn == 0
+    riding = len(RIDERS[turn])
     last = STRIPS - 1
     out = {}
     parts = {name: [] for name in ("h_lo", "h_hi", "z_lo", "n_lo", "q_lo", "z_hi", "n_hi", "lo", "hi")}
@@ -287,7 +287,7 @@
         picks.append((lower[2], higher[2]))
 
         def message(f):
-            rows = pl.ds(axis * STATE + f * MOVERS, MOVERS)
+            rows = pl.ds(axis * riding * STATE + f * MOVERS, MOVERS)
             pair = messages[axis]
             from_higher, from_lower = swap(is_odd(base_ref, axis), pair[0][rows, :], pair[1][rows, :])
             return from_lower, from_higher
@@ -332,11 +332,11 @@
         (dyn_out, still_out, trail, x_0, x_1, y_0, y_1, late_0, late_1, sem) = rest[4:]
     else:
         (dyn_out, still_out, trail, x_0, x_1, y_0, y_1, sem) = rest[4:]
-    ride = RIDERS[turn + 1 : turn + 2]
+    ride = RIDERS[turn + 1]
     start_chunk(ride, moves, base, tiles, y_0, y_1, sem.at[0])
     if final:
         start_chunk(LATE, moves, base, tiles, late_0, late_1, sem.at[1])
-    halo, picks = gather_halos(nb, base, dyn, fixed, ((x0, x1), (y0, y1)), first)
+    halo, picks = gather_halos(nb, base, dyn, fixed, ((x0, x1), (y0, y1)), turn)
     names = ("z_lo", "n_lo", "z_hi", "n_hi", "q_lo")
     if not first:
         for j, name in enumerate(names):
@@ -404,8 +404,8 @@
             x_0[...] = up
             x_1[...] = down
         else:
-            y_0[pl.ds(STATE, MOVERS), :] = up
-            y_1[pl.ds(STATE, MOVERS), :] = down
+            y_0[pl.ds(len(ride) * STATE, MOVERS), :] = up
+            y_1[pl.ds(len(ride) * STATE, MOVERS), :] = down
     finish_chunk(ride, y_0, y_1, sem.at[0])
     if final:
         finish_chunk(LATE, late_0, late_1, sem.at[1])
@@ -413,7 +413,7 @@
 
 def run_tiles(
     queue, origin, count, moves_sources, tiles, nb_s, edges, columns, outs, before_loop,
-    inbox, outbox, water, stream_x, stream_y, slope_x, slope_y, rub_x, rub_y, in_sem, out_sem,
+    inbox, outbox, in_sem, out_sem, *spaces,
 ):
     depth, discharge, bed, friction = tiles
     depth_out, flow_out = outs
@@ -458,7 +458,7 @@
         pltpu.make_async_copy(box, box, out_sem.at[buf]).wait()
 
     def prime():
-        for j in range(BUFFERS - 1):
+        for j in range(BUFFERS - 2):
 
             @pl.when(j < count)
             def _():
@@ -474,27 +474,25 @@
     at_last = lane == TILE - 1
     bottom = row == part_rows - 1
 
-    def one_tile(j, carry):
-        t = queue[j]
-        buf = j % BUFFERS
-
-        @pl.when(j + BUFFERS - 1 < count)
+    def ready(j):
+        @pl.when(j < count)
         def _():
-            fetch(j + BUFFERS - 1)
-
-        arrived(buf)
-
-        @pl.when(j >= BUFFERS)
+            arrived(j % BUFFERS)
+
+        @pl.when((j >= OUT_BUFFERS) & (j < count))
         def _():
-            sent(buf)
-
-        box = inbox.at[buf]
-        out = outbox.at[buf]
+            sent(j % OUT_BUFFERS)
+
+    def work(j, space):
+        water, stream_x, stream_y, slope_x, slope_y, rub_x, rub_y = space
+        t = queue[jnp.minimum(j, count - 1)]
+        box = inbox.at[j % BUFFERS]
+        out = outbox.at[j % OUT_BUFFERS]
         wall_x = nb_s[1, t] < 0
         wall_y = nb_s[3, t] < 0
 
-        def edge_row(j):
-            return edges[j, pl.ds(t, 1), :]
+        def edge_row(e):
+            return edges[e, pl.ds(t, 1), :]
 
         z_next = edge_row(8)
         n_next = edge_row(9)
@@ -551,11 +549,30 @@
                     water[rows, :] = h_new
                 else:
                     out[rows, :] = h_new * UNIT_H
-        send(t, buf)
+
+    def two_tiles(pair, carry):
+        for i in range(2):
+            j = 2 * pair + i
+
+            @pl.when(j + BUFFERS - 2 < count)
+            def _():
+                fetch(j + BUFFERS - 2)
+
+            ready(j)
+        half = len(spaces) // 2
+        for i in range(2):
+            work(2 * pair + i, spaces[i * half : (i + 1) * half])
+        for i in range(2):
+            j = 2 * pair + i
+
+            @pl.when(j < count)
+            def _():
+                send(queue[j], j % OUT_BUFFERS)
+
         return carry
 
-    lax.fori_loop(0, count, one_tile, 0)
-    for b in range(BUFFERS):
+    lax.fori_loop(0, (count + 1) // 2, two_tiles, 0)
+    for b in range(OUT_BUFFERS):
 
         @pl.when(b < count)
         def _():
@@ -582,7 +599,7 @@
 
 def tile_kernel(
     moves, base, ids, nb_s, nb, dyn, fixed, still, x_0, x_1, l3, u3, t0, t1, t2,
-    l0, l1, l2, u0, u1, u2, early_0, early_1, depth, discharge, bed, friction,
+    l1, l2, u1, u2, early_0, early_1, depth, discharge, bed, friction,
     depth_out, flow_out, edges, columns,
     zeros, turned, queue, origin, zero_sem, *scratch,
 ):
@@ -595,7 +612,7 @@
     def mark(t, code):
         origin[t] = code
 
-    note_arrivals(EARLY + RIDERS, moves, base, mark)
+    note_arrivals(EARLY + RIDERS[1] + RIDERS[2] + RIDERS[3], moves, base, mark)
     note_arrivals(LATE, moves, base, lambda t, code: mark(t, -1))
 
     def enqueue(t, size):
@@ -615,7 +632,7 @@
 
     def before_loop():
         lax.fori_loop(live, SLOTS, blank, 0)
-        halo, _ = gather_halos(nb, base, dyn, fixed, ((x_0, x_1), (l3, u3)), False)
+        halo, _ = gather_halos(nb, base, dyn, fixed, ((x_0, x_1), (l3, u3)), 3)
 
         def kept(j):
             return still[:, pl.ds(j * TILE, TILE)]
@@ -645,8 +662,8 @@
         columns[2] = turned[...].T
 
     sources = chunk_sources(EARLY, early_0, early_1)
-    for m, chunk_0, chunk_1 in zip(RIDERS, (l0, l1, l2, l3), (u0, u1, u2, u3)):
-        sources += chunk_sources((m,), chunk_0, chunk_1)
+    for entries, chunk_0, chunk_1 in zip(RIDERS[1:], (l1, l2, l3), (u1, u2, u3)):
+        sources += chunk_sources(entries, chunk_0, chunk_1)
     run_tiles(
         queue, origin, count, sources, (depth, discharge, bed, friction), nb_s, edges, columns,
         (depth_out, flow_out), before_loop, *scratch,
@@ -721,18 +738,18 @@
 
 
 def loop_scratch():
+    space = [
+        pltpu.VMEM((TILE + 8, TILE), f32),
+        pltpu.VMEM((TILE + 8, TILE), f32),
+        *[pltpu.VMEM((TILE, TILE), f32)] * 5,
+    ]
     return [
         pltpu.VMEM((BUFFERS, STATE, TILE), f32),
-        pltpu.VMEM((BUFFERS, 3 * TILE, TILE), f32),
-        pltpu.VMEM((TILE + 8, TILE), f32),
-        pltpu.VMEM((TILE + 8, TILE), f32),
-        pltpu.VMEM((TILE, TILE), f32),
-        pltpu.VMEM((TILE, TILE), f32),
-        pltpu.VMEM((TILE, TILE), f32),
-        pltpu.VMEM((TILE, TILE), f32),
-        pltpu.VMEM((TILE, TILE), f32),
+        pltpu.VMEM((OUT_BUFFERS, 3 * TILE, TILE), f32),
         pltpu.SemaphoreType.DMA((BUFFERS,)),
-        pltpu.SemaphoreType.DMA((BUFFERS,)),
+        pltpu.SemaphoreType.DMA((OUT_BUFFERS,)),
+        *space,
+        *space,
     ]
 
 
@@ -766,9 +783,8 @@
             pltpu.VMEM((SLOTS * 2 * TILE, TILE), f32),
             pltpu.VMEM((SLOTS * TILE, TILE), f32),
             pltpu.VMEM((SLOTS * TILE, TILE), f32),
-            pltpu.VMEM((5, TILE, TILE), f32),
-            pltpu.VMEM((5, TILE, TILE), f32),
-            pltpu.VMEM((TILE, TILE), f32),
+            pltpu.VMEM((2, 5, TILE, TILE), f32),
+            pltpu.VMEM((2, TILE, TILE), f32),
             pltpu.SemaphoreType.DMA((SLOTS // GROUP, 4)),
             pltpu.SemaphoreType.DMA((2,)),
         ],
@@ -788,8 +804,8 @@
             held(2 * SLOTS, 2 * FIELD),
             held(first_rows, TILE),
             held(first_rows, TILE),
-            held(STATE + first_rows, TILE),
-            held(STATE + first_rows, TILE),
+            held(len(RIDERS[0]) * STATE + first_rows, TILE),
+            held(len(RIDERS[0]) * STATE + first_rows, TILE),
         ],
         scratch_shapes=[pltpu.SemaphoreType.DMA((2,))],
         compiler_params=pltpu.CompilerParams(vmem_limit_bytes=12 * 2**20),
@@ -811,8 +827,8 @@
             (2 * SLOTS, 2 * TILE),
             (MOVERS, TILE),
             (MOVERS, TILE),
-            (STATE + MOVERS, TILE),
-            (STATE + MOVERS, TILE),
+            (len(RIDERS[turn + 1]) * STATE + MOVERS, TILE),
+            (len(RIDERS[turn + 1]) * STATE + MOVERS, TILE),
         ]
         if turn == 2:
             shapes += [(len(LATE) * STATE, TILE)] * 2
@@ -833,7 +849,7 @@
 
     late_0, late_1 = trade_both(*late, "gy")
     kept_inputs = on_core(
-        nb, dyn, fixed, *still, *got, *trails, *lows[:3], *highs[:3], early_0, early_1
+        nb, dyn, fixed, *still, *got, *trails, *lows[1:3], *highs[1:3], early_0, early_1
     )
     new_depth, new_flow, edges, columns = call(
         tile_kernel,

time: 137 us -> 149 us (1.088)
  the two profiles are of different devices: /device:TPU:100 before, /device:TPU:39 now
where the time goes in v4:
time: 149 us; the launch traced here: 148 us
  starting transfers between devices  55.3 us (37%)
  waiting for transfers between devices  46.2 us (31%)
  Pallas kernels  45.2 us (30%)
    ppermute x22, starting transfers between devices, trade(): return lax.ppermute(block, axis, pairs)  55.3 us
    ppermute x22, waiting for transfers between devices, trade(): return lax.ppermute(block, axis, pairs)  46.2 us
    pallas_call x1, Pallas kernels, shards(): call(tile_kernel, in_specs=[SMEM] * 4 + [VMEM] * len(kept_inputs) + [HBM]...  22.4 us
    pallas_call x3, Pallas kernels, shards(): call(body, in_specs=[SMEM, SMEM] + [VMEM] * (7 + len(still)) + [HBM] * 4,...  8.55 us
    pallas_call x1, Pallas kernels, shards(): pl.pallas_call(extract_kernel, in_specs=[SMEM, SMEM] + [HBM] * 4, out_spe...  6.8 us
    pallas_call x1, Pallas kernels, shards(): pl.pallas_call(late_kernel, in_specs=[SMEM] * 3 + [VMEM] * 4 + [HBM] * 2,...  6.04 us
  transfers between devices with their start and end apart: 22, of which 10 were waited for; matrix products, arithmetic and copies ran while one was open for 0% of the time, Pallas kernels for 17%

profile of v4, /device:TPU:39, one launch (start us, length us, event | category | flops | bytes accessed | tf_op | source)
XLA Modules:
  0.0 148.5 jit_solution(3876788885798457961)
XLA Ops:
  1.3 6.8 %extract.1 = (f32[64,5120]{1,0:T(8,128)S(1)}, f32[8,10240]{1,0:T(8,128)S(1)}, f32[8,10240]{1,0:T(8,128)S(1)}, f32[1280,128]{1,0:T(8,128)S(1)}, f32[1280,128]{1,0:T(8,128)S(1)}) custom-call(s32[2,2,8]{2,1,0:T(2,128)S(1)} %bitcast.11, s32[1]{0:T(128)} %bitcast.2.base.refs_1_, f32[4096,128]{1,0:T(8,128)} %bitcast.31, f32[8192,128]{1,0:T(8,128)} %bitcast.25, ...), custom_call_target="tpu_custom_call" | custom-call | tf_op jit(solution)/shard_map/extract/pallas_call | solution.py:770
  9.1 4.9 %collective-permute-start.1 = (f32[8,10240]{1,0:T(8,128)S(1)}, f32[8,10240]{1,0:T(8,128)S(1)}, u32[]{:S(2)}, u32[]{:S(2)}) collective-permute-start(f32[8,10240]{1,0:T(8,128)S(1)} %get-tuple-element.44), channel_id=1, source_target_pairs={{1,2},{2,1},{3,4},{4,3},{5,6},{6,5},{7,8},{8,7},{9,10},{10,9},{11,... | collective-permute-start | bytes 983048 | tf_op jit(solution)/shard_map/ppermute | solution.py:709
  14.1 2.5 %collective-permute-done.from_0 = f32[8,10240]{1,0:T(8,128)S(1)} collective-permute-done((f32[8,10240]{1,0:T(8,128)S(1)}, f32[8,10240]{1,0:T(8,128)S(1)}, u32[]{:S(2)}, u32[]{:S(2)}) %collective-permute-start) | collective-permute-done | bytes 327712 | tf_op jit(solution)/shard_map/ppermute | solution.py:709
  16.5 4.5 %collective-permute-done.1.from_1 = f32[8,10240]{1,0:T(8,128)S(1)} collective-permute-done((f32[8,10240]{1,0:T(8,128)S(1)}, f32[8,10240]{1,0:T(8,128)S(1)}, u32[]{:S(2)}, u32[]{:S(2)}) %collective-permute-start.1) | collective-permute-done | bytes 327712 | tf_op jit(solution)/shard_map/ppermute | solution.py:709
  22.5 2.3 %collective-permute-start.2 = (f32[32,128]{1,0:T(8,128)S(1)}, f32[32,128]{1,0:T(8,128)S(1)}, u32[]{:S(2)}, u32[]{:S(2)}) collective-permute-start(f32[32,128]{1,0:T(8,128)S(1)} %get-tuple-element.47), channel_id=1, source_target_pairs={{0,16},{16,0},{32,48},{48,32},{64,80},{80,64},{96,112},{112,96},{1... | collective-permute-start | bytes 49160 | tf_op jit(solution)/shard_map/ppermute | solution.py:709
  24.8 3.5 %collective-permute-start.3 = (f32[32,128]{1,0:T(8,128)S(1)}, f32[32,128]{1,0:T(8,128)S(1)}, u32[]{:S(2)}, u32[]{:S(2)}) collective-permute-start(f32[32,128]{1,0:T(8,128)S(1)} %get-tuple-element.48), channel_id=1, source_target_pairs={{16,32},{32,16},{48,64},{64,48},{80,96},{96,80},{17,33},{33,17},{4... | collective-permute-start | bytes 49160 | tf_op jit(solution)/shard_map/ppermute | solution.py:709
  28.4 4.7 %collective-permute-start.5 = (f32[32,128]{1,0:T(8,128)S(1)}, f32[32,128]{1,0:T(8,128)S(1)}, u32[]{:S(2)}, u32[]{:S(2)}) collective-permute-start(f32[32,128]{1,0:T(8,128)S(1)} %get-tuple-element.50), channel_id=1, source_target_pairs={{1,2},{2,1},{3,4},{4,3},{5,6},{6,5},{7,8},{8,7},{9,10},{10,9},{11,... | collective-permute-start | bytes 49160 | tf_op jit(solution)/shard_map/ppermute | solution.py:709
  33.1 2.0 %collective-permute-done.5.refs_8_ = f32[32,128]{1,0:T(8,128)S(1)} collective-permute-done((f32[32,128]{1,0:T(8,128)S(1)}, f32[32,128]{1,0:T(8,128)S(1)}, u32[]{:S(2)}, u32[]{:S(2)}) %collective-permute-start.5) | collective-permute-done | bytes 16416 | tf_op jit(solution)/shard_map/ppermute | solution.py:709
  35.0 2.6 %shard_map.87 = (f32[64,3072]{1,0:T(8,128)S(1)}, f32[64,640]{1,0:T(8,128)S(1)}, f32[64,256]{1,0:T(8,128)S(1)}, f32[8,128]{1,0:T(8,128)S(1)}, f32[8,128]{1,0:T(8,...) custom-call(s32[2,2,8]{2,1,0:T(2,128)S(1)} %bitcast.13, s32[1]{0:T(128)} %bitcast.2.base.refs_1_, ...), custom_call_target="tpu_custom_call" | custom-call | tf_op jit(solution)/shard_map/pallas_call | solution.py:835
  37.8 4.6 %collective-permute-start.9 = (f32[648,128]{1,0:T(8,128)S(1)}, f32[648,128]{1,0:T(8,128)S(1)}, u32[]{:S(2)}, u32[]{:S(2)}) collective-permute-start(f32[648,128]{1,0:T(8,128)S(1)} %get-tuple-element.56), channel_id=1, source_target_pairs={{1,2},{2,1},{3,4},{4,3},{5,6},{6,5},{7,8},{8,7},{9,10},{10,9},{11,... | collective-permute-start | bytes 995336 | tf_op jit(solution)/shard_map/ppermute | solution.py:709
  42.6 3.8 %collective-permute-start.7 = (f32[8,128]{1,0:T(8,128)S(1)}, f32[8,128]{1,0:T(8,128)S(1)}, u32[]{:S(2)}, u32[]{:S(2)}) collective-permute-start(f32[8,128]{1,0:T(8,128)S(1)} %get-tuple-element.54), channel_id=1, source_target_pairs={{16,32},{32,16},{48,64},{64,48},{80,96},{96,80},{17,33},{33,17},{4... | collective-permute-start | bytes 12296 | tf_op jit(solution)/shard_map/ppermute | solution.py:709
  48.0 2.8 %collective-permute-done.9.refs_9_.u1 = f32[648,128]{1,0:T(8,128)S(1)} collective-permute-done((f32[648,128]{1,0:T(8,128)S(1)}, f32[648,128]{1,0:T(8,128)S(1)}, u32[]{:S(2)}, u32[]{:S(2)}) %collective-permute-start.9) | collective-permute-done | bytes 331808 | tf_op jit(solution)/shard_map/ppermute | solution.py:709
  50.7 2.4 %shard_map.88 = (f32[64,3072]{1,0:T(8,128)S(1)}, f32[64,640]{1,0:T(8,128)S(1)}, f32[64,256]{1,0:T(8,128)S(1)}, f32[8,128]{1,0:T(8,128)S(1)}, f32[8,128]{1,0:T(8,...) custom-call(s32[2,2,8]{2,1,0:T(2,128)S(1)} %bitcast.14, s32[1]{0:T(128)} %bitcast.2.base.refs_1_, ...), custom_call_target="tpu_custom_call" | custom-call | tf_op jit(solution)/shard_map/pallas_call | solution.py:835
  53.2 5.1 %collective-permute-start.13 = (f32[648,128]{1,0:T(8,128)S(1)}, f32[648,128]{1,0:T(8,128)S(1)}, u32[]{:S(2)}, u32[]{:S(2)}) collective-permute-start(f32[648,128]{1,0:T(8,128)S(1)} %get-tuple-element.62), channel_id=1, source_target_pairs={{1,2},{2,1},{3,4},{4,3},{5,6},{6,5},{7,8},{8,7},{9,10},{10,9},{11,... | collective-permute-start | bytes 995336 | tf_op jit(solution)/shard_map/ppermute | solution.py:709
  59.5 3.3 %collective-permute-start.11 = (f32[8,128]{1,0:T(8,128)S(1)}, f32[8,128]{1,0:T(8,128)S(1)}, u32[]{:S(2)}, u32[]{:S(2)}) collective-permute-start(f32[8,128]{1,0:T(8,128)S(1)} %get-tuple-element.60), channel_id=1, source_target_pairs={{16,32},{32,16},{48,64},{64,48},{80,96},{96,80},{17,33},{33,17},{4... | collective-permute-start | bytes 12296 | tf_op jit(solution)/shard_map/ppermute | solution.py:709
  65.4 3.5 %shard_map.89 = (f32[64,3072]{1,0:T(8,128)S(1)}, f32[64,640]{1,0:T(8,128)S(1)}, f32[64,256]{1,0:T(8,128)S(1)}, f32[8,128]{1,0:T(8,128)S(1)}, f32[8,128]{1,0:T(8,...) custom-call(s32[2,2,8]{2,1,0:T(2,128)S(1)} %bitcast.15, ...), custom_call_target="tpu_custom_call" | custom-call | tf_op jit(solution)/shard_map/pallas_call | solution.py:835
  69.4 4.5 %collective-permute-start.21 = (f32[1920,128]{1,0:T(8,128)S(1)}, f32[1920,128]{1,0:T(8,128)S(1)}, u32[]{:S(2)}, u32[]{:S(2)}) collective-permute-start(f32[1920,128]{1,0:T(8,128)S(1)} %get-tuple-element.77), channel_id=1, source_target_pairs={{1,2},{2,1},{3,4},{4,3},{5,6},{6,5},{7,8},{8,7},{9,10},{10,9},{11,... | collective-permute-start | bytes 2949128 | tf_op jit(solution)/shard_map/ppermute | solution.py:709
  74.0 2.9 %collective-permute-start.19 = (f32[1280,128]{1,0:T(8,128)S(1)}, f32[1280,128]{1,0:T(8,128)S(1)}, u32[]{:S(2)}, u32[]{:S(2)}) collective-permute-start(f32[1280,128]{1,0:T(8,128)S(1)} %get-tuple-element.73), channel_id=1, source_target_pairs={{1,2},{2,1},{3,4},{4,3},{5,6},{6,5},{7,8},{8,7},{9,10},{10,9},{11,... | collective-permute-start | bytes 1966088 | tf_op jit(solution)/shard_map/ppermute | solution.py:709
  76.9 4.5 %collective-permute-start.17 = (f32[648,128]{1,0:T(8,128)S(1)}, f32[648,128]{1,0:T(8,128)S(1)}, u32[]{:S(2)}, u32[]{:S(2)}) collective-permute-start(f32[648,128]{1,0:T(8,128)S(1)} %get-tuple-element.68), channel_id=1, source_target_pairs={{1,2},{2,1},{3,4},{4,3},{5,6},{6,5},{7,8},{8,7},{9,10},{10,9},{11,... | collective-permute-start | bytes 995336 | tf_op jit(solution)/shard_map/ppermute | solution.py:709
  81.5 28.2 %collective-permute-done.19.early_1 = f32[1280,128]{1,0:T(8,128)S(1)} collective-permute-done((f32[1280,128]{1,0:T(8,128)S(1)}, f32[1280,128]{1,0:T(8,128)S(1)}, u32[]{:S(2)}, u32[]{:S(2)}) %collective-permute-start.19) | collective-permute-done | bytes 655392 | tf_op jit(solution)/shard_map/ppermute | solution.py:709
  109.7 3.4 %collective-permute-start.14 = (f32[8,128]{1,0:T(8,128)S(1)}, f32[8,128]{1,0:T(8,128)S(1)}, u32[]{:S(2)}, u32[]{:S(2)}) collective-permute-start(f32[8,128]{1,0:T(8,128)S(1)} %get-tuple-element.65), channel_id=1, source_target_pairs={{0,16},{16,0},{32,48},{48,32},{64,80},{80,64},{96,112},{112,96},{1... | collective-permute-start | bytes 12296 | tf_op jit(solution)/shard_map/ppermute | solution.py:709
  114.0 4.6 %collective-permute-start.15 = (f32[8,128]{1,0:T(8,128)S(1)}, f32[8,128]{1,0:T(8,128)S(1)}, u32[]{:S(2)}, u32[]{:S(2)}) collective-permute-start(f32[8,128]{1,0:T(8,128)S(1)} %get-tuple-element.66), channel_id=1, source_target_pairs={{16,32},{32,16},{48,64},{64,48},{80,96},{96,80},{17,33},{33,17},{4... | collective-permute-start | bytes 12296 | tf_op jit(solution)/shard_map/ppermute | solution.py:709
  119.9 22.4 %shard_map.90 = (f32[4096,128]{1,0:T(8,128)}, f32[8192,128]{1,0:T(8,128)}, f32[10,32,128]{2,1,0:T(8,128)S(1)}, f32[3,128,128]{2,1,0:T(8,128)S(1)}) custom-call(s32[2,2,8]{2,1,0:T(2,128)S(1)} %bitcast.16, s32[1]{0:T(128)} %bitcast.2.base.refs_1_, s32[32]{0:T(128)S(1)} %copy-done.3, s32[4,32]{1,0:T(4,128)S(1)} %bitcast.22, s32[4,32]{1,0:T(4,128)S(1)} %bitcast.23, ...), custom_call_target="tpu_custom_call" | custom-call | tf_op jit(solution)/shard_map/pallas_call | solution.py:854
  142.3 6.0 %late_tiles.1 = (f32[4096,128]{1,0:T(8,128)}, f32[8192,128]{1,0:T(8,128)}) custom-call(s32[2,2,8]{2,1,0:T(2,128)S(1)} %bitcast.17, s32[1]{0:T(128)} %bitcast.2.base.refs_1_, s32[4,32]{1,0:T(4,128)S(1)} %bitcast.24, f32[10,32,128]{2,1,0:T(8,128)S(1)} %get-tuple-element.74.edges, ...), custom_call_target="tpu_custom_call", output_to_operand_aliasing={{0}: (7, {}), {1}: (8, {})} | custom-call | tf_op jit(solution)/shard_map/late_tiles/pallas_call | solution.py:874
  (35 shorter events, 11.7 us)
Async XLA Ops:
  8.1 8.4 %collective-permute-start = (f32[8,10240]{1,0:T(8,128)S(1)}, f32[8,10240]{1,0:T(8,128)S(1)}, u32[]{:S(2)}, u32[]{:S(2)}) collective-permute-start(f32[8,10240]{1,0:T(8,128)S(1)} %get-tuple-element.43), channel_id=1, source_target_pairs={{0,1},{1,0},{2,3},{3,2},{4,5},{5,4},{6,7},{7,6},{8,9},{9,8},{10,11... | collective-permute-start | bytes 983048 | tf_op jit(solution)/shard_map/ppermute | solution.py:709
  9.1 11.9 %collective-permute-start.1 = (f32[8,10240]{1,0:T(8,128)S(1)}, f32[8,10240]{1,0:T(8,128)S(1)}, u32[]{:S(2)}, u32[]{:S(2)}) collective-permute-start(f32[8,10240]{1,0:T(8,128)S(1)} %get-tuple-element.44), channel_id=1, source_target_pairs={{1,2},{2,1},{3,4},{4,3},{5,6},{6,5},{7,8},{8,7},{9,10},{10,9},{11,... | collective-permute-start | bytes 983048 | tf_op jit(solution)/shard_map/ppermute | solution.py:709
  22.5 10.6 %collective-permute-start.2 = (f32[32,128]{1,0:T(8,128)S(1)}, f32[32,128]{1,0:T(8,128)S(1)}, u32[]{:S(2)}, u32[]{:S(2)}) collective-permute-start(f32[32,128]{1,0:T(8,128)S(1)} %get-tuple-element.47), channel_id=1, source_target_pairs={{0,16},{16,0},{32,48},{48,32},{64,80},{80,64},{96,112},{112,96},{1... | collective-permute-start | bytes 49160 | tf_op jit(solution)/shard_map/ppermute | solution.py:709
  24.8 8.3 %collective-permute-start.3 = (f32[32,128]{1,0:T(8,128)S(1)}, f32[32,128]{1,0:T(8,128)S(1)}, u32[]{:S(2)}, u32[]{:S(2)}) collective-permute-start(f32[32,128]{1,0:T(8,128)S(1)} %get-tuple-element.48), channel_id=1, source_target_pairs={{16,32},{32,16},{48,64},{64,48},{80,96},{96,80},{17,33},{33,17},{4... | collective-permute-start | bytes 49160 | tf_op jit(solution)/shard_map/ppermute | solution.py:709
  28.3 4.8 %collective-permute-start.4 = (f32[32,128]{1,0:T(8,128)S(1)}, f32[32,128]{1,0:T(8,128)S(1)}, u32[]{:S(2)}, u32[]{:S(2)}) collective-permute-start(f32[32,128]{1,0:T(8,128)S(1)} %get-tuple-element.49), channel_id=1, source_target_pairs={{0,1},{1,0},{2,3},{3,2},{4,5},{5,4},{6,7},{7,6},{8,9},{9,8},{10,11... | collective-permute-start | bytes 49160 | tf_op jit(solution)/shard_map/ppermute | solution.py:709
  28.4 6.7 %collective-permute-start.5 = (f32[32,128]{1,0:T(8,128)S(1)}, f32[32,128]{1,0:T(8,128)S(1)}, u32[]{:S(2)}, u32[]{:S(2)}) collective-permute-start(f32[32,128]{1,0:T(8,128)S(1)} %get-tuple-element.50), channel_id=1, source_target_pairs={{1,2},{2,1},{3,4},{4,3},{5,6},{6,5},{7,8},{8,7},{9,10},{10,9},{11,... | collective-permute-start | bytes 49160 | tf_op jit(solution)/shard_map/ppermute | solution.py:709
  37.7 10.3 %collective-permute-start.8 = (f32[648,128]{1,0:T(8,128)S(1)}, f32[648,128]{1,0:T(8,128)S(1)}, u32[]{:S(2)}, u32[]{:S(2)}) collective-permute-start(f32[648,128]{1,0:T(8,128)S(1)} %get-tuple-element.55), channel_id=1, source_target_pairs={{0,1},{1,0},{2,3},{3,2},{4,5},{5,4},{6,7},{7,6},{8,9},{9,8},{10,11... | collective-permute-start | bytes 995336 | tf_op jit(solution)/shard_map/ppermute | solution.py:709
  37.8 13.0 %collective-permute-start.9 = (f32[648,128]{1,0:T(8,128)S(1)}, f32[648,128]{1,0:T(8,128)S(1)}, u32[]{:S(2)}, u32[]{:S(2)}) collective-permute-start(f32[648,128]{1,0:T(8,128)S(1)} %get-tuple-element.56), channel_id=1, source_target_pairs={{1,2},{2,1},{3,4},{4,3},{5,6},{6,5},{7,8},{8,7},{9,10},{10,9},{11,... | collective-permute-start | bytes 995336 | tf_op jit(solution)/shard_map/ppermute | solution.py:709
  42.4 4.0 %collective-permute-start.6 = (f32[8,128]{1,0:T(8,128)S(1)}, f32[8,128]{1,0:T(8,128)S(1)}, u32[]{:S(2)}, u32[]{:S(2)}) collective-permute-start(f32[8,128]{1,0:T(8,128)S(1)} %get-tuple-element.53), channel_id=1, source_target_pairs={{0,16},{16,0},{32,48},{48,32},{64,80},{80,64},{96,112},{112,96},{1... | collective-permute-start | bytes 12296 | tf_op jit(solution)/shard_map/ppermute | solution.py:709
  42.6 5.3 %collective-permute-start.7 = (f32[8,128]{1,0:T(8,128)S(1)}, f32[8,128]{1,0:T(8,128)S(1)}, u32[]{:S(2)}, u32[]{:S(2)}) collective-permute-start(f32[8,128]{1,0:T(8,128)S(1)} %get-tuple-element.54), channel_id=1, source_target_pairs={{16,32},{32,16},{48,64},{64,48},{80,96},{96,80},{17,33},{33,17},{4... | collective-permute-start | bytes 12296 | tf_op jit(solution)/shard_map/ppermute | solution.py:709
  53.1 11.6 %collective-permute-start.12 = (f32[648,128]{1,0:T(8,128)S(1)}, f32[648,128]{1,0:T(8,128)S(1)}, u32[]{:S(2)}, u32[]{:S(2)}) collective-permute-start(f32[648,128]{1,0:T(8,128)S(1)} %get-tuple-element.61), channel_id=1, source_target_pairs={{0,1},{1,0},{2,3},{3,2},{4,5},{5,4},{6,7},{7,6},{8,9},{9,8},{10,11... | collective-permute-start | bytes 995336 | tf_op jit(solution)/shard_map/ppermute | solution.py:709
  53.2 12.1 %collective-permute-start.13 = (f32[648,128]{1,0:T(8,128)S(1)}, f32[648,128]{1,0:T(8,128)S(1)}, u32[]{:S(2)}, u32[]{:S(2)}) collective-permute-start(f32[648,128]{1,0:T(8,128)S(1)} %get-tuple-element.62), channel_id=1, source_target_pairs={{1,2},{2,1},{3,4},{4,3},{5,6},{6,5},{7,8},{8,7},{9,10},{10,9},{11,... | collective-permute-start | bytes 995336 | tf_op jit(solution)/shard_map/ppermute | solution.py:709
  58.3 18.6 %collective-permute-start.18 = (f32[1280,128]{1,0:T(8,128)S(1)}, f32[1280,128]{1,0:T(8,128)S(1)}, u32[]{:S(2)}, u32[]{:S(2)}) collective-permute-start(f32[1280,128]{1,0:T(8,128)S(1)} %get-tuple-element.72), channel_id=1, source_target_pairs={{0,1},{1,0},{2,3},{3,2},{4,5},{5,4},{6,7},{7,6},{8,9},{9,8},{10,11... | collective-permute-start | bytes 1966088 | tf_op jit(solution)/shard_map/ppermute | solution.py:709
  58.4 4.4 %collective-permute-start.10 = (f32[8,128]{1,0:T(8,128)S(1)}, f32[8,128]{1,0:T(8,128)S(1)}, u32[]{:S(2)}, u32[]{:S(2)}) collective-permute-start(f32[8,128]{1,0:T(8,128)S(1)} %get-tuple-element.59), channel_id=1, source_target_pairs={{0,16},{16,0},{32,48},{48,32},{64,80},{80,64},{96,112},{112,96},{1... | collective-permute-start | bytes 12296 | tf_op jit(solution)/shard_map/ppermute | solution.py:709
  59.5 5.2 %collective-permute-start.11 = (f32[8,128]{1,0:T(8,128)S(1)}, f32[8,128]{1,0:T(8,128)S(1)}, u32[]{:S(2)}, u32[]{:S(2)}) collective-permute-start(f32[8,128]{1,0:T(8,128)S(1)} %get-tuple-element.60), channel_id=1, source_target_pairs={{16,32},{32,16},{48,64},{64,48},{80,96},{96,80},{17,33},{33,17},{4... | collective-permute-start | bytes 12296 | tf_op jit(solution)/shard_map/ppermute | solution.py:709
  65.4 54.5 %copy-start.1 = (s32[1,2,8,2]{2,3,1,0:T(2,128)S(1)}, s32[1,2,8,2]{2,3,1,0:T(2,128)}, u32[]{:S(2)}) copy-start(s32[1,2,8,2]{2,3,1,0:T(2,128)} %param.13) | copy-start | bytes 388
  65.4 54.5 %copy-start.3 = (s32[32]{0:T(128)S(1)}, s32[32]{0:T(128)}, u32[]{:S(2)}) copy-start(s32[32]{0:T(128)} %ids.1) | copy-start | bytes 388
  68.9 73.4 %collective-permute-start.20 = (f32[1920,128]{1,0:T(8,128)S(1)}, f32[1920,128]{1,0:T(8,128)S(1)}, u32[]{:S(2)}, u32[]{:S(2)}) collective-permute-start(f32[1920,128]{1,0:T(8,128)S(1)} %get-tuple-element.76), channel_id=1, source_target_pairs={{0,1},{1,0},{2,3},{3,2},{4,5},{5,4},{6,7},{7,6},{8,9},{9,8},{10,11... | collective-permute-start | bytes 2949128 | tf_op jit(solution)/shard_map/ppermute | solution.py:709
  69.4 72.8 %collective-permute-start.21 = (f32[1920,128]{1,0:T(8,128)S(1)}, f32[1920,128]{1,0:T(8,128)S(1)}, u32[]{:S(2)}, u32[]{:S(2)}) collective-permute-start(f32[1920,128]{1,0:T(8,128)S(1)} %get-tuple-element.77), channel_id=1, source_target_pairs={{1,2},{2,1},{3,4},{4,3},{5,6},{6,5},{7,8},{8,7},{9,10},{10,9},{11,... | collective-permute-start | bytes 2949128 | tf_op jit(solution)/shard_map/ppermute | solution.py:709
  74.0 35.8 %collective-permute-start.19 = (f32[1280,128]{1,0:T(8,128)S(1)}, f32[1280,128]{1,0:T(8,128)S(1)}, u32[]{:S(2)}, u32[]{:S(2)}) collective-permute-start(f32[1280,128]{1,0:T(8,128)S(1)} %get-tuple-element.73), channel_id=1, source_target_pairs={{1,2},{2,1},{3,4},{4,3},{5,6},{6,5},{7,8},{8,7},{9,10},{10,9},{11,... | collective-permute-start | bytes 1966088 | tf_op jit(solution)/shard_map/ppermute | solution.py:709
  76.8 43.0 %collective-permute-start.16 = (f32[648,128]{1,0:T(8,128)S(1)}, f32[648,128]{1,0:T(8,128)S(1)}, u32[]{:S(2)}, u32[]{:S(2)}) collective-permute-start(f32[648,128]{1,0:T(8,128)S(1)} %get-tuple-element.67), channel_id=1, source_target_pairs={{0,1},{1,0},{2,3},{3,2},{4,5},{5,4},{6,7},{7,6},{8,9},{9,8},{10,11... | collective-permute-start | bytes 995336 | tf_op jit(solution)/shard_map/ppermute | solution.py:709
  76.9 42.9 %collective-permute-start.17 = (f32[648,128]{1,0:T(8,128)S(1)}, f32[648,128]{1,0:T(8,128)S(1)}, u32[]{:S(2)}, u32[]{:S(2)}) collective-permute-start(f32[648,128]{1,0:T(8,128)S(1)} %get-tuple-element.68), channel_id=1, source_target_pairs={{1,2},{2,1},{3,4},{4,3},{5,6},{6,5},{7,8},{8,7},{9,10},{10,9},{11,... | collective-permute-start | bytes 995336 | tf_op jit(solution)/shard_map/ppermute | solution.py:709
  109.7 4.3 %collective-permute-start.14 = (f32[8,128]{1,0:T(8,128)S(1)}, f32[8,128]{1,0:T(8,128)S(1)}, u32[]{:S(2)}, u32[]{:S(2)}) collective-permute-start(f32[8,128]{1,0:T(8,128)S(1)} %get-tuple-element.65), channel_id=1, source_target_pairs={{0,16},{16,0},{32,48},{48,32},{64,80},{80,64},{96,112},{112,96},{1... | collective-permute-start | bytes 12296 | tf_op jit(solution)/shard_map/ppermute | solution.py:709
  114.0 5.9 %collective-permute-start.15 = (f32[8,128]{1,0:T(8,128)S(1)}, f32[8,128]{1,0:T(8,128)S(1)}, u32[]{:S(2)}, u32[]{:S(2)}) collective-permute-start(f32[8,128]{1,0:T(8,128)S(1)} %get-tuple-element.66), channel_id=1, source_target_pairs={{16,32},{32,16},{48,64},{64,48},{80,96},{96,80},{17,33},{33,17},{4... | collective-permute-start | bytes 12296 | tf_op jit(solution)/shard_map/ppermute | solution.py:709
  (2 other events, 20.4 us)

commit v5 on v4

--- a/solution.py
+++ b/solution.py
@@ -13,9 +13,9 @@
 STRIPS = 2 * DEPTH
 FIELD = STRIPS * TILE
 STATE = 5 * TILE
-EARLY = (0, 1)
-RIDERS = ((), (2,), (3,), (4,))
-LATE = (5, 6, 7)
+EARLY = (0,)
+CHUNKS = ((1,), (2,), (3,), (4, 5, 6, 7))
+LATE = CHUNKS[3]
 GROUP = 8
 GY = 16
 BUFFERS = 6
@@ -216,10 +216,9 @@
 
 def settle_kernel(
     moves, base, nb, frames, from_0, from_1, depth, discharge, bed, friction,
-    dyn, fixed, x_0, x_1, y_0, y_1, sem,
+    dyn, fixed, x_0, x_1, y_0, y_1, chunk_0, chunk_1, sem,
 ):
-    ride = RIDERS[0]
-    start_chunk(ride, moves, base, (depth, discharge, bed, friction), y_0, y_1, sem)
+    start_chunk(CHUNKS[0], moves, base, (depth, discharge, bed, friction), chunk_0, chunk_1, sem)
     shape = (SLOTS, 2 * MOVERS)
     land = jnp.zeros(shape, f32)
     left = jnp.zeros((SLOTS, TILE), f32)
@@ -264,18 +263,16 @@
                 x_0[pl.ds(f * MOVERS, MOVERS), :] = up
                 x_1[pl.ds(f * MOVERS, MOVERS), :] = down
             else:
-                y_0[pl.ds(len(ride) * STATE + f * MOVERS, MOVERS), :] = up
-                y_1[pl.ds(len(ride) * STATE + f * MOVERS, MOVERS), :] = down
-    finish_chunk(ride, y_0, y_1, sem)
+                y_0[pl.ds(f * MOVERS, MOVERS), :] = up
+                y_1[pl.ds(f * MOVERS, MOVERS), :] = down
+    finish_chunk(CHUNKS[0], chunk_0, chunk_1, sem)
 
 
 def other_axis(x):
     return jnp.concatenate([x[SLOTS:], x[:SLOTS]], 0)
 
 
-def gather_halos(nb, base_ref, dyn, fixed, messages, turn):
-    first = turn == 0
-    riding = len(RIDERS[turn])
+def gather_halos(nb, base_ref, dyn, fixed, messages, first):
     last = STRIPS - 1
     out = {}
     parts = {name: [] for name in ("h_lo", "h_hi", "z_lo", "n_lo", "q_lo", "z_hi", "n_hi", "lo", "hi")}
@@ -287,7 +284,7 @@
         picks.append((lower[2], higher[2]))
 
         def message(f):
-            rows = pl.ds(axis * riding * STATE + f * MOVERS, MOVERS)
+            rows = pl.ds(f * MOVERS, MOVERS)
             pair = messages[axis]
             from_higher, from_lower = swap(is_odd(base_ref, axis), pair[0][rows, :], pair[1][rows, :])
             return from_lower, from_higher
@@ -327,16 +324,9 @@
         (x0, x1, y0, y1), rest = rest[1:5], rest[5:]
     depth, discharge, bed, friction = rest[:4]
     tiles = (depth, discharge, bed, friction)
-    final = turn == 2
-    if final:
-        (dyn_out, still_out, trail, x_0, x_1, y_0, y_1, late_0, late_1, sem) = rest[4:]
-    else:
-        (dyn_out, still_out, trail, x_0, x_1, y_0, y_1, sem) = rest[4:]
-    ride = RIDERS[turn + 1]
-    start_chunk(ride, moves, base, tiles, y_0, y_1, sem.at[0])
-    if final:
-        start_chunk(LATE, moves, base, tiles, late_0, late_1, sem.at[1])
-    halo, picks = gather_halos(nb, base, dyn, fixed, ((x0, x1), (y0, y1)), turn)
+    dyn_out, still_out, trail, x_0, x_1, y_0, y_1, chunk_0, chunk_1, sem = rest[4:]
+    start_chunk(CHUNKS[turn + 1], moves, base, tiles, chunk_0, chunk_1, sem)
+    halo, picks = gather_halos(nb, base, dyn, fixed, ((x0, x1), (y0, y1)), first)
     names = ("z_lo", "n_lo", "z_hi", "n_hi", "q_lo")
     if not first:
         for j, name in enumerate(names):
@@ -404,11 +394,9 @@
             x_0[...] = up
             x_1[...] = down
         else:
-            y_0[pl.ds(len(ride) * STATE, MOVERS), :] = up
-            y_1[pl.ds(len(ride) * STATE, MOVERS), :] = down
-    finish_chunk(ride, y_0, y_1, sem.at[0])
-    if final:
-        finish_chunk(LATE, late_0, late_1, sem.at[1])
+            y_0[...] = up
+            y_1[...] = down
+    finish_chunk(CHUNKS[turn + 1], chunk_0, chunk_1, sem)
 
 
 def run_tiles(
@@ -598,8 +586,8 @@
 
 
 def tile_kernel(
-    moves, base, ids, nb_s, nb, dyn, fixed, still, x_0, x_1, l3, u3, t0, t1, t2,
-    l1, l2, u1, u2, early_0, early_1, depth, discharge, bed, friction,
+    moves, base, ids, nb_s, nb, dyn, fixed, still, x_0, x_1, y_0, y_1, t0, t1, t2,
+    early_0, early_1, a_0, a_1, b_0, b_1, c_0, c_1, depth, discharge, bed, friction,
     depth_out, flow_out, edges, columns,
     zeros, turned, queue, origin, zero_sem, *scratch,
 ):
@@ -612,7 +600,7 @@
     def mark(t, code):
         origin[t] = code
 
-    note_arrivals(EARLY + RIDERS[1] + RIDERS[2] + RIDERS[3], moves, base, mark)
+    note_arrivals(EARLY + CHUNKS[0] + CHUNKS[1] + CHUNKS[2], moves, base, mark)
     note_arrivals(LATE, moves, base, lambda t, code: mark(t, -1))
 
     def enqueue(t, size):
@@ -632,7 +620,7 @@
 
     def before_loop():
         lax.fori_loop(live, SLOTS, blank, 0)
-        halo, _ = gather_halos(nb, base, dyn, fixed, ((x_0, x_1), (l3, u3)), 3)
+        halo, _ = gather_halos(nb, base, dyn, fixed, ((x_0, x_1), (y_0, y_1)), False)
 
         def kept(j):
             return still[:, pl.ds(j * TILE, TILE)]
@@ -662,8 +650,8 @@
         columns[2] = turned[...].T
 
     sources = chunk_sources(EARLY, early_0, early_1)
-    for entries, chunk_0, chunk_1 in zip(RIDERS[1:], (l1, l2, l3), (u1, u2, u3)):
-        sources += chunk_sources(entries, chunk_0, chunk_1)
+    for entries, *chunks in zip(CHUNKS, (a_0, b_0, c_0), (a_1, b_1, c_1)):
+        sources += chunk_sources(entries, *chunks)
     run_tiles(
         queue, origin, count, sources, (depth, discharge, bed, friction), nb_s, edges, columns,
         (depth_out, flow_out), before_loop, *scratch,
@@ -701,11 +689,7 @@
 
 def trade(block, axis, pairing):
     size = lax.axis_size(axis)
-    pairs = []
-    for i in range(size):
-        other = i ^ 1 if pairing == 0 else ((i + 1) ^ 1) - 1
-        if 0 <= other < size:
-            pairs.append((i, other))
+    pairs = [(i, (((i + pairing) ^ 1) - pairing) % size) for i in range(size)]
     return lax.ppermute(block, axis, pairs)
 
 
@@ -716,8 +700,8 @@
 
 
 def exchange(x_0, x_1, y_0, y_1):
+    got_x = trade_both(x_0, x_1, "gx")
     got_y = trade_both(y_0, y_1, "gy")
-    got_x = trade_both(x_0, x_1, "gx")
     return *got_x, *got_y
 
 
@@ -798,24 +782,23 @@
     dyn, fixed, *sends = call(
         settle_kernel,
         in_specs=[SMEM, SMEM] + [VMEM] * 4 + [HBM] * 4,
-        out_specs=[VMEM] * 6,
+        out_specs=[VMEM] * 8,
         out_shape=[
             held(2 * SLOTS, 3 * FIELD),
             held(2 * SLOTS, 2 * FIELD),
             held(first_rows, TILE),
             held(first_rows, TILE),
-            held(len(RIDERS[0]) * STATE + first_rows, TILE),
-            held(len(RIDERS[0]) * STATE + first_rows, TILE),
+            held(first_rows, TILE),
+            held(first_rows, TILE),
+            *[held(len(CHUNKS[0]) * STATE, TILE)] * 2,
         ],
         scratch_shapes=[pltpu.SemaphoreType.DMA((2,))],
         compiler_params=pltpu.CompilerParams(vmem_limit_bytes=12 * 2**20),
     )(plan, base, *on_core(nb, frames, from_0, from_1), *tiles)
-    got = exchange(*sends)
-    lows = [got[2]]
-    highs = [got[3]]
+    got = exchange(*sends[:4])
+    chunks = [trade_both(*sends[4:], "gy")]
     still = []
     trails = []
-    late = []
     for turn in range(3):
 
         def body(*refs, turn=turn):
@@ -827,29 +810,26 @@
             (2 * SLOTS, 2 * TILE),
             (MOVERS, TILE),
             (MOVERS, TILE),
-            (len(RIDERS[turn + 1]) * STATE + MOVERS, TILE),
-            (len(RIDERS[turn + 1]) * STATE + MOVERS, TILE),
+            (MOVERS, TILE),
+            (MOVERS, TILE),
+            *[(len(CHUNKS[turn + 1]) * STATE, TILE)] * 2,
         ]
-        if turn == 2:
-            shapes += [(len(LATE) * STATE, TILE)] * 2
         dyn, kept, trail, *sends = call(
             body,
             in_specs=[SMEM, SMEM] + [VMEM] * (7 + len(still)) + [HBM] * 4,
             out_specs=[VMEM] * len(shapes),
             out_shape=[held(*s) for s in shapes],
-            scratch_shapes=[pltpu.SemaphoreType.DMA((2, 2))],
+            scratch_shapes=[pltpu.SemaphoreType.DMA((2,))],
             compiler_params=pltpu.CompilerParams(vmem_limit_bytes=12 * 2**20),
         )(plan, base, *on_core(nb, dyn, fixed, *still, *got), *tiles)
         still = [kept]
         trails.append(trail)
-        late = sends[4:]
         got = exchange(*sends[:4])
-        lows.append(got[2])
-        highs.append(got[3])
-
-    late_0, late_1 = trade_both(*late, "gy")
+        chunks.append(trade_both(*sends[4:], "gy"))
+
+    late_0, late_1 = chunks[3]
     kept_inputs = on_core(
-        nb, dyn, fixed, *still, *got, *trails, *lows[1:3], *highs[1:3], early_0, early_1
+        nb, dyn, fixed, *still, *got, *trails, early_0, early_1, *chunks[0], *chunks[1], *chunks[2]
     )
     new_depth, new_flow, edges, columns = call(
         tile_kernel,

time: 149 us -> 158 us (1.060)
  the two profiles are of different devices: /device:TPU:39 before, /device:TPU:32 now
where the time goes in v5:
time: 158 us; the launch traced here: 157 us
  waiting for transfers between devices  71.8 us (45%)
  Pallas kernels  43.1 us (27%)
  starting transfers between devices  41 us (26%)
    ppermute x28, waiting for transfers between devices, trade(): return lax.ppermute(block, axis, pairs)  71.8 us
    ppermute x28, starting transfers between devices, trade(): return lax.ppermute(block, axis, pairs)  41 us
    pallas_call x1, Pallas kernels, shards(): call(tile_kernel, in_specs=[SMEM] * 4 + [VMEM] * len(kept_inputs) + [HBM]...  21.5 us
    pallas_call x3, Pallas kernels, shards(): call(body, in_specs=[SMEM, SMEM] + [VMEM] * (7 + len(still)) + [HBM] * 4,...  8.13 us
    pallas_call x1, Pallas kernels, shards(): pl.pallas_call(extract_kernel, in_specs=[SMEM, SMEM] + [HBM] * 4, out_spe...  6.29 us
    pallas_call x1, Pallas kernels, shards(): pl.pallas_call(late_kernel, in_specs=[SMEM] * 3 + [VMEM] * 4 + [HBM] * 2,...  4.7 us
  transfers between devices with their start and end apart: 28, of which 11 were waited for; matrix products, arithmetic and copies ran while one was open for 0% of the time, Pallas kernels for 14%

profile of v5, /device:TPU:32, one launch (start us, length us, event | category | flops | bytes accessed | tf_op | source)
XLA Modules:
  0.0 157.5 jit_solution(14480621303661761283)
XLA Ops:
  1.3 6.3 %extract.1 = (f32[64,5120]{1,0:T(8,128)S(1)}, f32[8,10240]{1,0:T(8,128)S(1)}, f32[8,10240]{1,0:T(8,128)S(1)}, f32[640,128]{1,0:T(8,128)S(1)}, f32[640,128]{1,0:T(8,128)S(1)}) custom-call(s32[2,2,8]{2,1,0:T(2,128)S(1)} %bitcast.11, s32[1]{0:T(128)} %bitcast.2.base.refs_1_, f32[4096,128]{1,0:T(8,128)} %bitcast.31, f32[8192,128]{1,0:T(8,128)} %bitcast.25, ...), custom_call_target="tpu_custom_call" | custom-call | tf_op jit(solution)/shard_map/extract/pallas_call | solution.py:754
  9.3 4.4 %collective-permute-start.1 = (f32[8,10240]{1,0:T(8,128)S(1)}, f32[8,10240]{1,0:T(8,128)S(1)}, u32[]{:S(2)}, u32[]{:S(2)}) collective-permute-start(f32[8,10240]{1,0:T(8,128)S(1)} %get-tuple-element.50), channel_id=1, source_target_pairs={{0,15},{1,2},{2,1},{3,4},{4,3},{5,6},{6,5},{7,8},{8,7},{9,10},{10,... | collective-permute-start | bytes 983048 | tf_op jit(solution)/shard_map/ppermute | solution.py:693
  13.7 3.5 %collective-permute-done.from_0 = f32[8,10240]{1,0:T(8,128)S(1)} collective-permute-done((f32[8,10240]{1,0:T(8,128)S(1)}, f32[8,10240]{1,0:T(8,128)S(1)}, u32[]{:S(2)}, u32[]{:S(2)}) %collective-permute-start) | collective-permute-done | bytes 327712 | tf_op jit(solution)/shard_map/ppermute | solution.py:693
  17.1 4.6 %collective-permute-done.1.from_1 = f32[8,10240]{1,0:T(8,128)S(1)} collective-permute-done((f32[8,10240]{1,0:T(8,128)S(1)}, f32[8,10240]{1,0:T(8,128)S(1)}, u32[]{:S(2)}, u32[]{:S(2)}) %collective-permute-start.1) | collective-permute-done | bytes 327712 | tf_op jit(solution)/shard_map/ppermute | solution.py:693
  24.5 4.4 %collective-permute-start.5 = (f32[32,128]{1,0:T(8,128)S(1)}, f32[32,128]{1,0:T(8,128)S(1)}, u32[]{:S(2)}, u32[]{:S(2)}) collective-permute-start(f32[32,128]{1,0:T(8,128)S(1)} %get-tuple-element.56), channel_id=1, source_target_pairs={{0,15},{1,2},{2,1},{3,4},{4,3},{5,6},{6,5},{7,8},{8,7},{9,10},{10,... | collective-permute-start | bytes 49160 | tf_op jit(solution)/shard_map/ppermute | solution.py:693
  29.0 2.7 %collective-permute-done.5.refs_8_ = f32[32,128]{1,0:T(8,128)S(1)} collective-permute-done((f32[32,128]{1,0:T(8,128)S(1)}, f32[32,128]{1,0:T(8,128)S(1)}, u32[]{:S(2)}, u32[]{:S(2)}) %collective-permute-start.5) | collective-permute-done | bytes 16416 | tf_op jit(solution)/shard_map/ppermute | solution.py:693
  31.6 2.7 %shard_map.87 = (f32[64,3072]{1,0:T(8,128)S(1)}, f32[64,640]{1,0:T(8,128)S(1)}, f32[64,256]{1,0:T(8,128)S(1)}, f32[8,128]{1,0:T(8,128)S(1)}, f32[8,128]{1,0:T(8,...) custom-call(s32[2,2,8]{2,1,0:T(2,128)S(1)} %bitcast.13, ...), custom_call_target="tpu_custom_call" | custom-call | tf_op jit(solution)/shard_map/pallas_call | solution.py:817
  35.2 3.4 %collective-permute-start.7 = (f32[8,128]{1,0:T(8,128)S(1)}, f32[8,128]{1,0:T(8,128)S(1)}, u32[]{:S(2)}, u32[]{:S(2)}) collective-permute-start(f32[8,128]{1,0:T(8,128)S(1)} %get-tuple-element.60), channel_id=1, source_target_pairs={{0,112},{16,32},{32,16},{48,64},{64,48},{80,96},{96,80},{112,0},{1... | collective-permute-start | bytes 12296 | tf_op jit(solution)/shard_map/ppermute | solution.py:693
  38.6 4.4 %collective-permute-start.9 = (f32[8,128]{1,0:T(8,128)S(1)}, f32[8,128]{1,0:T(8,128)S(1)}, u32[]{:S(2)}, u32[]{:S(2)}) collective-permute-start(f32[8,128]{1,0:T(8,128)S(1)} %get-tuple-element.62), channel_id=1, source_target_pairs={{0,15},{1,2},{2,1},{3,4},{4,3},{5,6},{6,5},{7,8},{8,7},{9,10},{10,... | collective-permute-start | bytes 12296 | tf_op jit(solution)/shard_map/ppermute | solution.py:693
  42.9 2.6 %collective-permute-done.9.refs_9_ = f32[8,128]{1,0:T(8,128)S(1)} collective-permute-done((f32[8,128]{1,0:T(8,128)S(1)}, f32[8,128]{1,0:T(8,128)S(1)}, u32[]{:S(2)}, u32[]{:S(2)}) %collective-permute-start.9) | collective-permute-done | bytes 4128 | tf_op jit(solution)/shard_map/ppermute | solution.py:693
  48.6 4.4 %collective-permute-start.13 = (f32[8,128]{1,0:T(8,128)S(1)}, f32[8,128]{1,0:T(8,128)S(1)}, u32[]{:S(2)}, u32[]{:S(2)}) collective-permute-start(f32[8,128]{1,0:T(8,128)S(1)} %get-tuple-element.68), channel_id=1, source_target_pairs={{0,15},{1,2},{2,1},{3,4},{4,3},{5,6},{6,5},{7,8},{8,7},{9,10},{10,... | collective-permute-start | bytes 12296 | tf_op jit(solution)/shard_map/ppermute | solution.py:693
  53.0 2.5 %collective-permute-done.13.refs_9_ = f32[8,128]{1,0:T(8,128)S(1)} collective-permute-done((f32[8,128]{1,0:T(8,128)S(1)}, f32[8,128]{1,0:T(8,128)S(1)}, u32[]{:S(2)}, u32[]{:S(2)}) %collective-permute-start.13) | collective-permute-done | bytes 4128 | tf_op jit(solution)/shard_map/ppermute | solution.py:693
  55.5 2.9 %shard_map.89 = (f32[64,3072]{1,0:T(8,128)S(1)}, f32[64,640]{1,0:T(8,128)S(1)}, f32[64,256]{1,0:T(8,128)S(1)}, f32[8,128]{1,0:T(8,128)S(1)}, f32[8,128]{1,0:T(8,...) custom-call(s32[2,2,8]{2,1,0:T(2,128)S(1)} %bitcast.15, ...), custom_call_target="tpu_custom_call" | custom-call | tf_op jit(solution)/shard_map/pallas_call | solution.py:817
  58.5 4.9 %collective-permute-start.27 = (f32[2560,128]{1,0:T(8,128)S(1)}, f32[2560,128]{1,0:T(8,128)S(1)}, u32[]{:S(2)}, u32[]{:S(2)}) collective-permute-start(f32[2560,128]{1,0:T(8,128)S(1)} %get-tuple-element.89), channel_id=1, source_target_pairs={{0,15},{1,2},{2,1},{3,4},{4,3},{5,6},{6,5},{7,8},{8,7},{9,10},{10,... | collective-permute-start | bytes 3932168 | tf_op jit(solution)/shard_map/ppermute | solution.py:693
  65.4 29.7 %collective-permute-done.18.early_0 = f32[640,128]{1,0:T(8,128)S(1)} collective-permute-done((f32[640,128]{1,0:T(8,128)S(1)}, f32[640,128]{1,0:T(8,128)S(1)}, u32[]{:S(2)}, u32[]{:S(2)}) %collective-permute-start.18) | collective-permute-done | bytes 327712 | tf_op jit(solution)/shard_map/ppermute | solution.py:693
  95.1 3.4 %collective-permute-done.19.early_1 = f32[640,128]{1,0:T(8,128)S(1)} collective-permute-done((f32[640,128]{1,0:T(8,128)S(1)}, f32[640,128]{1,0:T(8,128)S(1)}, u32[]{:S(2)}, u32[]{:S(2)}) %collective-permute-start.19) | collective-permute-done | bytes 327712 | tf_op jit(solution)/shard_map/ppermute | solution.py:693
  98.5 4.5 %collective-permute-start.17 = (f32[8,128]{1,0:T(8,128)S(1)}, f32[8,128]{1,0:T(8,128)S(1)}, u32[]{:S(2)}, u32[]{:S(2)}) collective-permute-start(f32[8,128]{1,0:T(8,128)S(1)} %get-tuple-element.74), channel_id=1, source_target_pairs={{0,15},{1,2},{2,1},{3,4},{4,3},{5,6},{6,5},{7,8},{8,7},{9,10},{10,... | collective-permute-start | bytes 12296 | tf_op jit(solution)/shard_map/ppermute | solution.py:693
  103.1 3.6 %collective-permute-start.21 = (f32[640,128]{1,0:T(8,128)S(1)}, f32[640,128]{1,0:T(8,128)S(1)}, u32[]{:S(2)}, u32[]{:S(2)}) collective-permute-start(f32[640,128]{1,0:T(8,128)S(1)} %get-tuple-element.81), channel_id=1, source_target_pairs={{0,15},{1,2},{2,1},{3,4},{4,3},{5,6},{6,5},{7,8},{8,7},{9,10},{10,... | collective-permute-start | bytes 983048 | tf_op jit(solution)/shard_map/ppermute | solution.py:693
  106.7 6.9 %collective-permute-done.20.a_0 = f32[640,128]{1,0:T(8,128)S(1)} collective-permute-done((f32[640,128]{1,0:T(8,128)S(1)}, f32[640,128]{1,0:T(8,128)S(1)}, u32[]{:S(2)}, u32[]{:S(2)}) %collective-permute-start.20) | collective-permute-done | bytes 327712 | tf_op jit(solution)/shard_map/ppermute | solution.py:693
  114.5 6.2 %collective-permute-done.22.b_0 = f32[640,128]{1,0:T(8,128)S(1)} collective-permute-done((f32[640,128]{1,0:T(8,128)S(1)}, f32[640,128]{1,0:T(8,128)S(1)}, u32[]{:S(2)}, u32[]{:S(2)}) %collective-permute-start.22) | collective-permute-done | bytes 327712 | tf_op jit(solution)/shard_map/ppermute | solution.py:693
  121.5 5.7 %collective-permute-done.23.b_1 = f32[640,128]{1,0:T(8,128)S(1)} collective-permute-done((f32[640,128]{1,0:T(8,128)S(1)}, f32[640,128]{1,0:T(8,128)S(1)}, u32[]{:S(2)}, u32[]{:S(2)}) %collective-permute-start.23) | collective-permute-done | bytes 327712 | tf_op jit(solution)/shard_map/ppermute | solution.py:693
  127.2 3.9 %collective-permute-done.25.c_1 = f32[640,128]{1,0:T(8,128)S(1)} collective-permute-done((f32[640,128]{1,0:T(8,128)S(1)}, f32[640,128]{1,0:T(8,128)S(1)}, u32[]{:S(2)}, u32[]{:S(2)}) %collective-permute-start.25) | collective-permute-done | bytes 327712 | tf_op jit(solution)/shard_map/ppermute | solution.py:693
  131.1 21.5 %shard_map.90 = (f32[4096,128]{1,0:T(8,128)}, f32[8192,128]{1,0:T(8,128)}, f32[10,32,128]{2,1,0:T(8,128)S(1)}, f32[3,128,128]{2,1,0:T(8,128)S(1)}) custom-call(s32[2,2,8]{2,1,0:T(2,128)S(1)} %bitcast.16, s32[1]{0:T(128)} %bitcast.2.base.refs_1_, s32[32]{0:T(128)S(1)} %copy-done.3, s32[4,32]{1,0:T(4,128)S(1)} %bitcast.22, s32[4,32]{1,0:T(4,128)S(1)} %bitcast.23, ...), custom_call_target="tpu_custom_call" | custom-call | tf_op jit(solution)/shard_map/pallas_call | solution.py:834
  152.6 4.7 %late_tiles.1 = (f32[4096,128]{1,0:T(8,128)}, f32[8192,128]{1,0:T(8,128)}) custom-call(s32[2,2,8]{2,1,0:T(2,128)S(1)} %bitcast.17, s32[1]{0:T(128)} %bitcast.2.base.refs_1_, s32[4,32]{1,0:T(4,128)S(1)} %bitcast.24, f32[10,32,128]{2,1,0:T(8,128)S(1)} %get-tuple-element.86.edges, ...), custom_call_target="tpu_custom_call", output_to_operand_aliasing={{0}: (7, {}), {1}: (8, {})} | custom-call | tf_op jit(solution)/shard_map/late_tiles/pallas_call | solution.py:854
  (47 shorter events, 12.6 us)
Async XLA Ops:
  7.6 9.5 %collective-permute-start = (f32[8,10240]{1,0:T(8,128)S(1)}, f32[8,10240]{1,0:T(8,128)S(1)}, u32[]{:S(2)}, u32[]{:S(2)}) collective-permute-start(f32[8,10240]{1,0:T(8,128)S(1)} %get-tuple-element.49), channel_id=1, source_target_pairs={{0,1},{1,0},{2,3},{3,2},{4,5},{5,4},{6,7},{7,6},{8,9},{9,8},{10,11... | collective-permute-start | bytes 983048 | tf_op jit(solution)/shard_map/ppermute | solution.py:693
  9.3 12.5 %collective-permute-start.1 = (f32[8,10240]{1,0:T(8,128)S(1)}, f32[8,10240]{1,0:T(8,128)S(1)}, u32[]{:S(2)}, u32[]{:S(2)}) collective-permute-start(f32[8,10240]{1,0:T(8,128)S(1)} %get-tuple-element.50), channel_id=1, source_target_pairs={{0,15},{1,2},{2,1},{3,4},{4,3},{5,6},{6,5},{7,8},{8,7},{9,10},{10,... | collective-permute-start | bytes 983048 | tf_op jit(solution)/shard_map/ppermute | solution.py:693
  24.2 4.7 %collective-permute-start.2 = (f32[32,128]{1,0:T(8,128)S(1)}, f32[32,128]{1,0:T(8,128)S(1)}, u32[]{:S(2)}, u32[]{:S(2)}) collective-permute-start(f32[32,128]{1,0:T(8,128)S(1)} %get-tuple-element.53), channel_id=1, source_target_pairs={{0,16},{16,0},{32,48},{48,32},{64,80},{80,64},{96,112},{112,96},{1... | collective-permute-start | bytes 49160 | tf_op jit(solution)/shard_map/ppermute | solution.py:693
  24.3 4.6 %collective-permute-start.3 = (f32[32,128]{1,0:T(8,128)S(1)}, f32[32,128]{1,0:T(8,128)S(1)}, u32[]{:S(2)}, u32[]{:S(2)}) collective-permute-start(f32[32,128]{1,0:T(8,128)S(1)} %get-tuple-element.54), channel_id=1, source_target_pairs={{0,112},{16,32},{32,16},{48,64},{64,48},{80,96},{96,80},{112,0},{1... | collective-permute-start | bytes 49160 | tf_op jit(solution)/shard_map/ppermute | solution.py:693
  24.5 7.1 %collective-permute-start.5 = (f32[32,128]{1,0:T(8,128)S(1)}, f32[32,128]{1,0:T(8,128)S(1)}, u32[]{:S(2)}, u32[]{:S(2)}) collective-permute-start(f32[32,128]{1,0:T(8,128)S(1)} %get-tuple-element.56), channel_id=1, source_target_pairs={{0,15},{1,2},{2,1},{3,4},{4,3},{5,6},{6,5},{7,8},{8,7},{9,10},{10,... | collective-permute-start | bytes 49160 | tf_op jit(solution)/shard_map/ppermute | solution.py:693
  34.4 8.6 %collective-permute-start.6 = (f32[8,128]{1,0:T(8,128)S(1)}, f32[8,128]{1,0:T(8,128)S(1)}, u32[]{:S(2)}, u32[]{:S(2)}) collective-permute-start(f32[8,128]{1,0:T(8,128)S(1)} %get-tuple-element.59), channel_id=1, source_target_pairs={{0,16},{16,0},{32,48},{48,32},{64,80},{80,64},{96,112},{112,96},{1... | collective-permute-start | bytes 12296 | tf_op jit(solution)/shard_map/ppermute | solution.py:693
  35.2 7.8 %collective-permute-start.7 = (f32[8,128]{1,0:T(8,128)S(1)}, f32[8,128]{1,0:T(8,128)S(1)}, u32[]{:S(2)}, u32[]{:S(2)}) collective-permute-start(f32[8,128]{1,0:T(8,128)S(1)} %get-tuple-element.60), channel_id=1, source_target_pairs={{0,112},{16,32},{32,16},{48,64},{64,48},{80,96},{96,80},{112,0},{1... | collective-permute-start | bytes 12296 | tf_op jit(solution)/shard_map/ppermute | solution.py:693
  38.6 6.9 %collective-permute-start.9 = (f32[8,128]{1,0:T(8,128)S(1)}, f32[8,128]{1,0:T(8,128)S(1)}, u32[]{:S(2)}, u32[]{:S(2)}) collective-permute-start(f32[8,128]{1,0:T(8,128)S(1)} %get-tuple-element.62), channel_id=1, source_target_pairs={{0,15},{1,2},{2,1},{3,4},{4,3},{5,6},{6,5},{7,8},{8,7},{9,10},{10,... | collective-permute-start | bytes 12296 | tf_op jit(solution)/shard_map/ppermute | solution.py:693
  48.0 5.0 %collective-permute-start.10 = (f32[8,128]{1,0:T(8,128)S(1)}, f32[8,128]{1,0:T(8,128)S(1)}, u32[]{:S(2)}, u32[]{:S(2)}) collective-permute-start(f32[8,128]{1,0:T(8,128)S(1)} %get-tuple-element.65), channel_id=1, source_target_pairs={{0,16},{16,0},{32,48},{48,32},{64,80},{80,64},{96,112},{112,96},{1... | collective-permute-start | bytes 12296 | tf_op jit(solution)/shard_map/ppermute | solution.py:693
  48.1 4.9 %collective-permute-start.11 = (f32[8,128]{1,0:T(8,128)S(1)}, f32[8,128]{1,0:T(8,128)S(1)}, u32[]{:S(2)}, u32[]{:S(2)}) collective-permute-start(f32[8,128]{1,0:T(8,128)S(1)} %get-tuple-element.66), channel_id=1, source_target_pairs={{0,112},{16,32},{32,16},{48,64},{64,48},{80,96},{96,80},{112,0},{1... | collective-permute-start | bytes 12296 | tf_op jit(solution)/shard_map/ppermute | solution.py:693
  48.6 6.9 %collective-permute-start.13 = (f32[8,128]{1,0:T(8,128)S(1)}, f32[8,128]{1,0:T(8,128)S(1)}, u32[]{:S(2)}, u32[]{:S(2)}) collective-permute-start(f32[8,128]{1,0:T(8,128)S(1)} %get-tuple-element.68), channel_id=1, source_target_pairs={{0,15},{1,2},{2,1},{3,4},{4,3},{5,6},{6,5},{7,8},{8,7},{9,10},{10,... | collective-permute-start | bytes 12296 | tf_op jit(solution)/shard_map/ppermute | solution.py:693
  58.4 94.2 %collective-permute-start.26 = (f32[2560,128]{1,0:T(8,128)S(1)}, f32[2560,128]{1,0:T(8,128)S(1)}, u32[]{:S(2)}, u32[]{:S(2)}) collective-permute-start(f32[2560,128]{1,0:T(8,128)S(1)} %get-tuple-element.88), channel_id=1, source_target_pairs={{0,1},{1,0},{2,3},{3,2},{4,5},{5,4},{6,7},{7,6},{8,9},{9,8},{10,11... | collective-permute-start | bytes 3932168 | tf_op jit(solution)/shard_map/ppermute | solution.py:693
  58.5 94.1 %collective-permute-start.27 = (f32[2560,128]{1,0:T(8,128)S(1)}, f32[2560,128]{1,0:T(8,128)S(1)}, u32[]{:S(2)}, u32[]{:S(2)}) collective-permute-start(f32[2560,128]{1,0:T(8,128)S(1)} %get-tuple-element.89), channel_id=1, source_target_pairs={{0,15},{1,2},{2,1},{3,4},{4,3},{5,6},{6,5},{7,8},{8,7},{9,10},{10,... | collective-permute-start | bytes 3932168 | tf_op jit(solution)/shard_map/ppermute | solution.py:693
  63.4 31.7 %collective-permute-start.18 = (f32[640,128]{1,0:T(8,128)S(1)}, f32[640,128]{1,0:T(8,128)S(1)}, u32[]{:S(2)}, u32[]{:S(2)}) collective-permute-start(f32[640,128]{1,0:T(8,128)S(1)} %get-tuple-element.78), channel_id=1, source_target_pairs={{0,1},{1,0},{2,3},{3,2},{4,5},{5,4},{6,7},{7,6},{8,9},{9,8},{10,11... | collective-permute-start | bytes 983048 | tf_op jit(solution)/shard_map/ppermute | solution.py:693
  63.4 35.1 %collective-permute-start.19 = (f32[640,128]{1,0:T(8,128)S(1)}, f32[640,128]{1,0:T(8,128)S(1)}, u32[]{:S(2)}, u32[]{:S(2)}) collective-permute-start(f32[640,128]{1,0:T(8,128)S(1)} %get-tuple-element.79), channel_id=1, source_target_pairs={{0,15},{1,2},{2,1},{3,4},{4,3},{5,6},{6,5},{7,8},{8,7},{9,10},{10,... | collective-permute-start | bytes 983048 | tf_op jit(solution)/shard_map/ppermute | solution.py:693
  65.4 33.2 %collective-permute-start.14 = (f32[8,128]{1,0:T(8,128)S(1)}, f32[8,128]{1,0:T(8,128)S(1)}, u32[]{:S(2)}, u32[]{:S(2)}) collective-permute-start(f32[8,128]{1,0:T(8,128)S(1)} %get-tuple-element.71), channel_id=1, source_target_pairs={{0,16},{16,0},{32,48},{48,32},{64,80},{80,64},{96,112},{112,96},{1... | collective-permute-start | bytes 12296 | tf_op jit(solution)/shard_map/ppermute | solution.py:693
  95.1 8.0 %collective-permute-start.15 = (f32[8,128]{1,0:T(8,128)S(1)}, f32[8,128]{1,0:T(8,128)S(1)}, u32[]{:S(2)}, u32[]{:S(2)}) collective-permute-start(f32[8,128]{1,0:T(8,128)S(1)} %get-tuple-element.72), channel_id=1, source_target_pairs={{0,112},{16,32},{32,16},{48,64},{64,48},{80,96},{96,80},{112,0},{1... | collective-permute-start | bytes 12296 | tf_op jit(solution)/shard_map/ppermute | solution.py:693
  98.5 8.2 %collective-permute-start.17 = (f32[8,128]{1,0:T(8,128)S(1)}, f32[8,128]{1,0:T(8,128)S(1)}, u32[]{:S(2)}, u32[]{:S(2)}) collective-permute-start(f32[8,128]{1,0:T(8,128)S(1)} %get-tuple-element.74), channel_id=1, source_target_pairs={{0,15},{1,2},{2,1},{3,4},{4,3},{5,6},{6,5},{7,8},{8,7},{9,10},{10,... | collective-permute-start | bytes 12296 | tf_op jit(solution)/shard_map/ppermute | solution.py:693
  103.1 10.6 %collective-permute-start.20 = (f32[640,128]{1,0:T(8,128)S(1)}, f32[640,128]{1,0:T(8,128)S(1)}, u32[]{:S(2)}, u32[]{:S(2)}) collective-permute-start(f32[640,128]{1,0:T(8,128)S(1)} %get-tuple-element.80), channel_id=1, source_target_pairs={{0,1},{1,0},{2,3},{3,2},{4,5},{5,4},{6,7},{7,6},{8,9},{9,8},{10,11... | collective-permute-start | bytes 983048 | tf_op jit(solution)/shard_map/ppermute | solution.py:693
  103.1 11.4 %collective-permute-start.21 = (f32[640,128]{1,0:T(8,128)S(1)}, f32[640,128]{1,0:T(8,128)S(1)}, u32[]{:S(2)}, u32[]{:S(2)}) collective-permute-start(f32[640,128]{1,0:T(8,128)S(1)} %get-tuple-element.81), channel_id=1, source_target_pairs={{0,15},{1,2},{2,1},{3,4},{4,3},{5,6},{6,5},{7,8},{8,7},{9,10},{10,... | collective-permute-start | bytes 983048 | tf_op jit(solution)/shard_map/ppermute | solution.py:693
  106.7 14.0 %collective-permute-start.22 = (f32[640,128]{1,0:T(8,128)S(1)}, f32[640,128]{1,0:T(8,128)S(1)}, u32[]{:S(2)}, u32[]{:S(2)}) collective-permute-start(f32[640,128]{1,0:T(8,128)S(1)} %get-tuple-element.82), channel_id=1, source_target_pairs={{0,1},{1,0},{2,3},{3,2},{4,5},{5,4},{6,7},{7,6},{8,9},{9,8},{10,11... | collective-permute-start | bytes 983048 | tf_op jit(solution)/shard_map/ppermute | solution.py:693
  113.6 13.5 %collective-permute-start.23 = (f32[640,128]{1,0:T(8,128)S(1)}, f32[640,128]{1,0:T(8,128)S(1)}, u32[]{:S(2)}, u32[]{:S(2)}) collective-permute-start(f32[640,128]{1,0:T(8,128)S(1)} %get-tuple-element.83), channel_id=1, source_target_pairs={{0,15},{1,2},{2,1},{3,4},{4,3},{5,6},{6,5},{7,8},{8,7},{9,10},{10,... | collective-permute-start | bytes 983048 | tf_op jit(solution)/shard_map/ppermute | solution.py:693
  114.5 12.7 %collective-permute-start.24 = (f32[640,128]{1,0:T(8,128)S(1)}, f32[640,128]{1,0:T(8,128)S(1)}, u32[]{:S(2)}, u32[]{:S(2)}) collective-permute-start(f32[640,128]{1,0:T(8,128)S(1)} %get-tuple-element.84), channel_id=1, source_target_pairs={{0,1},{1,0},{2,3},{3,2},{4,5},{5,4},{6,7},{7,6},{8,9},{9,8},{10,11... | collective-permute-start | bytes 983048 | tf_op jit(solution)/shard_map/ppermute | solution.py:693
  120.7 10.4 %collective-permute-start.25 = (f32[640,128]{1,0:T(8,128)S(1)}, f32[640,128]{1,0:T(8,128)S(1)}, u32[]{:S(2)}, u32[]{:S(2)}) collective-permute-start(f32[640,128]{1,0:T(8,128)S(1)} %get-tuple-element.85), channel_id=1, source_target_pairs={{0,15},{1,2},{2,1},{3,4},{4,3},{5,6},{6,5},{7,8},{8,7},{9,10},{10,... | collective-permute-start | bytes 983048 | tf_op jit(solution)/shard_map/ppermute | solution.py:693
  (8 other events, 124.5 us)

commit v6 on v5

--- a/solution.py
+++ b/solution.py
@@ -16,6 +16,7 @@
 EARLY = (0,)
 CHUNKS = ((1,), (2,), (3,), (4, 5, 6, 7))
 LATE = CHUNKS[3]
+LOADS = (EARLY,) + CHUNKS
 GROUP = 8
 GY = 16
 BUFFERS = 6
@@ -115,8 +116,7 @@
 
 
 def extract_kernel(
-    moves, base, depth, discharge, bed, friction, frames, out_0, out_1, early_0, early_1,
-    depth_v, flow_v, bed_v, rough_v, acc, turned, load_sem, sem,
+    depth, discharge, bed, friction, frames, depth_v, flow_v, bed_v, rough_v, acc, turned, load_sem,
 ):
     lane = iota((TILE, TILE), 1)
     groups = SLOTS // GROUP
@@ -129,7 +129,6 @@
         for c in copies:
             c.start()
         loads.append(copies)
-    start_chunk(EARLY, moves, base, (depth, discharge, bed, friction), early_0, early_1, sem)
 
     def strip(f, k):
         return pl.ds((f * STRIPS + k) * TILE, TILE)
@@ -162,20 +161,36 @@
                 frames[pl.ds(SLOTS + half * per, per), strip(to, k)] = turned[
                     half, pl.ds((k + DEPTH) % STRIPS, per, stride=STRIPS), :
                 ]
-    shape = (2 * MOVERS, SLOTS)
-    pick = jnp.zeros(shape, f32)
-    for m in range(MOVERS):
+
+
+def pack_kernel(moves, base, depth, discharge, bed, friction, out_0, out_1, *rest):
+    boxes, (acc, turned, sem) = rest[: 2 * len(LOADS)], rest[2 * len(LOADS) :]
+    for g, entries in enumerate(LOADS):
+        start_chunk(entries, moves, base, (depth, discharge, bed, friction), *boxes[2 * g : 2 * g + 2], sem.at[g])
+    lane = iota((TILE, TILE), 1)
+    outs = (out_0, out_1)
+    for g, entries in enumerate(LOADS):
+        finish_chunk(entries, *boxes[2 * g : 2 * g + 2], sem.at[g])
+        for i, m in enumerate(entries):
+            for pairing in range(2):
+                box = boxes[2 * g + pairing]
+                at = (2 * m + pairing) * STRIPS
+                for f in range(5):
+                    top = i * STATE + f * TILE
+                    for k in range(STRIPS):
+                        row = k if k < DEPTH else TILE - STRIPS + k
+                        to = pl.ds((f * STRIPS + k) * TILE, TILE)
+                        outs[pairing][pl.ds(m, 1), to] = box[pl.ds(top + row, 1), :]
+                    turn = pltpu.roll(box[pl.ds(top, TILE), :], (at + DEPTH) % TILE, 1)
+                    acc[f] = turn if at == 0 else jnp.where(lane >= at, turn, acc[f])
+    for f in range(5):
+        to = 5 * STRIPS + (0, 2, 1, 3, 4)[f] * STRIPS
+        turned[...] = acc[f].T
         for pairing in range(2):
-            leaver = moves[way_of(base, pairing), 0, m] - base[0]
-            spot = (iota(shape, 0) == pairing * MOVERS + m) & (iota(shape, 1) == leaver)
-            pick = jnp.where(spot, 1.0, pick)
-    for axis in range(2):
-        for c in range(5):
-            got = route(pick, frames[pl.ds(axis * SLOTS, SLOTS), pl.ds(c * FIELD, FIELD)])
-            to = pl.ds((axis * 5 + c) * FIELD, FIELD)
-            out_0[:, to] = got[:MOVERS]
-            out_1[:, to] = got[MOVERS:]
-    finish_chunk(EARLY, early_0, early_1, sem)
+            for k in range(STRIPS):
+                outs[pairing][:, pl.ds((to + k) * TILE, TILE)] = turned[
+                    pl.ds(pairing * STRIPS + (k + DEPTH) % STRIPS, MOVERS, stride=2 * STRIPS), :
+                ]
 
 
 def start_chunk(entries, moves, base, tiles, out_0, out_1, sem):
@@ -215,10 +230,8 @@
 
 
 def settle_kernel(
-    moves, base, nb, frames, from_0, from_1, depth, discharge, bed, friction,
-    dyn, fixed, x_0, x_1, y_0, y_1, chunk_0, chunk_1, sem,
+    moves, base, nb, frames, from_0, from_1, dyn, fixed, x_0, x_1, y_0, y_1,
 ):
-    start_chunk(CHUNKS[0], moves, base, (depth, discharge, bed, friction), chunk_0, chunk_1, sem)
     shape = (SLOTS, 2 * MOVERS)
     land = jnp.zeros(shape, f32)
     left = jnp.zeros((SLOTS, TILE), f32)
@@ -265,7 +278,6 @@
             else:
                 y_0[pl.ds(f * MOVERS, MOVERS), :] = up
                 y_1[pl.ds(f * MOVERS, MOVERS), :] = down
-    finish_chunk(CHUNKS[0], chunk_0, chunk_1, sem)
 
 
 def other_axis(x):
@@ -314,7 +326,7 @@
     return out, picks
 
 
-def step_kernel(turn, moves, base, nb, dyn, fixed, *rest):
+def step_kernel(turn, base, nb, dyn, fixed, *rest):
     first = turn == 0
     if first:
         still = None
@@ -322,10 +334,7 @@
     else:
         still = rest[0]
         (x0, x1, y0, y1), rest = rest[1:5], rest[5:]
-    depth, discharge, bed, friction = rest[:4]
-    tiles = (depth, discharge, bed, friction)
-    dyn_out, still_out, trail, x_0, x_1, y_0, y_1, chunk_0, chunk_1, sem = rest[4:]
-    start_chunk(CHUNKS[turn + 1], moves, base, tiles, chunk_0, chunk_1, sem)
+    dyn_out, still_out, trail, x_0, x_1, y_0, y_1 = rest
     halo, picks = gather_halos(nb, base, dyn, fixed, ((x0, x1), (y0, y1)), first)
     names = ("z_lo", "n_lo", "z_hi", "n_hi", "q_lo")
     if not first:
@@ -396,7 +405,6 @@
         else:
             y_0[...] = up
             y_1[...] = down
-    finish_chunk(CHUNKS[turn + 1], chunk_0, chunk_1, sem)
 
 
 def run_tiles(
@@ -454,7 +462,7 @@
 
     prime()
     before_loop()
-    part_rows = 16
+    part_rows = 32
     parts = TILE // part_rows
     lane = iota((part_rows, TILE), 1)
     row = iota((part_rows, TILE), 0)
@@ -750,18 +758,26 @@
             friction.reshape(SLOTS * TILE, TILE),
         )
     ]
-    early_rows = len(EARLY) * STATE
-    frames, up, down, early_0, early_1 = pl.pallas_call(
+    out_0, out_1, *cargo = call(
+        pack_kernel,
+        in_specs=[SMEM, SMEM] + [HBM] * 4,
+        out_specs=[VMEM] * (2 + 2 * len(LOADS)),
+        out_shape=[held(MOVERS, 10 * FIELD)] * 2
+        + [held(len(entries) * STATE, TILE) for entries in LOADS for _ in range(2)],
+        scratch_shapes=[
+            pltpu.VMEM((5, TILE, TILE), f32),
+            pltpu.VMEM((TILE, TILE), f32),
+            pltpu.SemaphoreType.DMA((len(LOADS), 2)),
+        ],
+        compiler_params=pltpu.CompilerParams(vmem_limit_bytes=12 * 2**20),
+    )(plan, base, *tiles)
+    from_0, from_1 = trade_both(out_0, out_1, "gy")
+    early_0, early_1 = trade_both(*cargo[:2], "gy")
+    frames = call(
         extract_kernel,
-        in_specs=[SMEM, SMEM] + [HBM] * 4,
-        out_specs=[VMEM] * 5,
-        out_shape=[
-            held(2 * SLOTS, 5 * FIELD),
-            held(MOVERS, 10 * FIELD),
-            held(MOVERS, 10 * FIELD),
-            held(early_rows, TILE),
-            held(early_rows, TILE),
-        ],
+        in_specs=[HBM] * 4,
+        out_specs=VMEM,
+        out_shape=held(2 * SLOTS, 5 * FIELD),
         scratch_shapes=[
             pltpu.VMEM((SLOTS * TILE, TILE), f32),
             pltpu.VMEM((SLOTS * 2 * TILE, TILE), f32),
@@ -770,19 +786,15 @@
             pltpu.VMEM((2, 5, TILE, TILE), f32),
             pltpu.VMEM((2, TILE, TILE), f32),
             pltpu.SemaphoreType.DMA((SLOTS // GROUP, 4)),
-            pltpu.SemaphoreType.DMA((2,)),
         ],
         compiler_params=pltpu.CompilerParams(vmem_limit_bytes=20 * 2**20),
-        name="extract",
-    )(plan, base, *tiles)
-    from_0, from_1 = trade_both(up, down, "gy")
-    early_0, early_1 = trade_both(early_0, early_1, "gy")
+    )(*tiles)
 
     first_rows = 4 * MOVERS
     dyn, fixed, *sends = call(
         settle_kernel,
-        in_specs=[SMEM, SMEM] + [VMEM] * 4 + [HBM] * 4,
-        out_specs=[VMEM] * 8,
+        in_specs=[SMEM, SMEM] + [VMEM] * 4,
+        out_specs=[VMEM] * 6,
         out_shape=[
             held(2 * SLOTS, 3 * FIELD),
             held(2 * SLOTS, 2 * FIELD),
@@ -790,13 +802,11 @@
             held(first_rows, TILE),
             held(first_rows, TILE),
             held(first_rows, TILE),
-            *[held(len(CHUNKS[0]) * STATE, TILE)] * 2,
         ],
-        scratch_shapes=[pltpu.SemaphoreType.DMA((2,))],
         compiler_params=pltpu.CompilerParams(vmem_limit_bytes=12 * 2**20),
-    )(plan, base, *on_core(nb, frames, from_0, from_1), *tiles)
-    got = exchange(*sends[:4])
-    chunks = [trade_both(*sends[4:], "gy")]
+    )(plan, base, *on_core(nb, frames, from_0, from_1))
+    got = exchange(*sends)
+    chunks = [trade_both(*cargo[2:4], "gy")]
     still = []
     trails = []
     for turn in range(3):
@@ -812,20 +822,18 @@
             (MOVERS, TILE),
             (MOVERS, TILE),
             (MOVERS, TILE),
-            *[(len(CHUNKS[turn + 1]) * STATE, TILE)] * 2,
         ]
         dyn, kept, trail, *sends = call(
             body,
-            in_specs=[SMEM, SMEM] + [VMEM] * (7 + len(still)) + [HBM] * 4,
+            in_specs=[SMEM] + [VMEM] * (7 + len(still)),
             out_specs=[VMEM] * len(shapes),
             out_shape=[held(*s) for s in shapes],
-            scratch_shapes=[pltpu.SemaphoreType.DMA((2,))],
-            compiler_params=pltpu.CompilerParams(vmem_limit_bytes=12 * 2**20),
-        )(plan, base, *on_core(nb, dyn, fixed, *still, *got), *tiles)
+                compiler_params=pltpu.CompilerParams(vmem_limit_bytes=12 * 2**20),
+        )(base, *on_core(nb, dyn, fixed, *still, *got))
         still = [kept]
         trails.append(trail)
-        got = exchange(*sends[:4])
-        chunks.append(trade_both(*sends[4:], "gy"))
+        got = exchange(*sends)
+        chunks.append(trade_both(*cargo[2 * turn + 4 : 2 * turn + 6], "gy"))
 
     late_0, late_1 = chunks[3]
     kept_inputs = on_core(

time: 158 us -> 145 us (0.918)
  the two profiles are of different devices: /device:TPU:32 before, /device:TPU:96 now
where the time goes in v6:
time: 145 us
  waiting for transfers between devices  67.4 us (46%)
  starting transfers between devices  38.4 us (26%)
  Pallas kernels  37.7 us (26%)
    ppermute x28, waiting for transfers between devices, trade(): return lax.ppermute(block, axis, pairs)  67.4 us
    ppermute x28, starting transfers between devices, trade(): return lax.ppermute(block, axis, pairs)  38.4 us
    pallas_call x1, Pallas kernels, shards(): call(tile_kernel, in_specs=[SMEM] * 4 + [VMEM] * len(kept_inputs) + [HBM]...  19.1 us
    pallas_call x1, Pallas kernels, shards(): call(extract_kernel, in_specs=[HBM] * 4, out_specs=VMEM, out_shape=held(2...  5.4 us
    pallas_call x1, Pallas kernels, shards(): call(pack_kernel, in_specs=[SMEM, SMEM] + [HBM] * 4, out_specs=[VMEM] * (...  4.58 us
    pallas_call x1, Pallas kernels, shards(): pl.pallas_call(late_kernel, in_specs=[SMEM] * 3 + [VMEM] * 4 + [HBM] * 2,...  4.53 us
  transfers between devices with their start and end apart: 28, of which 15 were waited for; matrix products, arithmetic and copies ran while one was open for 0% of the time, Pallas kernels for 20%

profile of v6, /device:TPU:96, one launch (start us, length us, event | category | flops | bytes accessed | tf_op | source)
XLA Modules:
  0.0 145.2 jit_solution(3055566336745079901)
XLA Ops:
  1.3 4.6 %shard_map.87 = (f32[8,10240]{1,0:T(8,128)S(1)}, f32[8,10240]{1,0:T(8,128)S(1)}, f32[640,128]{1,0:T(8,128)S(1)}, f32[640,128]{1,0:T(8,128)S(1)}, f32[640,128]{1,...) custom-call(s32[2,2,8]{2,1,0:T(2,128)S(1)} %bitcast.18, ...), custom_call_target="tpu_custom_call" | custom-call | tf_op jit(solution)/shard_map/pallas_call | solution.py:761
  8.0 6.0 %collective-permute-start.27 = (f32[2560,128]{1,0:T(8,128)S(1)}, f32[2560,128]{1,0:T(8,128)S(1)}, u32[]{:S(2)}, u32[]{:S(2)}) collective-permute-start(f32[2560,128]{1,0:T(8,128)S(1)} %get-tuple-element.87), channel_id=1, source_target_pairs={{0,15},{1,2},{2,1},{3,4},{4,3},{5,6},{6,5},{7,8},{8,7},{9,10},{10,... | collective-permute-start | bytes 3932168 | tf_op jit(solution)/shard_map/ppermute | solution.py:701
  14.1 2.5 %collective-permute-done.from_0 = f32[8,10240]{1,0:T(8,128)S(1)} collective-permute-done((f32[8,10240]{1,0:T(8,128)S(1)}, f32[8,10240]{1,0:T(8,128)S(1)}, u32[]{:S(2)}, u32[]{:S(2)}) %collective-permute-start) | collective-permute-done | bytes 327712 | tf_op jit(solution)/shard_map/ppermute | solution.py:701
  16.6 6.0 %collective-permute-start.19 = (f32[640,128]{1,0:T(8,128)S(1)}, f32[640,128]{1,0:T(8,128)S(1)}, u32[]{:S(2)}, u32[]{:S(2)}) collective-permute-start(f32[640,128]{1,0:T(8,128)S(1)} %get-tuple-element.77), channel_id=1, source_target_pairs={{0,15},{1,2},{2,1},{3,4},{4,3},{5,6},{6,5},{7,8},{8,7},{9,10},{10,... | collective-permute-start | bytes 983048 | tf_op jit(solution)/shard_map/ppermute | solution.py:701
  22.6 5.4 %shard_map.86.frames = f32[64,5120]{1,0:T(8,128)S(1)} custom-call(f32[4096,128]{1,0:T(8,128)} %bitcast.26, f32[8192,128]{1,0:T(8,128)} %bitcast.23, f32[4096,128]{1,0:T(8,128)} %bitcast.29, f32[4096,128]{1,0:T(8,128)} %bitcast.32), custom_call_target="tpu_custom_call" | custom-call | tf_op jit(solution)/shard_map/pallas_call | solution.py:776
  28.0 22.7 %collective-permute-done.1.from_1 = f32[8,10240]{1,0:T(8,128)S(1)} collective-permute-done((f32[8,10240]{1,0:T(8,128)S(1)}, f32[8,10240]{1,0:T(8,128)S(1)}, u32[]{:S(2)}, u32[]{:S(2)}) %collective-permute-start.1) | collective-permute-done | bytes 327712 | tf_op jit(solution)/shard_map/ppermute | solution.py:701
  53.4 3.2 %collective-permute-done.3.refs_5_ = f32[32,128]{1,0:T(8,128)S(1)} collective-permute-done((f32[32,128]{1,0:T(8,128)S(1)}, f32[32,128]{1,0:T(8,128)S(1)}, u32[]{:S(2)}, u32[]{:S(2)}) %collective-permute-start.3) | collective-permute-done | bytes 16416 | tf_op jit(solution)/shard_map/ppermute | solution.py:701
  56.5 3.7 %collective-permute-done.4.refs_6_ = f32[32,128]{1,0:T(8,128)S(1)} collective-permute-done((f32[32,128]{1,0:T(8,128)S(1)}, f32[32,128]{1,0:T(8,128)S(1)}, u32[]{:S(2)}, u32[]{:S(2)}) %collective-permute-start.4) | collective-permute-done | bytes 16416 | tf_op jit(solution)/shard_map/ppermute | solution.py:701
  60.3 5.3 %collective-permute-start.5 = (f32[32,128]{1,0:T(8,128)S(1)}, f32[32,128]{1,0:T(8,128)S(1)}, u32[]{:S(2)}, u32[]{:S(2)}) collective-permute-start(f32[32,128]{1,0:T(8,128)S(1)} %get-tuple-element.54), channel_id=1, source_target_pairs={{0,15},{1,2},{2,1},{3,4},{4,3},{5,6},{6,5},{7,8},{8,7},{9,10},{10,... | collective-permute-start | bytes 49160 | tf_op jit(solution)/shard_map/ppermute | solution.py:701
  65.6 1.7 %collective-permute-done.5.refs_7_ = f32[32,128]{1,0:T(8,128)S(1)} collective-permute-done((f32[32,128]{1,0:T(8,128)S(1)}, f32[32,128]{1,0:T(8,128)S(1)}, u32[]{:S(2)}, u32[]{:S(2)}) %collective-permute-start.5) | collective-permute-done | bytes 16416 | tf_op jit(solution)/shard_map/ppermute | solution.py:701
  69.7 5.3 %collective-permute-start.9 = (f32[8,128]{1,0:T(8,128)S(1)}, f32[8,128]{1,0:T(8,128)S(1)}, u32[]{:S(2)}, u32[]{:S(2)}) collective-permute-start(f32[8,128]{1,0:T(8,128)S(1)} %get-tuple-element.60), channel_id=1, source_target_pairs={{0,15},{1,2},{2,1},{3,4},{4,3},{5,6},{6,5},{7,8},{8,7},{9,10},{10,... | collective-permute-start | bytes 12296 | tf_op jit(solution)/shard_map/ppermute | solution.py:701
  75.1 2.6 %collective-permute-start.21 = (f32[640,128]{1,0:T(8,128)S(1)}, f32[640,128]{1,0:T(8,128)S(1)}, u32[]{:S(2)}, u32[]{:S(2)}) collective-permute-start(f32[640,128]{1,0:T(8,128)S(1)} %get-tuple-element.79), channel_id=1, source_target_pairs={{0,15},{1,2},{2,1},{3,4},{4,3},{5,6},{6,5},{7,8},{8,7},{9,10},{10,... | collective-permute-start | bytes 983048 | tf_op jit(solution)/shard_map/ppermute | solution.py:701
  78.6 7.0 %collective-permute-done.20.a_0 = f32[640,128]{1,0:T(8,128)S(1)} collective-permute-done((f32[640,128]{1,0:T(8,128)S(1)}, f32[640,128]{1,0:T(8,128)S(1)}, u32[]{:S(2)}, u32[]{:S(2)}) %collective-permute-start.20) | collective-permute-done | bytes 327712 | tf_op jit(solution)/shard_map/ppermute | solution.py:701
  85.6 2.6 %collective-permute-done.21.a_1 = f32[640,128]{1,0:T(8,128)S(1)} collective-permute-done((f32[640,128]{1,0:T(8,128)S(1)}, f32[640,128]{1,0:T(8,128)S(1)}, u32[]{:S(2)}, u32[]{:S(2)}) %collective-permute-start.21) | collective-permute-done | bytes 327712 | tf_op jit(solution)/shard_map/ppermute | solution.py:701
  88.7 3.2 %collective-permute-done.22.b_0 = f32[640,128]{1,0:T(8,128)S(1)} collective-permute-done((f32[640,128]{1,0:T(8,128)S(1)}, f32[640,128]{1,0:T(8,128)S(1)}, u32[]{:S(2)}, u32[]{:S(2)}) %collective-permute-start.22) | collective-permute-done | bytes 327712 | tf_op jit(solution)/shard_map/ppermute | solution.py:701
  92.1 1.9 %collective-permute-start.13 = (f32[8,128]{1,0:T(8,128)S(1)}, f32[8,128]{1,0:T(8,128)S(1)}, u32[]{:S(2)}, u32[]{:S(2)}) collective-permute-start(f32[8,128]{1,0:T(8,128)S(1)} %get-tuple-element.66), channel_id=1, source_target_pairs={{0,15},{1,2},{2,1},{3,4},{4,3},{5,6},{6,5},{7,8},{8,7},{9,10},{10,... | collective-permute-start | bytes 12296 | tf_op jit(solution)/shard_map/ppermute | solution.py:701
  94.0 3.5 %collective-permute-start.23 = (f32[640,128]{1,0:T(8,128)S(1)}, f32[640,128]{1,0:T(8,128)S(1)}, u32[]{:S(2)}, u32[]{:S(2)}) collective-permute-start(f32[640,128]{1,0:T(8,128)S(1)} %get-tuple-element.81), channel_id=1, source_target_pairs={{0,15},{1,2},{2,1},{3,4},{4,3},{5,6},{6,5},{7,8},{8,7},{9,10},{10,... | collective-permute-start | bytes 983048 | tf_op jit(solution)/shard_map/ppermute | solution.py:701
  99.1 1.9 %collective-permute-start.25 = (f32[640,128]{1,0:T(8,128)S(1)}, f32[640,128]{1,0:T(8,128)S(1)}, u32[]{:S(2)}, u32[]{:S(2)}) collective-permute-start(f32[640,128]{1,0:T(8,128)S(1)} %get-tuple-element.83), channel_id=1, source_target_pairs={{0,15},{1,2},{2,1},{3,4},{4,3},{5,6},{6,5},{7,8},{8,7},{9,10},{10,... | collective-permute-start | bytes 983048 | tf_op jit(solution)/shard_map/ppermute | solution.py:701
  101.6 6.3 %collective-permute-done.23.b_1 = f32[640,128]{1,0:T(8,128)S(1)} collective-permute-done((f32[640,128]{1,0:T(8,128)S(1)}, f32[640,128]{1,0:T(8,128)S(1)}, u32[]{:S(2)}, u32[]{:S(2)}) %collective-permute-start.23) | collective-permute-done | bytes 327712 | tf_op jit(solution)/shard_map/ppermute | solution.py:701
  108.5 5.9 %collective-permute-done.25.c_1 = f32[640,128]{1,0:T(8,128)S(1)} collective-permute-done((f32[640,128]{1,0:T(8,128)S(1)}, f32[640,128]{1,0:T(8,128)S(1)}, u32[]{:S(2)}, u32[]{:S(2)}) %collective-permute-start.25) | collective-permute-done | bytes 327712 | tf_op jit(solution)/shard_map/ppermute | solution.py:701
  114.4 2.0 %collective-permute-start.17 = (f32[8,128]{1,0:T(8,128)S(1)}, f32[8,128]{1,0:T(8,128)S(1)}, u32[]{:S(2)}, u32[]{:S(2)}) collective-permute-start(f32[8,128]{1,0:T(8,128)S(1)} %get-tuple-element.72), channel_id=1, source_target_pairs={{0,15},{1,2},{2,1},{3,4},{4,3},{5,6},{6,5},{7,8},{8,7},{9,10},{10,... | collective-permute-start | bytes 12296 | tf_op jit(solution)/shard_map/ppermute | solution.py:701
  118.0 3.3 %collective-permute-done.17.y_1 = f32[8,128]{1,0:T(8,128)S(1)} collective-permute-done((f32[8,128]{1,0:T(8,128)S(1)}, f32[8,128]{1,0:T(8,128)S(1)}, u32[]{:S(2)}, u32[]{:S(2)}) %collective-permute-start.17) | collective-permute-done | bytes 4128 | tf_op jit(solution)/shard_map/ppermute | solution.py:701
  121.4 19.1 %shard_map.92 = (f32[4096,128]{1,0:T(8,128)}, f32[8192,128]{1,0:T(8,128)}, f32[10,32,128]{2,1,0:T(8,128)S(1)}, f32[3,128,128]{2,1,0:T(8,128)S(1)}) custom-call(s32[2,2,8]{2,1,0:T(2,128)S(1)} %bitcast.20, s32[1]{0:T(128)} %bitcast.2.base.refs_0_, s32[32]{0:T(128)S(1)} %copy-done.3, s32[4,32]{1,0:T(4,128)S(1)} %bitcast.15, s32[4,32]{1,0:T(4,128)S(1)} %bitcast.16, ...), custom_call_target="tpu_custom_call" | custom-call | tf_op jit(solution)/shard_map/pallas_call | solution.py:842
  140.5 4.5 %late_tiles.1 = (f32[4096,128]{1,0:T(8,128)}, f32[8192,128]{1,0:T(8,128)}) custom-call(s32[2,2,8]{2,1,0:T(2,128)S(1)} %bitcast.21, s32[1]{0:T(128)} %bitcast.2.base.refs_0_, s32[4,32]{1,0:T(4,128)S(1)} %bitcast.17, f32[10,32,128]{2,1,0:T(8,128)S(1)} %get-tuple-element.84.edges, ...), custom_call_target="tpu_custom_call", output_to_operand_aliasing={{0}: (7, {}), {1}: (8, {})} | custom-call | tf_op jit(solution)/shard_map/late_tiles/pallas_call | solution.py:862
  (48 shorter events, 13.9 us)
Async XLA Ops:
  5.9 10.7 %collective-permute-start = (f32[8,10240]{1,0:T(8,128)S(1)}, f32[8,10240]{1,0:T(8,128)S(1)}, u32[]{:S(2)}, u32[]{:S(2)}) collective-permute-start(f32[8,10240]{1,0:T(8,128)S(1)} %get-tuple-element.47), channel_id=1, source_target_pairs={{0,1},{1,0},{2,3},{3,2},{4,5},{5,4},{6,7},{7,6},{8,9},{9,8},{10,11... | collective-permute-start | bytes 983048 | tf_op jit(solution)/shard_map/ppermute | solution.py:701
  7.2 133.3 %collective-permute-start.26 = (f32[2560,128]{1,0:T(8,128)S(1)}, f32[2560,128]{1,0:T(8,128)S(1)}, u32[]{:S(2)}, u32[]{:S(2)}) collective-permute-start(f32[2560,128]{1,0:T(8,128)S(1)} %get-tuple-element.86), channel_id=1, source_target_pairs={{0,1},{1,0},{2,3},{3,2},{4,5},{5,4},{6,7},{7,6},{8,9},{9,8},{10,11... | collective-permute-start | bytes 3932168 | tf_op jit(solution)/shard_map/ppermute | solution.py:701
  8.0 132.5 %collective-permute-start.27 = (f32[2560,128]{1,0:T(8,128)S(1)}, f32[2560,128]{1,0:T(8,128)S(1)}, u32[]{:S(2)}, u32[]{:S(2)}) collective-permute-start(f32[2560,128]{1,0:T(8,128)S(1)} %get-tuple-element.87), channel_id=1, source_target_pairs={{0,15},{1,2},{2,1},{3,4},{4,3},{5,6},{6,5},{7,8},{8,7},{9,10},{10,... | collective-permute-start | bytes 3932168 | tf_op jit(solution)/shard_map/ppermute | solution.py:701
  14.0 36.6 %collective-permute-start.1 = (f32[8,10240]{1,0:T(8,128)S(1)}, f32[8,10240]{1,0:T(8,128)S(1)}, u32[]{:S(2)}, u32[]{:S(2)}) collective-permute-start(f32[8,10240]{1,0:T(8,128)S(1)} %get-tuple-element.48), channel_id=1, source_target_pairs={{0,15},{1,2},{2,1},{3,4},{4,3},{5,6},{6,5},{7,8},{8,7},{9,10},{10,... | collective-permute-start | bytes 983048 | tf_op jit(solution)/shard_map/ppermute | solution.py:701
  14.1 54.5 %collective-permute-start.18 = (f32[640,128]{1,0:T(8,128)S(1)}, f32[640,128]{1,0:T(8,128)S(1)}, u32[]{:S(2)}, u32[]{:S(2)}) collective-permute-start(f32[640,128]{1,0:T(8,128)S(1)} %get-tuple-element.76), channel_id=1, source_target_pairs={{0,1},{1,0},{2,3},{3,2},{4,5},{5,4},{6,7},{7,6},{8,9},{9,8},{10,11... | collective-permute-start | bytes 983048 | tf_op jit(solution)/shard_map/ppermute | solution.py:701
  16.6 52.1 %collective-permute-start.19 = (f32[640,128]{1,0:T(8,128)S(1)}, f32[640,128]{1,0:T(8,128)S(1)}, u32[]{:S(2)}, u32[]{:S(2)}) collective-permute-start(f32[640,128]{1,0:T(8,128)S(1)} %get-tuple-element.77), channel_id=1, source_target_pairs={{0,15},{1,2},{2,1},{3,4},{4,3},{5,6},{6,5},{7,8},{8,7},{9,10},{10,... | collective-permute-start | bytes 983048 | tf_op jit(solution)/shard_map/ppermute | solution.py:701
  56.5 3.7 %collective-permute-start.4 = (f32[32,128]{1,0:T(8,128)S(1)}, f32[32,128]{1,0:T(8,128)S(1)}, u32[]{:S(2)}, u32[]{:S(2)}) collective-permute-start(f32[32,128]{1,0:T(8,128)S(1)} %get-tuple-element.53), channel_id=1, source_target_pairs={{0,1},{1,0},{2,3},{3,2},{4,5},{5,4},{6,7},{7,6},{8,9},{9,8},{10,11... | collective-permute-start | bytes 49160 | tf_op jit(solution)/shard_map/ppermute | solution.py:701
  60.3 7.1 %collective-permute-start.5 = (f32[32,128]{1,0:T(8,128)S(1)}, f32[32,128]{1,0:T(8,128)S(1)}, u32[]{:S(2)}, u32[]{:S(2)}) collective-permute-start(f32[32,128]{1,0:T(8,128)S(1)} %get-tuple-element.54), channel_id=1, source_target_pairs={{0,15},{1,2},{2,1},{3,4},{4,3},{5,6},{6,5},{7,8},{8,7},{9,10},{10,... | collective-permute-start | bytes 49160 | tf_op jit(solution)/shard_map/ppermute | solution.py:701
  68.6 6.5 %collective-permute-start.7 = (f32[8,128]{1,0:T(8,128)S(1)}, f32[8,128]{1,0:T(8,128)S(1)}, u32[]{:S(2)}, u32[]{:S(2)}) collective-permute-start(f32[8,128]{1,0:T(8,128)S(1)} %get-tuple-element.58), channel_id=1, source_target_pairs={{0,112},{16,32},{32,16},{48,64},{64,48},{80,96},{96,80},{112,0},{1... | collective-permute-start | bytes 12296 | tf_op jit(solution)/shard_map/ppermute | solution.py:701
  68.7 6.4 %collective-permute-start.8 = (f32[8,128]{1,0:T(8,128)S(1)}, f32[8,128]{1,0:T(8,128)S(1)}, u32[]{:S(2)}, u32[]{:S(2)}) collective-permute-start(f32[8,128]{1,0:T(8,128)S(1)} %get-tuple-element.59), channel_id=1, source_target_pairs={{0,1},{1,0},{2,3},{3,2},{4,5},{5,4},{6,7},{7,6},{8,9},{9,8},{10,11... | collective-permute-start | bytes 12296 | tf_op jit(solution)/shard_map/ppermute | solution.py:701
  69.7 8.0 %collective-permute-start.9 = (f32[8,128]{1,0:T(8,128)S(1)}, f32[8,128]{1,0:T(8,128)S(1)}, u32[]{:S(2)}, u32[]{:S(2)}) collective-permute-start(f32[8,128]{1,0:T(8,128)S(1)} %get-tuple-element.60), channel_id=1, source_target_pairs={{0,15},{1,2},{2,1},{3,4},{4,3},{5,6},{6,5},{7,8},{8,7},{9,10},{10,... | collective-permute-start | bytes 12296 | tf_op jit(solution)/shard_map/ppermute | solution.py:701
  75.1 10.6 %collective-permute-start.20 = (f32[640,128]{1,0:T(8,128)S(1)}, f32[640,128]{1,0:T(8,128)S(1)}, u32[]{:S(2)}, u32[]{:S(2)}) collective-permute-start(f32[640,128]{1,0:T(8,128)S(1)} %get-tuple-element.78), channel_id=1, source_target_pairs={{0,1},{1,0},{2,3},{3,2},{4,5},{5,4},{6,7},{7,6},{8,9},{9,8},{10,11... | collective-permute-start | bytes 983048 | tf_op jit(solution)/shard_map/ppermute | solution.py:701
  75.1 13.2 %collective-permute-start.21 = (f32[640,128]{1,0:T(8,128)S(1)}, f32[640,128]{1,0:T(8,128)S(1)}, u32[]{:S(2)}, u32[]{:S(2)}) collective-permute-start(f32[640,128]{1,0:T(8,128)S(1)} %get-tuple-element.79), channel_id=1, source_target_pairs={{0,15},{1,2},{2,1},{3,4},{4,3},{5,6},{6,5},{7,8},{8,7},{9,10},{10,... | collective-permute-start | bytes 983048 | tf_op jit(solution)/shard_map/ppermute | solution.py:701
  77.7 14.1 %collective-permute-start.22 = (f32[640,128]{1,0:T(8,128)S(1)}, f32[640,128]{1,0:T(8,128)S(1)}, u32[]{:S(2)}, u32[]{:S(2)}) collective-permute-start(f32[640,128]{1,0:T(8,128)S(1)} %get-tuple-element.80), channel_id=1, source_target_pairs={{0,1},{1,0},{2,3},{3,2},{4,5},{5,4},{6,7},{7,6},{8,9},{9,8},{10,11... | collective-permute-start | bytes 983048 | tf_op jit(solution)/shard_map/ppermute | solution.py:701
  85.6 6.5 %collective-permute-start.10 = (f32[8,128]{1,0:T(8,128)S(1)}, f32[8,128]{1,0:T(8,128)S(1)}, u32[]{:S(2)}, u32[]{:S(2)}) collective-permute-start(f32[8,128]{1,0:T(8,128)S(1)} %get-tuple-element.63), channel_id=1, source_target_pairs={{0,16},{16,0},{32,48},{48,32},{64,80},{80,64},{96,112},{112,96},{1... | collective-permute-start | bytes 12296 | tf_op jit(solution)/shard_map/ppermute | solution.py:701
  88.2 5.8 %collective-permute-start.11 = (f32[8,128]{1,0:T(8,128)S(1)}, f32[8,128]{1,0:T(8,128)S(1)}, u32[]{:S(2)}, u32[]{:S(2)}) collective-permute-start(f32[8,128]{1,0:T(8,128)S(1)} %get-tuple-element.64), channel_id=1, source_target_pairs={{0,112},{16,32},{32,16},{48,64},{64,48},{80,96},{96,80},{112,0},{1... | collective-permute-start | bytes 12296 | tf_op jit(solution)/shard_map/ppermute | solution.py:701
  91.8 5.6 %collective-permute-start.12 = (f32[8,128]{1,0:T(8,128)S(1)}, f32[8,128]{1,0:T(8,128)S(1)}, u32[]{:S(2)}, u32[]{:S(2)}) collective-permute-start(f32[8,128]{1,0:T(8,128)S(1)} %get-tuple-element.65), channel_id=1, source_target_pairs={{0,1},{1,0},{2,3},{3,2},{4,5},{5,4},{6,7},{7,6},{8,9},{9,8},{10,11... | collective-permute-start | bytes 12296 | tf_op jit(solution)/shard_map/ppermute | solution.py:701
  92.1 6.9 %collective-permute-start.13 = (f32[8,128]{1,0:T(8,128)S(1)}, f32[8,128]{1,0:T(8,128)S(1)}, u32[]{:S(2)}, u32[]{:S(2)}) collective-permute-start(f32[8,128]{1,0:T(8,128)S(1)} %get-tuple-element.66), channel_id=1, source_target_pairs={{0,15},{1,2},{2,1},{3,4},{4,3},{5,6},{6,5},{7,8},{8,7},{9,10},{10,... | collective-permute-start | bytes 12296 | tf_op jit(solution)/shard_map/ppermute | solution.py:701
  94.0 13.9 %collective-permute-start.23 = (f32[640,128]{1,0:T(8,128)S(1)}, f32[640,128]{1,0:T(8,128)S(1)}, u32[]{:S(2)}, u32[]{:S(2)}) collective-permute-start(f32[640,128]{1,0:T(8,128)S(1)} %get-tuple-element.81), channel_id=1, source_target_pairs={{0,15},{1,2},{2,1},{3,4},{4,3},{5,6},{6,5},{7,8},{8,7},{9,10},{10,... | collective-permute-start | bytes 983048 | tf_op jit(solution)/shard_map/ppermute | solution.py:701
  97.5 10.4 %collective-permute-start.24 = (f32[640,128]{1,0:T(8,128)S(1)}, f32[640,128]{1,0:T(8,128)S(1)}, u32[]{:S(2)}, u32[]{:S(2)}) collective-permute-start(f32[640,128]{1,0:T(8,128)S(1)} %get-tuple-element.82), channel_id=1, source_target_pairs={{0,1},{1,0},{2,3},{3,2},{4,5},{5,4},{6,7},{7,6},{8,9},{9,8},{10,11... | collective-permute-start | bytes 983048 | tf_op jit(solution)/shard_map/ppermute | solution.py:701
  99.1 15.4 %collective-permute-start.25 = (f32[640,128]{1,0:T(8,128)S(1)}, f32[640,128]{1,0:T(8,128)S(1)}, u32[]{:S(2)}, u32[]{:S(2)}) collective-permute-start(f32[640,128]{1,0:T(8,128)S(1)} %get-tuple-element.83), channel_id=1, source_target_pairs={{0,15},{1,2},{2,1},{3,4},{4,3},{5,6},{6,5},{7,8},{8,7},{9,10},{10,... | collective-permute-start | bytes 983048 | tf_op jit(solution)/shard_map/ppermute | solution.py:701
  107.9 6.5 %collective-permute-start.14 = (f32[8,128]{1,0:T(8,128)S(1)}, f32[8,128]{1,0:T(8,128)S(1)}, u32[]{:S(2)}, u32[]{:S(2)}) collective-permute-start(f32[8,128]{1,0:T(8,128)S(1)} %get-tuple-element.69), channel_id=1, source_target_pairs={{0,16},{16,0},{32,48},{48,32},{64,80},{80,64},{96,112},{112,96},{1... | collective-permute-start | bytes 12296 | tf_op jit(solution)/shard_map/ppermute | solution.py:701
  107.9 8.6 %collective-permute-start.15 = (f32[8,128]{1,0:T(8,128)S(1)}, f32[8,128]{1,0:T(8,128)S(1)}, u32[]{:S(2)}, u32[]{:S(2)}) collective-permute-start(f32[8,128]{1,0:T(8,128)S(1)} %get-tuple-element.70), channel_id=1, source_target_pairs={{0,112},{16,32},{32,16},{48,64},{64,48},{80,96},{96,80},{112,0},{1... | collective-permute-start | bytes 12296 | tf_op jit(solution)/shard_map/ppermute | solution.py:701
  114.4 6.9 %collective-permute-start.17 = (f32[8,128]{1,0:T(8,128)S(1)}, f32[8,128]{1,0:T(8,128)S(1)}, u32[]{:S(2)}, u32[]{:S(2)}) collective-permute-start(f32[8,128]{1,0:T(8,128)S(1)} %get-tuple-element.72), channel_id=1, source_target_pairs={{0,15},{1,2},{2,1},{3,4},{4,3},{5,6},{6,5},{7,8},{8,7},{9,10},{10,... | collective-permute-start | bytes 12296 | tf_op jit(solution)/shard_map/ppermute | solution.py:701
  (8 other events, 132.2 us)

commit v7 on v6

--- a/solution.py
+++ b/solution.py
@@ -19,8 +19,9 @@
 LOADS = (EARLY,) + CHUNKS
 GROUP = 8
 GY = 16
-BUFFERS = 6
-OUT_BUFFERS = 4
+SIDE = 2
+BUFFERS = SIDE + 4
+OUT_BUFFERS = 2 * SIDE
 
 gravity = 9.81
 step_time = 0.25
@@ -409,7 +410,7 @@
 
 def run_tiles(
     queue, origin, count, moves_sources, tiles, nb_s, edges, columns, outs, before_loop,
-    inbox, outbox, in_sem, out_sem, *spaces,
+    inbox, outbox, in_sem, out_sem, *spaces, direct=None,
 ):
     depth, discharge, bed, friction = tiles
     depth_out, flow_out = outs
@@ -432,11 +433,13 @@
                 pltpu.make_async_copy(bed.at[one], box.at[pl.ds(3 * TILE, TILE)], sem).start()
                 pltpu.make_async_copy(friction.at[one], box.at[pl.ds(4 * TILE, TILE)], sem).start()
 
-        for code, ref, at in moves_sources:
-
-            @pl.when(kind == code)
-            def _():
-                pltpu.make_async_copy(ref.at[pl.ds(at, STATE)], box, sem).start()
+        @pl.when(kind != 0)
+        def _():
+            for code, ref, at in moves_sources:
+
+                @pl.when(kind == code)
+                def _():
+                    pltpu.make_async_copy(ref.at[pl.ds(at, STATE)], box, sem).start()
 
     def arrived(buf):
         box = inbox.at[buf]
@@ -454,14 +457,15 @@
         pltpu.make_async_copy(box, box, out_sem.at[buf]).wait()
 
     def prime():
-        for j in range(BUFFERS - 2):
+        for j in range(BUFFERS - SIDE):
 
             @pl.when(j < count)
             def _():
                 fetch(j)
 
-    prime()
-    before_loop()
+    if direct is None:
+        prime()
+        before_loop()
     part_rows = 32
     parts = TILE // part_rows
     lane = iota((part_rows, TILE), 1)
@@ -479,11 +483,8 @@
         def _():
             sent(j % OUT_BUFFERS)
 
-    def work(j, space):
+    def work(t, box, out, space):
         water, stream_x, stream_y, slope_x, slope_y, rub_x, rub_y = space
-        t = queue[jnp.minimum(j, count - 1)]
-        box = inbox.at[j % BUFFERS]
-        out = outbox.at[j % OUT_BUFFERS]
         wall_x = nb_s[1, t] < 0
         wall_y = nb_s[3, t] < 0
 
@@ -546,20 +547,22 @@
                 else:
                     out[rows, :] = h_new * UNIT_H
 
-    def two_tiles(pair, carry):
-        for i in range(2):
-            j = 2 * pair + i
-
-            @pl.when(j + BUFFERS - 2 < count)
+    def side_by_side(turn, carry):
+        for i in range(SIDE):
+            j = SIDE * turn + i
+
+            @pl.when(j + BUFFERS - SIDE < count)
             def _():
-                fetch(j + BUFFERS - 2)
+                fetch(j + BUFFERS - SIDE)
 
             ready(j)
-        half = len(spaces) // 2
-        for i in range(2):
-            work(2 * pair + i, spaces[i * half : (i + 1) * half])
-        for i in range(2):
-            j = 2 * pair + i
+        share = len(spaces) // SIDE
+        for i in range(SIDE):
+            j = SIDE * turn + i
+            t = queue[jnp.minimum(j, count - 1)]
+            work(t, inbox.at[j % BUFFERS], outbox.at[j % OUT_BUFFERS], spaces[i * share : (i + 1) * share])
+        for i in range(SIDE):
+            j = SIDE * turn + i
 
             @pl.when(j < count)
             def _():
@@ -567,7 +570,10 @@
 
         return carry
 
-    lax.fori_loop(0, (count + 1) // 2, two_tiles, 0)
+    if direct is not None:
+        direct(work, send, sent, outbox, spaces)
+        return
+    lax.fori_loop(0, (count + SIDE - 1) // SIDE, side_by_side, 0)
     for b in range(OUT_BUFFERS):
 
         @pl.when(b < count)
@@ -674,19 +680,49 @@
 
 def late_kernel(
     moves, base, nb_s, edges, columns, late_0, late_1, depth_in, flow_in,
-    depth_out, flow_out, queue, origin, size, *scratch,
+    depth_out, flow_out, *scratch,
 ):
-    size[0] = 0
-
-    def enqueue(t, code):
-        queue[size[0]] = t
-        origin[t] = code
-        size[0] = size[0] + 1
-
-    note_arrivals(LATE, moves, base, enqueue)
+    chunks = (late_0, late_1)
+
+    def lander(i, pairing):
+        return moves[way_of(base, pairing), 1, LATE[0] + i]
+
+    def each_pair(work, send, sent, outbox, spaces):
+        share = len(spaces) // 2
+
+        def two(i, carry):
+            for pairing in range(2):
+                @pl.when((i >= 2) & (lander(jnp.maximum(i - 2, 0), pairing) >= 0))
+                def _():
+                    sent((2 * i + pairing) % 4)
+
+            for pairing in range(2):
+                t = jnp.clip(lander(i, pairing) - base[0], 0, SLOTS - 1)
+                box = chunks[pairing].at[pl.ds(pl.multiple_of(i * STATE, STATE), STATE)]
+                work(t, box, outbox.at[(2 * i + pairing) % 4], spaces[pairing * share : (pairing + 1) * share])
+            for pairing in range(2):
+
+                @pl.when(lander(i, pairing) >= 0)
+                def _():
+                    send(lander(i, pairing) - base[0], (2 * i + pairing) % 4)
+
+            return carry
+
+        used = 0
+        for i in range(len(LATE)):
+            used = used + jnp.where((lander(i, 0) >= 0) | (lander(i, 1) >= 0), 1, 0)
+        lax.fori_loop(0, used, two, 0)
+        for back in range(2):
+            for pairing in range(2):
+                i = used - 1 - back
+
+                @pl.when((i >= 0) & (lander(jnp.maximum(i, 0), pairing) >= 0))
+                def _():
+                    sent((2 * i + pairing) % 4)
+
     run_tiles(
-        queue, origin, size[0], chunk_sources(LATE, late_0, late_1), (None,) * 4, nb_s, edges, columns,
-        (depth_out, flow_out), lambda: None, *scratch,
+        None, None, 0, (), (None,) * 4, nb_s, edges, columns, (depth_out, flow_out), None, *scratch,
+        direct=each_pair,
     )
 
 
@@ -740,8 +776,7 @@
         pltpu.VMEM((OUT_BUFFERS, 3 * TILE, TILE), f32),
         pltpu.SemaphoreType.DMA((BUFFERS,)),
         pltpu.SemaphoreType.DMA((OUT_BUFFERS,)),
-        *space,
-        *space,
+        *(space * SIDE),
     ]
 
 
@@ -865,12 +900,7 @@
         out_specs=[HBM, HBM],
         out_shape=[struct(SLOTS * TILE, TILE), struct(SLOTS * 2 * TILE, TILE)],
         input_output_aliases={7: 0, 8: 1},
-        scratch_shapes=[
-            pltpu.SMEM((SLOTS,), i32),
-            pltpu.SMEM((SLOTS,), i32),
-            pltpu.SMEM((1,), i32),
-            *loop_scratch(),
-        ],
+        scratch_shapes=loop_scratch(),
         compiler_params=pltpu.CompilerParams(vmem_limit_bytes=12 * 2**20),
         name="late_tiles",
     )(plan, base, nb, *on_core(edges, columns, late_0, late_1), new_depth, new_flow)

time: 145 us -> 147 us (1.014)
    pallas_call x1, Pallas kernels: 4.53 us -> 6.05 us  [shards(): pl.pallas_call(late_kernel, in_specs=[SMEM] * 3 + [VMEM] * 4 + [HBM] * 2,...]
  transfers between devices with their start and end apart: 28 -> 28, of which waited for: 15 -> 15; matrix products, arithmetic and copies ran while one was open for 0% -> 0% of each run, Pallas kernels for 20% -> 19%
where the time goes in v7:
time: 147 us; the launch traced here: 146 us
  waiting for transfers between devices  67.4 us (46%)
  Pallas kernels  38.9 us (26%)
  starting transfers between devices  38.4 us (26%)
    ppermute x28, waiting for transfers between devices, trade(): return lax.ppermute(block, axis, pairs)  67.4 us
    ppermute x28, starting transfers between devices, trade(): return lax.ppermute(block, axis, pairs)  38.4 us
    pallas_call x1, Pallas kernels, shards(): call(tile_kernel, in_specs=[SMEM] * 4 + [VMEM] * len(kept_inputs) + [HBM]...  18.7 us
    pallas_call x1, Pallas kernels, shards(): pl.pallas_call(late_kernel, in_specs=[SMEM] * 3 + [VMEM] * 4 + [HBM] * 2,...  6.05 us
    pallas_call x1, Pallas kernels, shards(): call(extract_kernel, in_specs=[HBM] * 4, out_specs=VMEM, out_shape=held(2...  5.4 us
    pallas_call x1, Pallas kernels, shards(): call(pack_kernel, in_specs=[SMEM, SMEM] + [HBM] * 4, out_specs=[VMEM] * (...  4.58 us
  transfers between devices with their start and end apart: 28, of which 15 were waited for; matrix products, arithmetic and copies ran while one was open for 0% of the time, Pallas kernels for 19%

profile of v7, /device:TPU:96, one launch (start us, length us, event | category | flops | bytes accessed | tf_op | source)
XLA Modules:
  0.0 146.3 jit_solution(3447874187650614256)
XLA Ops:
  1.3 4.6 %shard_map.87 = (f32[8,10240]{1,0:T(8,128)S(1)}, f32[8,10240]{1,0:T(8,128)S(1)}, f32[640,128]{1,0:T(8,128)S(1)}, f32[640,128]{1,0:T(8,128)S(1)}, f32[640,128]{1,...) custom-call(s32[2,2,8]{2,1,0:T(2,128)S(1)} %bitcast.18, ...), custom_call_target="tpu_custom_call" | custom-call | tf_op jit(solution)/shard_map/pallas_call | solution.py:796
  8.0 6.0 %collective-permute-start.27 = (f32[2560,128]{1,0:T(8,128)S(1)}, f32[2560,128]{1,0:T(8,128)S(1)}, u32[]{:S(2)}, u32[]{:S(2)}) collective-permute-start(f32[2560,128]{1,0:T(8,128)S(1)} %get-tuple-element.87), channel_id=1, source_target_pairs={{0,15},{1,2},{2,1},{3,4},{4,3},{5,6},{6,5},{7,8},{8,7},{9,10},{10,... | collective-permute-start | bytes 3932168 | tf_op jit(solution)/shard_map/ppermute | solution.py:737
  14.1 2.5 %collective-permute-done.from_0 = f32[8,10240]{1,0:T(8,128)S(1)} collective-permute-done((f32[8,10240]{1,0:T(8,128)S(1)}, f32[8,10240]{1,0:T(8,128)S(1)}, u32[]{:S(2)}, u32[]{:S(2)}) %collective-permute-start) | collective-permute-done | bytes 327712 | tf_op jit(solution)/shard_map/ppermute | solution.py:737
  16.6 6.0 %collective-permute-start.19 = (f32[640,128]{1,0:T(8,128)S(1)}, f32[640,128]{1,0:T(8,128)S(1)}, u32[]{:S(2)}, u32[]{:S(2)}) collective-permute-start(f32[640,128]{1,0:T(8,128)S(1)} %get-tuple-element.77), channel_id=1, source_target_pairs={{0,15},{1,2},{2,1},{3,4},{4,3},{5,6},{6,5},{7,8},{8,7},{9,10},{10,... | collective-permute-start | bytes 983048 | tf_op jit(solution)/shard_map/ppermute | solution.py:737
  22.6 5.4 %shard_map.86.frames = f32[64,5120]{1,0:T(8,128)S(1)} custom-call(f32[4096,128]{1,0:T(8,128)} %bitcast.26, f32[8192,128]{1,0:T(8,128)} %bitcast.23, f32[4096,128]{1,0:T(8,128)} %bitcast.29, f32[4096,128]{1,0:T(8,128)} %bitcast.32), custom_call_target="tpu_custom_call" | custom-call | tf_op jit(solution)/shard_map/pallas_call | solution.py:811
  28.0 22.7 %collective-permute-done.1.from_1 = f32[8,10240]{1,0:T(8,128)S(1)} collective-permute-done((f32[8,10240]{1,0:T(8,128)S(1)}, f32[8,10240]{1,0:T(8,128)S(1)}, u32[]{:S(2)}, u32[]{:S(2)}) %collective-permute-start.1) | collective-permute-done | bytes 327712 | tf_op jit(solution)/shard_map/ppermute | solution.py:737
  53.4 3.2 %collective-permute-done.3.refs_5_ = f32[32,128]{1,0:T(8,128)S(1)} collective-permute-done((f32[32,128]{1,0:T(8,128)S(1)}, f32[32,128]{1,0:T(8,128)S(1)}, u32[]{:S(2)}, u32[]{:S(2)}) %collective-permute-start.3) | collective-permute-done | bytes 16416 | tf_op jit(solution)/shard_map/ppermute | solution.py:737
  56.5 3.7 %collective-permute-done.4.refs_6_ = f32[32,128]{1,0:T(8,128)S(1)} collective-permute-done((f32[32,128]{1,0:T(8,128)S(1)}, f32[32,128]{1,0:T(8,128)S(1)}, u32[]{:S(2)}, u32[]{:S(2)}) %collective-permute-start.4) | collective-permute-done | bytes 16416 | tf_op jit(solution)/shard_map/ppermute | solution.py:737
  60.3 5.3 %collective-permute-start.5 = (f32[32,128]{1,0:T(8,128)S(1)}, f32[32,128]{1,0:T(8,128)S(1)}, u32[]{:S(2)}, u32[]{:S(2)}) collective-permute-start(f32[32,128]{1,0:T(8,128)S(1)} %get-tuple-element.54), channel_id=1, source_target_pairs={{0,15},{1,2},{2,1},{3,4},{4,3},{5,6},{6,5},{7,8},{8,7},{9,10},{10,... | collective-permute-start | bytes 49160 | tf_op jit(solution)/shard_map/ppermute | solution.py:737
  65.6 1.7 %collective-permute-done.5.refs_7_ = f32[32,128]{1,0:T(8,128)S(1)} collective-permute-done((f32[32,128]{1,0:T(8,128)S(1)}, f32[32,128]{1,0:T(8,128)S(1)}, u32[]{:S(2)}, u32[]{:S(2)}) %collective-permute-start.5) | collective-permute-done | bytes 16416 | tf_op jit(solution)/shard_map/ppermute | solution.py:737
  69.7 5.3 %collective-permute-start.9 = (f32[8,128]{1,0:T(8,128)S(1)}, f32[8,128]{1,0:T(8,128)S(1)}, u32[]{:S(2)}, u32[]{:S(2)}) collective-permute-start(f32[8,128]{1,0:T(8,128)S(1)} %get-tuple-element.60), channel_id=1, source_target_pairs={{0,15},{1,2},{2,1},{3,4},{4,3},{5,6},{6,5},{7,8},{8,7},{9,10},{10,... | collective-permute-start | bytes 12296 | tf_op jit(solution)/shard_map/ppermute | solution.py:737
  75.1 2.6 %collective-permute-start.21 = (f32[640,128]{1,0:T(8,128)S(1)}, f32[640,128]{1,0:T(8,128)S(1)}, u32[]{:S(2)}, u32[]{:S(2)}) collective-permute-start(f32[640,128]{1,0:T(8,128)S(1)} %get-tuple-element.79), channel_id=1, source_target_pairs={{0,15},{1,2},{2,1},{3,4},{4,3},{5,6},{6,5},{7,8},{8,7},{9,10},{10,... | collective-permute-start | bytes 983048 | tf_op jit(solution)/shard_map/ppermute | solution.py:737
  78.6 7.0 %collective-permute-done.20.a_0 = f32[640,128]{1,0:T(8,128)S(1)} collective-permute-done((f32[640,128]{1,0:T(8,128)S(1)}, f32[640,128]{1,0:T(8,128)S(1)}, u32[]{:S(2)}, u32[]{:S(2)}) %collective-permute-start.20) | collective-permute-done | bytes 327712 | tf_op jit(solution)/shard_map/ppermute | solution.py:737
  85.6 2.6 %collective-permute-done.21.a_1 = f32[640,128]{1,0:T(8,128)S(1)} collective-permute-done((f32[640,128]{1,0:T(8,128)S(1)}, f32[640,128]{1,0:T(8,128)S(1)}, u32[]{:S(2)}, u32[]{:S(2)}) %collective-permute-start.21) | collective-permute-done | bytes 327712 | tf_op jit(solution)/shard_map/ppermute | solution.py:737
  88.7 3.2 %collective-permute-done.22.b_0 = f32[640,128]{1,0:T(8,128)S(1)} collective-permute-done((f32[640,128]{1,0:T(8,128)S(1)}, f32[640,128]{1,0:T(8,128)S(1)}, u32[]{:S(2)}, u32[]{:S(2)}) %collective-permute-start.22) | collective-permute-done | bytes 327712 | tf_op jit(solution)/shard_map/ppermute | solution.py:737
  92.1 1.9 %collective-permute-start.13 = (f32[8,128]{1,0:T(8,128)S(1)}, f32[8,128]{1,0:T(8,128)S(1)}, u32[]{:S(2)}, u32[]{:S(2)}) collective-permute-start(f32[8,128]{1,0:T(8,128)S(1)} %get-tuple-element.66), channel_id=1, source_target_pairs={{0,15},{1,2},{2,1},{3,4},{4,3},{5,6},{6,5},{7,8},{8,7},{9,10},{10,... | collective-permute-start | bytes 12296 | tf_op jit(solution)/shard_map/ppermute | solution.py:737
  94.0 3.5 %collective-permute-start.23 = (f32[640,128]{1,0:T(8,128)S(1)}, f32[640,128]{1,0:T(8,128)S(1)}, u32[]{:S(2)}, u32[]{:S(2)}) collective-permute-start(f32[640,128]{1,0:T(8,128)S(1)} %get-tuple-element.81), channel_id=1, source_target_pairs={{0,15},{1,2},{2,1},{3,4},{4,3},{5,6},{6,5},{7,8},{8,7},{9,10},{10,... | collective-permute-start | bytes 983048 | tf_op jit(solution)/shard_map/ppermute | solution.py:737
  99.1 1.9 %collective-permute-start.25 = (f32[640,128]{1,0:T(8,128)S(1)}, f32[640,128]{1,0:T(8,128)S(1)}, u32[]{:S(2)}, u32[]{:S(2)}) collective-permute-start(f32[640,128]{1,0:T(8,128)S(1)} %get-tuple-element.83), channel_id=1, source_target_pairs={{0,15},{1,2},{2,1},{3,4},{4,3},{5,6},{6,5},{7,8},{8,7},{9,10},{10,... | collective-permute-start | bytes 983048 | tf_op jit(solution)/shard_map/ppermute | solution.py:737
  101.6 6.3 %collective-permute-done.23.b_1 = f32[640,128]{1,0:T(8,128)S(1)} collective-permute-done((f32[640,128]{1,0:T(8,128)S(1)}, f32[640,128]{1,0:T(8,128)S(1)}, u32[]{:S(2)}, u32[]{:S(2)}) %collective-permute-start.23) | collective-permute-done | bytes 327712 | tf_op jit(solution)/shard_map/ppermute | solution.py:737
  108.5 5.9 %collective-permute-done.25.c_1 = f32[640,128]{1,0:T(8,128)S(1)} collective-permute-done((f32[640,128]{1,0:T(8,128)S(1)}, f32[640,128]{1,0:T(8,128)S(1)}, u32[]{:S(2)}, u32[]{:S(2)}) %collective-permute-start.25) | collective-permute-done | bytes 327712 | tf_op jit(solution)/shard_map/ppermute | solution.py:737
  114.4 2.0 %collective-permute-start.17 = (f32[8,128]{1,0:T(8,128)S(1)}, f32[8,128]{1,0:T(8,128)S(1)}, u32[]{:S(2)}, u32[]{:S(2)}) collective-permute-start(f32[8,128]{1,0:T(8,128)S(1)} %get-tuple-element.72), channel_id=1, source_target_pairs={{0,15},{1,2},{2,1},{3,4},{4,3},{5,6},{6,5},{7,8},{8,7},{9,10},{10,... | collective-permute-start | bytes 12296 | tf_op jit(solution)/shard_map/ppermute | solution.py:737
  118.0 3.3 %collective-permute-done.17.y_1 = f32[8,128]{1,0:T(8,128)S(1)} collective-permute-done((f32[8,128]{1,0:T(8,128)S(1)}, f32[8,128]{1,0:T(8,128)S(1)}, u32[]{:S(2)}, u32[]{:S(2)}) %collective-permute-start.17) | collective-permute-done | bytes 4128 | tf_op jit(solution)/shard_map/ppermute | solution.py:737
  121.4 18.7 %shard_map.92 = (f32[4096,128]{1,0:T(8,128)}, f32[8192,128]{1,0:T(8,128)}, f32[10,32,128]{2,1,0:T(8,128)S(1)}, f32[3,128,128]{2,1,0:T(8,128)S(1)}) custom-call(s32[2,2,8]{2,1,0:T(2,128)S(1)} %bitcast.20, s32[1]{0:T(128)} %bitcast.2.base.refs_0_, s32[32]{0:T(128)S(1)} %copy-done.3, s32[4,32]{1,0:T(4,128)S(1)} %bitcast.15, s32[4,32]{1,0:T(4,128)S(1)} %bitcast.16, ...), custom_call_target="tpu_custom_call" | custom-call | tf_op jit(solution)/shard_map/pallas_call | solution.py:877
  140.1 6.1 %late_tiles.1 = (f32[4096,128]{1,0:T(8,128)}, f32[8192,128]{1,0:T(8,128)}) custom-call(s32[2,2,8]{2,1,0:T(2,128)S(1)} %bitcast.21, s32[1]{0:T(128)} %bitcast.2.base.refs_0_, s32[4,32]{1,0:T(4,128)S(1)} %bitcast.17, f32[10,32,128]{2,1,0:T(8,128)S(1)} %get-tuple-element.84.edges, ...), custom_call_target="tpu_custom_call", output_to_operand_aliasing={{0}: (7, {}), {1}: (8, {})} | custom-call | tf_op jit(solution)/shard_map/late_tiles/pallas_call | solution.py:897
  (48 shorter events, 13.9 us)
Async XLA Ops:
  5.9 10.7 %collective-permute-start = (f32[8,10240]{1,0:T(8,128)S(1)}, f32[8,10240]{1,0:T(8,128)S(1)}, u32[]{:S(2)}, u32[]{:S(2)}) collective-permute-start(f32[8,10240]{1,0:T(8,128)S(1)} %get-tuple-element.47), channel_id=1, source_target_pairs={{0,1},{1,0},{2,3},{3,2},{4,5},{5,4},{6,7},{7,6},{8,9},{9,8},{10,11... | collective-permute-start | bytes 983048 | tf_op jit(solution)/shard_map/ppermute | solution.py:737
  7.2 132.9 %collective-permute-start.26 = (f32[2560,128]{1,0:T(8,128)S(1)}, f32[2560,128]{1,0:T(8,128)S(1)}, u32[]{:S(2)}, u32[]{:S(2)}) collective-permute-start(f32[2560,128]{1,0:T(8,128)S(1)} %get-tuple-element.86), channel_id=1, source_target_pairs={{0,1},{1,0},{2,3},{3,2},{4,5},{5,4},{6,7},{7,6},{8,9},{9,8},{10,11... | collective-permute-start | bytes 3932168 | tf_op jit(solution)/shard_map/ppermute | solution.py:737
  8.0 132.1 %collective-permute-start.27 = (f32[2560,128]{1,0:T(8,128)S(1)}, f32[2560,128]{1,0:T(8,128)S(1)}, u32[]{:S(2)}, u32[]{:S(2)}) collective-permute-start(f32[2560,128]{1,0:T(8,128)S(1)} %get-tuple-element.87), channel_id=1, source_target_pairs={{0,15},{1,2},{2,1},{3,4},{4,3},{5,6},{6,5},{7,8},{8,7},{9,10},{10,... | collective-permute-start | bytes 3932168 | tf_op jit(solution)/shard_map/ppermute | solution.py:737
  14.0 36.6 %collective-permute-start.1 = (f32[8,10240]{1,0:T(8,128)S(1)}, f32[8,10240]{1,0:T(8,128)S(1)}, u32[]{:S(2)}, u32[]{:S(2)}) collective-permute-start(f32[8,10240]{1,0:T(8,128)S(1)} %get-tuple-element.48), channel_id=1, source_target_pairs={{0,15},{1,2},{2,1},{3,4},{4,3},{5,6},{6,5},{7,8},{8,7},{9,10},{10,... | collective-permute-start | bytes 983048 | tf_op jit(solution)/shard_map/ppermute | solution.py:737
  14.1 54.5 %collective-permute-start.18 = (f32[640,128]{1,0:T(8,128)S(1)}, f32[640,128]{1,0:T(8,128)S(1)}, u32[]{:S(2)}, u32[]{:S(2)}) collective-permute-start(f32[640,128]{1,0:T(8,128)S(1)} %get-tuple-element.76), channel_id=1, source_target_pairs={{0,1},{1,0},{2,3},{3,2},{4,5},{5,4},{6,7},{7,6},{8,9},{9,8},{10,11... | collective-permute-start | bytes 983048 | tf_op jit(solution)/shard_map/ppermute | solution.py:737
  16.6 52.1 %collective-permute-start.19 = (f32[640,128]{1,0:T(8,128)S(1)}, f32[640,128]{1,0:T(8,128)S(1)}, u32[]{:S(2)}, u32[]{:S(2)}) collective-permute-start(f32[640,128]{1,0:T(8,128)S(1)} %get-tuple-element.77), channel_id=1, source_target_pairs={{0,15},{1,2},{2,1},{3,4},{4,3},{5,6},{6,5},{7,8},{8,7},{9,10},{10,... | collective-permute-start | bytes 983048 | tf_op jit(solution)/shard_map/ppermute | solution.py:737
  56.5 3.7 %collective-permute-start.4 = (f32[32,128]{1,0:T(8,128)S(1)}, f32[32,128]{1,0:T(8,128)S(1)}, u32[]{:S(2)}, u32[]{:S(2)}) collective-permute-start(f32[32,128]{1,0:T(8,128)S(1)} %get-tuple-element.53), channel_id=1, source_target_pairs={{0,1},{1,0},{2,3},{3,2},{4,5},{5,4},{6,7},{7,6},{8,9},{9,8},{10,11... | collective-permute-start | bytes 49160 | tf_op jit(solution)/shard_map/ppermute | solution.py:737
  60.3 7.1 %collective-permute-start.5 = (f32[32,128]{1,0:T(8,128)S(1)}, f32[32,128]{1,0:T(8,128)S(1)}, u32[]{:S(2)}, u32[]{:S(2)}) collective-permute-start(f32[32,128]{1,0:T(8,128)S(1)} %get-tuple-element.54), channel_id=1, source_target_pairs={{0,15},{1,2},{2,1},{3,4},{4,3},{5,6},{6,5},{7,8},{8,7},{9,10},{10,... | collective-permute-start | bytes 49160 | tf_op jit(solution)/shard_map/ppermute | solution.py:737
  68.6 6.5 %collective-permute-start.7 = (f32[8,128]{1,0:T(8,128)S(1)}, f32[8,128]{1,0:T(8,128)S(1)}, u32[]{:S(2)}, u32[]{:S(2)}) collective-permute-start(f32[8,128]{1,0:T(8,128)S(1)} %get-tuple-element.58), channel_id=1, source_target_pairs={{0,112},{16,32},{32,16},{48,64},{64,48},{80,96},{96,80},{112,0},{1... | collective-permute-start | bytes 12296 | tf_op jit(solution)/shard_map/ppermute | solution.py:737
  68.7 6.4 %collective-permute-start.8 = (f32[8,128]{1,0:T(8,128)S(1)}, f32[8,128]{1,0:T(8,128)S(1)}, u32[]{:S(2)}, u32[]{:S(2)}) collective-permute-start(f32[8,128]{1,0:T(8,128)S(1)} %get-tuple-element.59), channel_id=1, source_target_pairs={{0,1},{1,0},{2,3},{3,2},{4,5},{5,4},{6,7},{7,6},{8,9},{9,8},{10,11... | collective-permute-start | bytes 12296 | tf_op jit(solution)/shard_map/ppermute | solution.py:737
  69.7 8.0 %collective-permute-start.9 = (f32[8,128]{1,0:T(8,128)S(1)}, f32[8,128]{1,0:T(8,128)S(1)}, u32[]{:S(2)}, u32[]{:S(2)}) collective-permute-start(f32[8,128]{1,0:T(8,128)S(1)} %get-tuple-element.60), channel_id=1, source_target_pairs={{0,15},{1,2},{2,1},{3,4},{4,3},{5,6},{6,5},{7,8},{8,7},{9,10},{10,... | collective-permute-start | bytes 12296 | tf_op jit(solution)/shard_map/ppermute | solution.py:737
  75.1 10.6 %collective-permute-start.20 = (f32[640,128]{1,0:T(8,128)S(1)}, f32[640,128]{1,0:T(8,128)S(1)}, u32[]{:S(2)}, u32[]{:S(2)}) collective-permute-start(f32[640,128]{1,0:T(8,128)S(1)} %get-tuple-element.78), channel_id=1, source_target_pairs={{0,1},{1,0},{2,3},{3,2},{4,5},{5,4},{6,7},{7,6},{8,9},{9,8},{10,11... | collective-permute-start | bytes 983048 | tf_op jit(solution)/shard_map/ppermute | solution.py:737
  75.1 13.2 %collective-permute-start.21 = (f32[640,128]{1,0:T(8,128)S(1)}, f32[640,128]{1,0:T(8,128)S(1)}, u32[]{:S(2)}, u32[]{:S(2)}) collective-permute-start(f32[640,128]{1,0:T(8,128)S(1)} %get-tuple-element.79), channel_id=1, source_target_pairs={{0,15},{1,2},{2,1},{3,4},{4,3},{5,6},{6,5},{7,8},{8,7},{9,10},{10,... | collective-permute-start | bytes 983048 | tf_op jit(solution)/shard_map/ppermute | solution.py:737
  77.7 14.1 %collective-permute-start.22 = (f32[640,128]{1,0:T(8,128)S(1)}, f32[640,128]{1,0:T(8,128)S(1)}, u32[]{:S(2)}, u32[]{:S(2)}) collective-permute-start(f32[640,128]{1,0:T(8,128)S(1)} %get-tuple-element.80), channel_id=1, source_target_pairs={{0,1},{1,0},{2,3},{3,2},{4,5},{5,4},{6,7},{7,6},{8,9},{9,8},{10,11... | collective-permute-start | bytes 983048 | tf_op jit(solution)/shard_map/ppermute | solution.py:737
  85.6 6.5 %collective-permute-start.10 = (f32[8,128]{1,0:T(8,128)S(1)}, f32[8,128]{1,0:T(8,128)S(1)}, u32[]{:S(2)}, u32[]{:S(2)}) collective-permute-start(f32[8,128]{1,0:T(8,128)S(1)} %get-tuple-element.63), channel_id=1, source_target_pairs={{0,16},{16,0},{32,48},{48,32},{64,80},{80,64},{96,112},{112,96},{1... | collective-permute-start | bytes 12296 | tf_op jit(solution)/shard_map/ppermute | solution.py:737
  88.2 5.8 %collective-permute-start.11 = (f32[8,128]{1,0:T(8,128)S(1)}, f32[8,128]{1,0:T(8,128)S(1)}, u32[]{:S(2)}, u32[]{:S(2)}) collective-permute-start(f32[8,128]{1,0:T(8,128)S(1)} %get-tuple-element.64), channel_id=1, source_target_pairs={{0,112},{16,32},{32,16},{48,64},{64,48},{80,96},{96,80},{112,0},{1... | collective-permute-start | bytes 12296 | tf_op jit(solution)/shard_map/ppermute | solution.py:737
  91.8 5.6 %collective-permute-start.12 = (f32[8,128]{1,0:T(8,128)S(1)}, f32[8,128]{1,0:T(8,128)S(1)}, u32[]{:S(2)}, u32[]{:S(2)}) collective-permute-start(f32[8,128]{1,0:T(8,128)S(1)} %get-tuple-element.65), channel_id=1, source_target_pairs={{0,1},{1,0},{2,3},{3,2},{4,5},{5,4},{6,7},{7,6},{8,9},{9,8},{10,11... | collective-permute-start | bytes 12296 | tf_op jit(solution)/shard_map/ppermute | solution.py:737
  92.1 6.9 %collective-permute-start.13 = (f32[8,128]{1,0:T(8,128)S(1)}, f32[8,128]{1,0:T(8,128)S(1)}, u32[]{:S(2)}, u32[]{:S(2)}) collective-permute-start(f32[8,128]{1,0:T(8,128)S(1)} %get-tuple-element.66), channel_id=1, source_target_pairs={{0,15},{1,2},{2,1},{3,4},{4,3},{5,6},{6,5},{7,8},{8,7},{9,10},{10,... | collective-permute-start | bytes 12296 | tf_op jit(solution)/shard_map/ppermute | solution.py:737
  94.0 13.9 %collective-permute-start.23 = (f32[640,128]{1,0:T(8,128)S(1)}, f32[640,128]{1,0:T(8,128)S(1)}, u32[]{:S(2)}, u32[]{:S(2)}) collective-permute-start(f32[640,128]{1,0:T(8,128)S(1)} %get-tuple-element.81), channel_id=1, source_target_pairs={{0,15},{1,2},{2,1},{3,4},{4,3},{5,6},{6,5},{7,8},{8,7},{9,10},{10,... | collective-permute-start | bytes 983048 | tf_op jit(solution)/shard_map/ppermute | solution.py:737
  97.5 10.4 %collective-permute-start.24 = (f32[640,128]{1,0:T(8,128)S(1)}, f32[640,128]{1,0:T(8,128)S(1)}, u32[]{:S(2)}, u32[]{:S(2)}) collective-permute-start(f32[640,128]{1,0:T(8,128)S(1)} %get-tuple-element.82), channel_id=1, source_target_pairs={{0,1},{1,0},{2,3},{3,2},{4,5},{5,4},{6,7},{7,6},{8,9},{9,8},{10,11... | collective-permute-start | bytes 983048 | tf_op jit(solution)/shard_map/ppermute | solution.py:737
  99.1 15.4 %collective-permute-start.25 = (f32[640,128]{1,0:T(8,128)S(1)}, f32[640,128]{1,0:T(8,128)S(1)}, u32[]{:S(2)}, u32[]{:S(2)}) collective-permute-start(f32[640,128]{1,0:T(8,128)S(1)} %get-tuple-element.83), channel_id=1, source_target_pairs={{0,15},{1,2},{2,1},{3,4},{4,3},{5,6},{6,5},{7,8},{8,7},{9,10},{10,... | collective-permute-start | bytes 983048 | tf_op jit(solution)/shard_map/ppermute | solution.py:737
  107.9 6.5 %collective-permute-start.14 = (f32[8,128]{1,0:T(8,128)S(1)}, f32[8,128]{1,0:T(8,128)S(1)}, u32[]{:S(2)}, u32[]{:S(2)}) collective-permute-start(f32[8,128]{1,0:T(8,128)S(1)} %get-tuple-element.69), channel_id=1, source_target_pairs={{0,16},{16,0},{32,48},{48,32},{64,80},{80,64},{96,112},{112,96},{1... | collective-permute-start | bytes 12296 | tf_op jit(solution)/shard_map/ppermute | solution.py:737
  107.9 8.6 %collective-permute-start.15 = (f32[8,128]{1,0:T(8,128)S(1)}, f32[8,128]{1,0:T(8,128)S(1)}, u32[]{:S(2)}, u32[]{:S(2)}) collective-permute-start(f32[8,128]{1,0:T(8,128)S(1)} %get-tuple-element.70), channel_id=1, source_target_pairs={{0,112},{16,32},{32,16},{48,64},{64,48},{80,96},{96,80},{112,0},{1... | collective-permute-start | bytes 12296 | tf_op jit(solution)/shard_map/ppermute | solution.py:737
  114.4 6.9 %collective-permute-start.17 = (f32[8,128]{1,0:T(8,128)S(1)}, f32[8,128]{1,0:T(8,128)S(1)}, u32[]{:S(2)}, u32[]{:S(2)}) collective-permute-start(f32[8,128]{1,0:T(8,128)S(1)} %get-tuple-element.72), channel_id=1, source_target_pairs={{0,15},{1,2},{2,1},{3,4},{4,3},{5,6},{6,5},{7,8},{8,7},{9,10},{10,... | collective-permute-start | bytes 12296 | tf_op jit(solution)/shard_map/ppermute | solution.py:737
  (8 other events, 132.2 us)
